TPU v7x, 256 devices: a whole 4x4x8 slice. The times are simulated.
256 devices in a mesh: wide: 32 (over x_hi, z, core), narrow: 8 (over y, x_lo).
Axes of the slice: x: 4 (x_hi: 2, x_lo: 2; x = x_hi * 2 + x_lo), y: 4, z: 8, core: 2. Of those that a mesh axis runs over, the one named last changes fastest.
Arguments:
- image_tokens: bfloat16 [64, 512, 1024], P('narrow', 'wide'), may hold values from -24 to 24
- qkv_weight: bfloat16 [1024, 3072], P('wide'), may hold values from -0.1875 to 0.1875
- block_list: int32 [8, 64], P('narrow', 'wide'), may hold values from 0 to 1, as said below
- block_count: int32 [8, 32], P('narrow', 'wide'), may hold values from 1 to 2, as said below
- out_grad: bfloat16 [64, 512, 1024], P('narrow', 'wide'), may hold values from -6 to 6
Outputs:
- attn_out: bfloat16 [64, 512, 1024], P('narrow', 'wide')
- grad_x: bfloat16 [64, 512, 1024], P('narrow', 'wide')
- grad_w: float32 [1024, 3072], P('wide')
Inputs may be any that keep to these rules, and one draw needn't show every extreme that they name: `block_list`: each tile's 2 entries are distinct block numbers of that tile, 0 to 1, row-major over its blocks; entries past the tile's count are padding. `block_count`: some tile's list is full.
All inputs are finite; a program needn't handle non-finite values.
Results may differ from a plain program's by a relative error of at most 0.0065.
The roundings to bfloat16 on the way count: a program that leaves them out, or rounds other values in their place, can miss the bound.
Values may be sent and summed in bfloat16 or wider, within the bound.
A program may use at most 128 MiB of HBM per device.

v0:
```python
import math

import jax
import jax.numpy as jnp
from jax import lax
from jax.sharding import PartitionSpec as P

HEADS = 16
WIN = 13
BLK = 8


NEGATIVE = -1e30


def padded_2(cells, sides, width):
    for axis, dim in sides:
        count = lax.axis_size(axis)
        ends = count - 1
        head = lax.slice_in_dim(cells, 0, width, axis=dim)
        tail = lax.slice_in_dim(cells, cells.shape[dim] - width, cells.shape[dim], axis=dim)
        cells = jnp.concatenate(
            [
                lax.ppermute(tail, axis, [(i, (i + 1) % count) for i in range(ends)]),
                cells,
                lax.ppermute(head, axis, [((i + 1) % count, i) for i in range(ends)]),
            ],
            axis=dim,
        )
    return cells


def copy_for_each(array, axis):
    peers = lax.axis_size(axis)
    return lax.all_to_all(
        jnp.broadcast_to(array[None], (peers, *array.shape)), axis, 0, 0, tiled=True
    )


def taken_together(array, axis):
    return copy_for_each(array, axis).sum(axis=0)


def window_table(block, window):
    radius = window // 2
    region = block + 2 * radius
    inner = jnp.arange(block * block, dtype=jnp.int32)
    outer = jnp.arange(region * region, dtype=jnp.int32)
    down = outer[None, :] // region - radius - inner[:, None] // block
    across = outer[None, :] % region - radius - inner[:, None] % block
    return (jnp.abs(down) <= radius) & (jnp.abs(across) <= radius)


def to_blocks(tile, block):
    rest = tile.shape[2:]
    shaped = tile.reshape((tile.shape[0] // block, block, tile.shape[1] // block, block) + rest)
    shaped = jnp.swapaxes(shaped, 1, 2)
    return shaped.reshape((tile.shape[0] // block * (tile.shape[1] // block), block * block) + rest)


def from_blocks(stacked, row_count, col_count, block):
    rest = stacked.shape[2:]
    shaped = stacked.reshape((row_count // block, col_count // block, block, block) + rest)
    shaped = jnp.swapaxes(shaped, 1, 2)
    return shaped.reshape((row_count, col_count) + rest)


def regions(padded, chosen, across, block, region):
    trailing = padded.shape[2:]

    def regions_single(number):
        start = (number // across * block, number % across * block) + (0,) * len(trailing)
        piece = lax.dynamic_slice(padded, start, (region, region) + trailing)
        return piece.reshape((region * region,) + trailing)

    return jax.vmap(regions_single)(chosen)


def by_groups(kernel, pairs, allowed, heads):
    group = 2

    def by_single(number):
        pieces = []
        for array, unit in pairs:
            piece = lax.dynamic_slice_in_dim(array, number * group * unit, group * unit, 2)
            if unit > 1:
                piece = piece.reshape(piece.shape[:2] + (group, unit))
            pieces.append(piece)
        return kernel(tuple(pieces), allowed)

    results = lax.map(by_single, jnp.arange(heads // group, dtype=jnp.int32))
    merged = []
    for result in results:
        moved = jnp.moveaxis(result, 0, 2)
        merged.append(moved.reshape(moved.shape[:2] + (-1,)))
    return tuple(merged)


def query_kernel(pieces, allowed):
    query, keys, values, grad_out = pieces
    scale = query.shape[-1] ** (-0.5)
    scores = jnp.einsum("bqhd,bkhd->bhqk", query, keys, preferred_element_type=jnp.float32) * scale
    scores = jnp.where(allowed[:, None], scores, NEGATIVE)
    top = jnp.max(scores, axis=-1, keepdims=True)
    total = jnp.sum(jnp.exp(scores - top), axis=-1, keepdims=True)
    logsum = top + jnp.log(total)
    probs = jnp.exp(scores - logsum)
    weights = probs.astype(jnp.bfloat16)
    output = jnp.einsum(
        "bhqk,bkhd->bqhd", weights, values, preferred_element_type=jnp.float32
    ).astype(jnp.bfloat16)
    delta = jnp.sum(grad_out.astype(jnp.float32) * output.astype(jnp.float32), axis=-1)
    dprobs = jnp.einsum("bqhd,bkhd->bhqk", grad_out, values, preferred_element_type=jnp.float32)
    dscores = (probs * (dprobs - jnp.swapaxes(delta, 1, 2)[..., None]) * scale).astype(jnp.bfloat16)
    grad_query = jnp.einsum(
        "bhqk,bkhd->bqhd", dscores, keys, preferred_element_type=jnp.float32
    ).astype(jnp.bfloat16)
    return (output, jnp.swapaxes(logsum[..., 0], 1, 2), delta, grad_query)


def key_kernel(pieces, allowed):
    keys, values, query, grad_out, logsum, delta = pieces
    scale = keys.shape[-1] ** (-0.5)
    scores = jnp.einsum("bjhd,bihd->bhji", keys, query, preferred_element_type=jnp.float32) * scale
    shift = jnp.swapaxes(logsum, 1, 2)[:, :, None, :]
    probs = jnp.where(allowed[:, None], jnp.exp(scores - shift), 0.0)
    weights = probs.astype(jnp.bfloat16)
    grad_values = jnp.einsum(
        "bhji,bihd->bjhd", weights, grad_out, preferred_element_type=jnp.float32
    ).astype(jnp.bfloat16)
    dprobs = jnp.einsum("bjhd,bihd->bhji", values, grad_out, preferred_element_type=jnp.float32)
    dscores = (probs * (dprobs - jnp.swapaxes(delta, 1, 2)[:, :, None, :]) * scale).astype(
        jnp.bfloat16
    )
    grad_keys = jnp.einsum(
        "bhji,bihd->bjhd", dscores, query, preferred_element_type=jnp.float32
    ).astype(jnp.bfloat16)
    return (grad_keys, grad_values)


def local(image_tokens, qkv_weight, block_list, block_count, out_grad):
    row_count, col_count, width = image_tokens.shape
    heads = HEADS
    head_dim = width // heads
    radius = WIN // 2
    region = BLK + 2 * radius
    across = col_count // BLK
    nblocks = row_count // BLK * across
    token_count = row_count * col_count
    flat = image_tokens.reshape(token_count, width)
    full_weight = lax.all_gather(qkv_weight, "wide", axis=0, tiled=True)
    projected = jnp.dot(flat, full_weight, preferred_element_type=jnp.float32)
    projected = projected.astype(jnp.bfloat16).reshape(row_count, col_count, 3 * width)
    query = projected[:, :, :width]
    keys = projected[:, :, width : 2 * width]
    values = projected[:, :, 2 * width :]
    padded_keys, padded_values = (
        padded_2(keys, (("narrow", 0), ("wide", 1)), radius),
        padded_2(values, (("narrow", 0), ("wide", 1)), radius),
    )
    row_place = (
        jnp.arange(row_count + 2 * radius, dtype=jnp.int32)
        + lax.axis_index("narrow") * row_count
        - radius
    )
    col_place = (
        jnp.arange(col_count + 2 * radius, dtype=jnp.int32)
        + lax.axis_index("wide") * col_count
        - radius
    )
    row_inside = (row_place >= 0) & (row_place < row_count * lax.axis_size("narrow"))
    col_inside = (col_place >= 0) & (col_place < col_count * lax.axis_size("wide"))
    inside = (row_inside[:, None] & col_inside[None, :]).astype(jnp.float32)[:, :, None]
    table = window_table(BLK, WIN)
    slots = block_list[0]
    count = block_count[0, 0]
    live = (jnp.arange(slots.shape[0], dtype=jnp.int32) < count).astype(jnp.float32)
    block_on = jnp.sum(
        (slots[:, None] == jnp.arange(nblocks, dtype=jnp.int32)[None, :]).astype(jnp.float32)
        * live[:, None],
        axis=0,
    )
    query_blocks = jnp.take(to_blocks(query, BLK), slots, axis=0)
    grad_blocks = jnp.take(to_blocks(out_grad, BLK), slots, axis=0)
    key_regions = regions(padded_keys, slots, across, BLK, region)
    value_regions = regions(padded_values, slots, across, BLK, region)
    valid_regions = regions(inside, slots, across, BLK, region)[:, :, 0]
    allowed = table[None] & (valid_regions > 0)[:, None, :]
    output, logsum, delta, grad_query = by_groups(
        query_kernel,
        (
            (query_blocks, head_dim),
            (key_regions, head_dim),
            (value_regions, head_dim),
            (grad_blocks, head_dim),
        ),
        allowed,
        heads,
    )
    keep_half = live.astype(jnp.bfloat16)[:, None, None]
    output = output * keep_half
    grad_query = grad_query * keep_half
    logsum = logsum * live[:, None, None]
    delta = delta * live[:, None, None]

    def place(stacked):
        return jnp.zeros((nblocks,) + stacked.shape[1:], stacked.dtype).at[slots].set(stacked)

    output = place(output)
    grad_query = place(grad_query)
    logsum = place(logsum)
    delta = place(delta)
    attn_out = from_blocks(output, row_count, col_count, BLK)
    query_grad = from_blocks(grad_query, row_count, col_count, BLK)
    logsum_tile = from_blocks(logsum, row_count, col_count, BLK)
    delta_tile = from_blocks(delta, row_count, col_count, BLK)
    token_on = from_blocks(
        jnp.broadcast_to(block_on[:, None], (nblocks, BLK * BLK)), row_count, col_count, BLK
    )
    padded_query, padded_grad = (
        padded_2(query, (("narrow", 0), ("wide", 1)), radius),
        padded_2(out_grad, (("narrow", 0), ("wide", 1)), radius),
    )
    padded_logsum, padded_delta, padded_on = (
        padded_2(logsum_tile, (("narrow", 0), ("wide", 1)), radius),
        padded_2(delta_tile, (("narrow", 0), ("wide", 1)), radius),
        padded_2(token_on, (("narrow", 0), ("wide", 1)), radius),
    )
    every = jnp.arange(nblocks, dtype=jnp.int32)
    on_regions = regions(padded_on[:, :, None], every, across, BLK, region)[:, :, 0]
    key_allowed = table[None] & (on_regions > 0)[:, None, :]
    grad_keys, grad_values = by_groups(
        key_kernel,
        (
            (to_blocks(keys, BLK), head_dim),
            (to_blocks(values, BLK), head_dim),
            (regions(padded_query, every, across, BLK, region), head_dim),
            (regions(padded_grad, every, across, BLK, region), head_dim),
            (regions(padded_logsum, every, across, BLK, region), 1),
            (regions(padded_delta, every, across, BLK, region), 1),
        ),
        key_allowed,
        heads,
    )
    key_grad = from_blocks(grad_keys, row_count, col_count, BLK)
    value_grad = from_blocks(grad_values, row_count, col_count, BLK)
    grads = jnp.concatenate([query_grad, key_grad, value_grad], axis=-1).reshape(
        token_count, 3 * width
    )
    input_grad = lax.dot_general(
        grads, full_weight, (((1,), (1,)), ((), ())), preferred_element_type=jnp.float32
    )
    grad_x = input_grad.astype(jnp.bfloat16).reshape(row_count, col_count, width)
    factor = 1.0 / math.sqrt(token_count * lax.axis_size("narrow") * lax.axis_size("wide"))
    partial_rows = lax.psum_scatter(
        lax.dot_general(flat, grads, (((0,), (0,)), ((), ())), preferred_element_type=jnp.float32),
        "wide",
        scatter_dimension=0,
        tiled=True,
    )
    grad_w = taken_together(partial_rows, "narrow") * factor
    return (attn_out, grad_x, grad_w)


def solution(mesh):
    placed = (
        P("narrow", "wide", None),
        P("wide", None),
        P("narrow", "wide"),
        P("narrow", "wide"),
        P("narrow", "wide", None),
    )
    return jax.shard_map(
        local,
        mesh=mesh,
        in_specs=placed,
        out_specs=(P("narrow", "wide", None), P("narrow", "wide", None), P("wide", None)),
        check_vma=False,
    )
```

profile of v0, /device:TPU:1, one launch (start us, length us, event | category | flops | bytes accessed | tf_op | source)
XLA Modules:
  0.0 594.2 jit_solution(11332187866630251206)
XLA Ops:
  10.1 1.3 collective-permute-start.13
  11.3 4.6 collective-permute-start.12
  17.1 1.3 collective-permute-start.21
  18.4 4.9 collective-permute-start.20
  25.5 2.7 while.36
  29.8 4.7 collective-permute-start.15
  34.6 2.1 collective-permute-start.14
  38.5 2.2 collective-permute-start.23
  40.7 3.4 collective-permute-start.22
  44.1 2.7 while.37
  47.0 1.4 collective-permute-done.23
  49.7 2.0 gather_fusion.4
  51.7 3.2 copy.280
  55.0 54.3 %all-gather.2.cloned.1.call-done = bf16[1024,3072]{1,0:T(8,128)(2,1)} async-done(((bf16[32,3072]{1,0:T(8,128)(2,1)}), bf16[1024,3072]{1,0:T(8,128)(2,1)}) %all-gather.2.cloned.1.call-update) | async-done | bytes 6291472 | tf_op jit(solution)/shard_map/all_gather | solution.py:151
  109.3 3.8 convolution_convert_fusion.2
  114.9 1.3 collective-permute-start.1
  117.2 4.7 collective-permute-start
  124.0 1.3 collective-permute-start.5
  126.3 4.0 collective-permute-start.4
  131.4 1.3 collective-permute-start.9
  135.6 4.0 collective-permute-start.8
  140.9 4.0 collective-permute-start.3
  144.9 2.9 collective-permute-start.2
  148.9 1.9 collective-permute-start.7
  150.8 3.6 collective-permute-start.6
  155.6 1.9 collective-permute-start.11
  157.5 3.8 collective-permute-start.10
  161.4 1.4 pad_maximum_fusion
  162.8 2.0 gather_fusion
  164.8 4.5 copy.250
  169.3 1.5 pad_maximum_fusion.1
  170.8 2.0 gather_fusion.1
  172.8 4.4 copy.256
  179.1 52.6 %while.38 = (s32[]{:T(128)}, bf16[8,2,64,2,64]{2,4,3,1,0:T(8,128)(2,1)}, f32[8,2,64,2]{2,3,1,0:T(2,128)S(1)}, f32[8,2,64,2]{2,3,1,0:T(2,128)S(1)}, bf16[8,2,64,2...) while((s32[]{:T(128)}, ...), condition=%wide.region_4.6_spmd.clone, body=%wide.region_0.5_spmd.clone.sunk | while | flops 53806596 | bytes 4801551 | solution.py:91
  180.3 1.3 constant_dynamic-slice_fusion.18
  186.9 1.3 constant_dynamic-slice_fusion.18
  193.5 1.3 constant_dynamic-slice_fusion.18
  200.0 1.3 constant_dynamic-slice_fusion.18
  206.6 1.3 constant_dynamic-slice_fusion.18
  213.2 1.3 constant_dynamic-slice_fusion.18
  219.7 1.3 constant_dynamic-slice_fusion.18
  226.3 1.3 constant_dynamic-slice_fusion.18
  231.6 1.5 copy.264
  238.2 5.5 collective-permute-start.16
  249.5 1.6 pad_maximum_fusion.2
  253.0 2.0 gather_fusion.2
  255.0 4.4 copy.268
  259.6 4.2 collective-permute-start.24
  264.8 2.0 collective-permute-start.19
  266.9 3.5 collective-permute-start.18
  270.4 1.6 pad_maximum_fusion.20
  272.0 1.9 collective-permute-start.27
  273.9 3.9 collective-permute-start.26
  284.0 52.7 %while.39 = (s32[]{:T(128)}, bf16[8,2,64,2,64]{2,4,3,1,0:T(8,128)(2,1)}, bf16[8,2,64,2,64]{2,4,3,1,0:T(8,128)(2,1)}, s32[8]{0:T(128)S(1)}, bf16[2,400,1024]{2,0,...) while((s32[]{:T(128)}, ...), condition=%wide.region_11.13_spmd.clone, body=%wide.region_10.12_spmd.clone.sunk | while | flops 53331976 | bytes 4312649 | solution.py:91
  336.6 1.5 copy.292
  340.9 6.4 %convolution_bitcast_fusion = f32[1024,3072]{0,1:T(8,128)} fusion(bf16[8,16,1024]{2,1,0:T(8,128)(2,1)S(1)} %copy-done, bf16[8,16,1024]{2,1,0:T(8,128)(2,1)S(1)} %get-tuple-element.636, bf16[8,16,1024]{2,1,0:T(8,128)(2,1)S(1)} %get-tuple-element.634, bf16[8,16,1024]{2,1,0:T(8,128)(2,1)S(1)} %copy-done.21), kind=kOutput, calls=%fused_computation.76 | convolution fusion | flops 807665664 | bytes 13631488 | tf_op jit(solution)/shard_map/dot_general | solution.py:256
  347.3 12.7 %copy.299 = f32[1024,3072]{1,0:T(8,128)} copy(f32[1024,3072]{0,1:T(8,128)} %convolution_bitcast_fusion) | data formatting | bytes 25165824
  360.0 184.8 %reduce-scatter.4.cloned.1.call-done = f32[32,3072]{1,0:T(8,128)} async-done(((f32[1024,3072]{1,0:T(8,128)}), f32[32,3072]{1,0:T(8,128)}) %reduce-scatter.4.cloned.1.call-update) | async-done | bytes 393232 | tf_op jit(solution)/shard_map/reduce_scatter | solution.py:255
  544.8 3.0 broadcast_in_dim.136
  547.8 4.0 all-to-all-start
  551.8 1.5 scatter_fusion
  554.1 6.0 %convolution_convert_fusion.3 = bf16[128,1024]{1,0:T(8,128)(2,1)} fusion(bf16[1024,3072]{1,0:T(8,128)(2,1)} %all-gather.2.cloned.1.call-done, bf16[128,1024]{1,0:T(8,128)(2,1)} %bitcast.280, bf16[128,1024]{1,0:T(8,128)(2,1)} %bitcast.281, bf16[128,1024]{1,0:T(8,128)(2,1)} %bitcast.279), kind=kOutput, calls=%fused_computation.82 | convolution fusion | flops 807796736 | bytes 7340032 | tf_op jit(solution)/shard_map/dot_general | solution.py:250
  560.1 24.5 %all-to-all-done = f32[8,32,3072]{2,1,0:T(8,128)S(1)} async-done(((f32[8,32,3072]{2,1,0:T(8,128)}), f32[8,32,3072]{2,1,0:T(8,128)S(1)}, u32[]{:S(2)}, u32[]{:S(2)}) %all-to-all-start) | async-done | bytes 3145760 | tf_op jit(solution)/shard_map/all_to_all | solution.py:35
  585.6 1.8 broadcast_multiply_fusion
  (423 shorter events, 133.2 us)
Async XLA Ops:
  7.2 102.1 %copy-start = (bf16[8,16,1024]{2,1,0:T(8,128)(2,1)S(1)}, bf16[8,16,1024]{2,1,0:T(8,128)(2,1)}, u32[]{:S(2)}) copy-start(bf16[8,16,1024]{2,1,0:T(8,128)(2,1)} %param.11) | copy-start | bytes 786436
  7.2 21.1 %copy-start.31 = (s32[1,2]{1,0:T(1,128)S(1)}, s32[1,2]{1,0:T(1,128)}, u32[]{:S(2)}) copy-start(s32[1,2]{1,0:T(1,128)} %param.13) | copy-start | bytes 28
  7.2 22.4 %copy-start.10 = (bf16[8,16,1024]{2,1,0:T(8,128)(2,1)S(1)}, bf16[8,16,1024]{2,1,0:T(8,128)(2,1)}, u32[]{:S(2)}) copy-start(bf16[8,16,1024]{2,1,0:T(8,128)(2,1)} %param.15) | copy-start | bytes 786436
  7.2 102.1 %all-gather.2.cloned.1.call-start = ((), (), s32[]{:S(2)}) async-start(), calls=%async_computation.2 | async-start | bytes 6488064 | tf_op jit(solution)/shard_map/all_gather | solution.py:151
  7.9 536.9 %reduce-scatter.4.cloned.1.call-start = ((), (), s32[]{:S(2)}) async-start(), calls=%async_computation.3 | async-start | bytes 12976128 | tf_op jit(solution)/shard_map/reduce_scatter | solution.py:255
  9.1 0.7 copy-start.28
  10.1 19.6 %collective-permute-start.13 = (f32[6,16]{1,0:T(8,128)S(1)}, f32[6,16]{1,0:T(8,128)S(1)}, u32[]{:S(2)}, u32[]{:S(2)}) collective-permute-start(f32[6,16]{1,0:T(8,128)S(1)} %slice.132), channel_id=1, source_target_pairs={{1,0},{2,1},{3,2},{4,3},{5,4},{6,5},{7,6},{9,8},{10,9},{11,10},{12... | collective-permute-start | bytes 1160 | tf_op jit(solution)/shard_map/ppermute | solution.py:26
  11.3 18.4 %collective-permute-start.12 = (f32[6,16]{1,0:T(8,128)S(1)}, f32[6,16]{1,0:T(8,128)S(1)}, u32[]{:S(2)}, u32[]{:S(2)}) collective-permute-start(f32[6,16]{1,0:T(8,128)S(1)} %slice.132), channel_id=1, source_target_pairs={{0,1},{1,2},{2,3},{3,4},{4,5},{5,6},{6,7},{8,9},{9,10},{10,11},{11... | collective-permute-start | bytes 1160 | tf_op jit(solution)/shard_map/ppermute | solution.py:24
  17.1 21.2 %collective-permute-start.21 = (bf16[6,16,1024]{2,0,1:T(8,128)(2,1)S(1)}, bf16[6,16,1024]{2,0,1:T(8,128)(2,1)S(1)}, u32[]{:S(2)}, u32[]{:S(2)}) collective-permute-start(bf16[6,16,1024]{2,0,1:T(8,128)(2,1)S(1)} %get-tuple-element.639), channel_id=1, source_target_pairs={{1,0},{2,1},{3,2},{4,3},{5,4},{6,5},{7,6},{9,8},{10,9},{11,10},{12... | collective-permute-start | bytes 589832 | tf_op jit(solution)/shard_map/ppermute | solution.py:26
  18.4 19.9 %collective-permute-start.20 = (bf16[6,16,1024]{2,0,1:T(8,128)(2,1)S(1)}, bf16[6,16,1024]{2,0,1:T(8,128)(2,1)S(1)}, u32[]{:S(2)}, u32[]{:S(2)}) collective-permute-start(bf16[6,16,1024]{2,0,1:T(8,128)(2,1)S(1)} %get-tuple-element.638), channel_id=1, source_target_pairs={{0,1},{1,2},{2,3},{3,4},{4,5},{5,6},{6,7},{8,9},{9,10},{10,11},{11... | collective-permute-start | bytes 589832 | tf_op jit(solution)/shard_map/ppermute | solution.py:24
  25.4 23.0 %copy-start.26 = (s32[1024]{0:T(1024)}, s32[1024]{0:T(1024)S(1)}, u32[]{:S(2)}) copy-start(s32[1024]{0:T(1024)S(1)} %pad_clamp_fusion) | copy-start | bytes 12292
  29.8 8.4 %collective-permute-start.15 = (f32[20,6]{1,0:T(8,128)S(1)}, f32[20,6]{1,0:T(8,128)S(1)}, u32[]{:S(2)}, u32[]{:S(2)}) collective-permute-start(f32[20,6]{1,0:T(8,128)S(1)} %get-tuple-element.645), channel_id=1, source_target_pairs={{8,0},{16,8},{24,16},{32,24},{40,32},{48,40},{56,48},{64,56},{72,6... | collective-permute-start | bytes 1448 | tf_op jit(solution)/shard_map/ppermute | solution.py:26
  34.6 3.6 collective-permute-start.14
  38.5 9.9 %collective-permute-start.23 = (bf16[20,6,1024]{2,0,1:T(8,128)(2,1)S(1)}, bf16[20,6,1024]{2,0,1:T(8,128)(2,1)S(1)}, u32[]{:S(2)}, u32[]{:S(2)}) collective-permute-start(bf16[20,6,1024]{2,0,1:T(8,128)(2,1)S(1)} %get-tuple-element.612), channel_id=1, source_target_pairs={{8,0},{16,8},{24,16},{32,24},{40,32},{48,40},{56,48},{64,56},{72,6... | collective-permute-start | bytes 737288 | tf_op jit(solution)/shard_map/ppermute | solution.py:26
  40.7 8.6 %collective-permute-start.22 = (bf16[20,6,1024]{2,0,1:T(8,128)(2,1)S(1)}, bf16[20,6,1024]{2,0,1:T(8,128)(2,1)S(1)}, u32[]{:S(2)}, u32[]{:S(2)}) collective-permute-start(bf16[20,6,1024]{2,0,1:T(8,128)(2,1)S(1)} %get-tuple-element.611), channel_id=1, source_target_pairs={{0,8},{8,16},{16,24},{24,32},{32,40},{40,48},{48,56},{56,64},{64,7... | collective-permute-start | bytes 737288 | tf_op jit(solution)/shard_map/ppermute | solution.py:24
  114.9 20.7 %collective-permute-start.1 = (bf16[6,16,1024]{2,0,1:T(8,128)(2,1)}, bf16[6,16,1024]{2,0,1:T(8,128)(2,1)}, u32[]{:S(2)}, u32[]{:S(2)}) collective-permute-start(bf16[6,16,1024]{2,0,1:T(8,128)(2,1)} %copy.308), channel_id=1, source_target_pairs={{1,0},{2,1},{3,2},{4,3},{5,4},{6,5},{7,6},{9,8},{10,9},{11,10},{12... | collective-permute-start | bytes 589832 | tf_op jit(solution)/shard_map/ppermute | solution.py:26
  116.2 16.5 %copy-start.11 = (bf16[2,64,1024]{2,1,0:T(8,128)(2,1)S(1)}, bf16[2,64,1024]{2,1,0:T(8,128)(2,1)}, u32[]{:S(2)}) copy-start(bf16[2,64,1024]{2,1,0:T(8,128)(2,1)} %gather_fusion.7) | copy-start | bytes 786436
  116.2 16.5 %copy-start.30 = (pred[2]{0:T(512)(128)(4,1)S(1)}, pred[2]{0:T(512)(128)(4,1)}, u32[]{:S(2)}) copy-start(pred[2]{0:T(512)(128)(4,1)} %compare_and_fusion) | copy-start | bytes 10
  116.3 23.3 %copy-start.2 = (bf16[8,16,1024]{2,0,1:T(8,128)(2,1)}, bf16[8,16,1024]{2,0,1:T(8,128)(2,1)S(1)}, u32[]{:S(2)}) copy-start(bf16[8,16,1024]{2,0,1:T(8,128)(2,1)S(1)} %copy.307) | copy-start | bytes 786436
  117.2 22.4 %collective-permute-start = (bf16[6,16,1024]{2,0,1:T(8,128)(2,1)}, bf16[6,16,1024]{2,0,1:T(8,128)(2,1)}, u32[]{:S(2)}, u32[]{:S(2)}) collective-permute-start(bf16[6,16,1024]{2,0,1:T(8,128)(2,1)} %copy.306), channel_id=1, source_target_pairs={{0,1},{1,2},{2,3},{3,4},{4,5},{5,6},{6,7},{8,9},{9,10},{10,11},{11... | collective-permute-start | bytes 589832 | tf_op jit(solution)/shard_map/ppermute | solution.py:24
  122.9 10.9 %copy-start.20 = (bf16[6,16,1024]{2,1,0:T(8,128)(2,1)S(1)}, bf16[6,16,1024]{2,1,0:T(8,128)(2,1)}, u32[]{:S(2)}) copy-start(bf16[6,16,1024]{2,1,0:T(8,128)(2,1)} %get-tuple-element.615) | copy-start | bytes 589828
  124.0 20.9 %collective-permute-start.5 = (bf16[6,16,1024]{2,0,1:T(8,128)(2,1)S(1)}, bf16[6,16,1024]{2,0,1:T(8,128)(2,1)S(1)}, u32[]{:S(2)}, u32[]{:S(2)}) collective-permute-start(bf16[6,16,1024]{2,0,1:T(8,128)(2,1)S(1)} %copy.312), channel_id=1, source_target_pairs={{1,0},{2,1},{3,2},{4,3},{5,4},{6,5},{7,6},{9,8},{10,9},{11,10},{12... | collective-permute-start | bytes 589832 | tf_op jit(solution)/shard_map/ppermute | solution.py:26
  126.3 21.5 %collective-permute-start.4 = (bf16[6,16,1024]{2,0,1:T(8,128)(2,1)S(1)}, bf16[6,16,1024]{2,0,1:T(8,128)(2,1)S(1)}, u32[]{:S(2)}, u32[]{:S(2)}) collective-permute-start(bf16[6,16,1024]{2,0,1:T(8,128)(2,1)S(1)} %copy.310), channel_id=1, source_target_pairs={{0,1},{1,2},{2,3},{3,4},{4,5},{5,6},{6,7},{8,9},{9,10},{10,11},{11... | collective-permute-start | bytes 589832 | tf_op jit(solution)/shard_map/ppermute | solution.py:24
  131.4 19.4 %collective-permute-start.9 = (bf16[6,16,1024]{2,0,1:T(8,128)(2,1)S(1)}, bf16[6,16,1024]{2,0,1:T(8,128)(2,1)S(1)}, u32[]{:S(2)}, u32[]{:S(2)}) collective-permute-start(bf16[6,16,1024]{2,0,1:T(8,128)(2,1)S(1)} %copy.314), channel_id=1, source_target_pairs={{1,0},{2,1},{3,2},{4,3},{5,4},{6,5},{7,6},{9,8},{10,9},{11,10},{12... | collective-permute-start | bytes 589832 | tf_op jit(solution)/shard_map/ppermute | solution.py:26
  133.8 15.1 %copy-start.4 = (bf16[8,16,1024]{2,0,1:T(8,128)(2,1)}, bf16[8,16,1024]{2,0,1:T(8,128)(2,1)S(1)}, u32[]{:S(2)}) copy-start(bf16[8,16,1024]{2,0,1:T(8,128)(2,1)S(1)} %copy.311) | copy-start | bytes 786436
  135.6 18.9 %collective-permute-start.8 = (bf16[6,16,1024]{2,0,1:T(8,128)(2,1)S(1)}, bf16[6,16,1024]{2,0,1:T(8,128)(2,1)S(1)}, u32[]{:S(2)}, u32[]{:S(2)}) collective-permute-start(bf16[6,16,1024]{2,0,1:T(8,128)(2,1)S(1)} %copy.313), channel_id=1, source_target_pairs={{0,1},{1,2},{2,3},{3,4},{4,5},{5,6},{6,7},{8,9},{9,10},{10,11},{11... | collective-permute-start | bytes 589832 | tf_op jit(solution)/shard_map/ppermute | solution.py:24
  140.9 20.5 %copy-start.3 = (bf16[8,16,1024]{2,0,1:T(8,128)(2,1)S(1)}, bf16[8,16,1024]{2,0,1:T(8,128)(2,1)}, u32[]{:S(2)}) copy-start(bf16[8,16,1024]{2,0,1:T(8,128)(2,1)} %copy-done.2) | copy-start | bytes 786436
  140.9 16.6 %collective-permute-start.3 = (bf16[20,6,1024]{2,0,1:T(8,128)(2,1)S(1)}, bf16[20,6,1024]{2,0,1:T(8,128)(2,1)S(1)}, u32[]{:S(2)}, u32[]{:S(2)}) collective-permute-start(bf16[20,6,1024]{2,0,1:T(8,128)(2,1)S(1)} %get-tuple-element.627), channel_id=1, source_target_pairs={{8,0},{16,8},{24,16},{32,24},{40,32},{48,40},{56,48},{64,56},{72,6... | collective-permute-start | bytes 737288 | tf_op jit(solution)/shard_map/ppermute | solution.py:26
  144.9 16.4 %copy-start.14 = (bf16[6,16,1024]{2,0,1:T(8,128)(2,1)}, bf16[6,16,1024]{2,0,1:T(8,128)(2,1)S(1)}, u32[]{:S(2)}) copy-start(bf16[6,16,1024]{2,0,1:T(8,128)(2,1)S(1)} %collective-permute-done.5) | copy-start | bytes 589828
  144.9 16.4 %collective-permute-start.2 = (bf16[20,6,1024]{2,0,1:T(8,128)(2,1)S(1)}, bf16[20,6,1024]{2,0,1:T(8,128)(2,1)S(1)}, u32[]{:S(2)}, u32[]{:S(2)}) collective-permute-start(bf16[20,6,1024]{2,0,1:T(8,128)(2,1)S(1)} %get-tuple-element.626), channel_id=1, source_target_pairs={{0,8},{8,16},{16,24},{24,32},{32,40},{40,48},{48,56},{56,64},{64,7... | collective-permute-start | bytes 737288 | tf_op jit(solution)/shard_map/ppermute | solution.py:24
  147.8 13.5 %copy-start.16 = (bf16[6,16,1024]{2,0,1:T(8,128)(2,1)}, bf16[6,16,1024]{2,0,1:T(8,128)(2,1)S(1)}, u32[]{:S(2)}) copy-start(bf16[6,16,1024]{2,0,1:T(8,128)(2,1)S(1)} %collective-permute-done.4) | copy-start | bytes 589828
  148.9 20.4 %collective-permute-start.7 = (bf16[20,6,1024]{2,0,1:T(8,128)(2,1)}, bf16[20,6,1024]{2,0,1:T(8,128)(2,1)}, u32[]{:S(2)}, u32[]{:S(2)}) collective-permute-start(bf16[20,6,1024]{2,0,1:T(8,128)(2,1)} %get-tuple-element.622), channel_id=1, source_target_pairs={{8,0},{16,8},{24,16},{32,24},{40,32},{48,40},{56,48},{64,56},{72,6... | collective-permute-start | bytes 737288 | tf_op jit(solution)/shard_map/ppermute | solution.py:26
  150.8 10.5 %copy-start.12 = (bf16[6,16,1024]{2,0,1:T(8,128)(2,1)}, bf16[6,16,1024]{2,0,1:T(8,128)(2,1)S(1)}, u32[]{:S(2)}) copy-start(bf16[6,16,1024]{2,0,1:T(8,128)(2,1)S(1)} %collective-permute-done.9) | copy-start | bytes 589828
  150.8 18.5 %collective-permute-start.6 = (bf16[20,6,1024]{2,0,1:T(8,128)(2,1)}, bf16[20,6,1024]{2,0,1:T(8,128)(2,1)}, u32[]{:S(2)}, u32[]{:S(2)}) collective-permute-start(bf16[20,6,1024]{2,0,1:T(8,128)(2,1)} %get-tuple-element.621), channel_id=1, source_target_pairs={{0,8},{8,16},{16,24},{24,32},{32,40},{40,48},{48,56},{56,64},{64,7... | collective-permute-start | bytes 737288 | tf_op jit(solution)/shard_map/ppermute | solution.py:24
  154.5 6.9 %copy-start.13 = (bf16[6,16,1024]{2,0,1:T(8,128)(2,1)}, bf16[6,16,1024]{2,0,1:T(8,128)(2,1)S(1)}, u32[]{:S(2)}) copy-start(bf16[6,16,1024]{2,0,1:T(8,128)(2,1)S(1)} %collective-permute-done.8) | copy-start | bytes 589828
  155.6 93.9 %collective-permute-start.11 = (bf16[20,6,1024]{2,0,1:T(8,128)(2,1)}, bf16[20,6,1024]{2,0,1:T(8,128)(2,1)}, u32[]{:S(2)}, u32[]{:S(2)}) collective-permute-start(bf16[20,6,1024]{2,0,1:T(8,128)(2,1)} %get-tuple-element.614), channel_id=1, source_target_pairs={{8,0},{16,8},{24,16},{32,24},{40,32},{48,40},{56,48},{64,56},{72,6... | collective-permute-start | bytes 737288 | tf_op jit(solution)/shard_map/ppermute | solution.py:26
  157.5 92.0 %collective-permute-start.10 = (bf16[20,6,1024]{2,0,1:T(8,128)(2,1)}, bf16[20,6,1024]{2,0,1:T(8,128)(2,1)}, u32[]{:S(2)}, u32[]{:S(2)}) collective-permute-start(bf16[20,6,1024]{2,0,1:T(8,128)(2,1)} %get-tuple-element.613), channel_id=1, source_target_pairs={{0,8},{8,16},{16,24},{24,32},{32,40},{40,48},{48,56},{56,64},{64,7... | collective-permute-start | bytes 737288 | tf_op jit(solution)/shard_map/ppermute | solution.py:24
  164.8 4.5 copy-start.5
  164.8 4.5 copy-start.15
  164.8 4.5 copy-start.17
  172.8 6.3 %copy-start.6 = (pred[64,400]{1,0:T(8,128)(4,1)S(1)}, pred[64,400]{1,0:T(8,128)(4,1)}, u32[]{:S(2)}) copy-start(pred[64,400]{1,0:T(8,128)(4,1)} %fusion.49) | copy-start | bytes 76804
  172.8 6.3 %copy-start.23 = (f32[8,2,64,2]{2,3,1,0:T(2,128)S(1)}, f32[8,2,64,2]{2,3,1,0:T(2,128)}, u32[]{:S(2)}) copy-start(f32[8,2,64,2]{2,3,1,0:T(2,128)} %custom-call.16) | copy-start | bytes 24580
  172.8 6.3 %copy-start.24 = (f32[8,2,64,2]{2,3,1,0:T(2,128)S(1)}, f32[8,2,64,2]{2,3,1,0:T(2,128)}, u32[]{:S(2)}) copy-start(f32[8,2,64,2]{2,3,1,0:T(2,128)} %custom-call.17) | copy-start | bytes 24580
  231.6 1.9 copy-start.8
  231.6 2.8 copy-start.29
  231.6 2.9 copy-start.25
  233.2 14.0 %copy-start.27 = (bf16[2]{0:T(256)(128)(2,1)S(1)}, bf16[2]{0:T(256)(128)(2,1)}, u32[]{:S(2)}) copy-start(bf16[2]{0:T(256)(128)(2,1)} %get-tuple-element.662) | copy-start | bytes 16
  235.2 14.3 %copy-start.18 = (f32[2,64,16]{2,1,0:T(8,128)}, f32[2,64,16]{2,1,0:T(8,128)S(1)}, u32[]{:S(2)}) copy-start(f32[2,64,16]{2,1,0:T(8,128)S(1)} %copy.271) | copy-start | bytes 24580
  236.1 27.7 %collective-permute-start.17 = (f32[6,16,16]{0,2,1:T(8,128)}, f32[6,16,16]{0,2,1:T(8,128)}, u32[]{:S(2)}, u32[]{:S(2)}) collective-permute-start(f32[6,16,16]{0,2,1:T(8,128)} %bitcast.35), channel_id=1, source_target_pairs={{1,0},{2,1},{3,2},{4,3},{5,4},{6,5},{7,6},{9,8},{10,9},{11,10},{12... | collective-permute-start | bytes 18440 | tf_op jit(solution)/shard_map/ppermute | solution.py:26
  238.2 25.6 %collective-permute-start.16 = (f32[6,16,16]{0,2,1:T(8,128)}, f32[6,16,16]{0,2,1:T(8,128)}, u32[]{:S(2)}, u32[]{:S(2)}) collective-permute-start(f32[6,16,16]{0,2,1:T(8,128)} %bitcast.32), channel_id=1, source_target_pairs={{0,1},{1,2},{2,3},{3,4},{4,5},{5,6},{6,7},{8,9},{9,10},{10,11},{11... | collective-permute-start | bytes 18440 | tf_op jit(solution)/shard_map/ppermute | solution.py:24
  244.4 2.8 copy-start.19
  245.9 24.6 %collective-permute-start.25 = (f32[6,16,16]{0,2,1:T(8,128)}, f32[6,16,16]{0,2,1:T(8,128)}, u32[]{:S(2)}, u32[]{:S(2)}) collective-permute-start(f32[6,16,16]{0,2,1:T(8,128)} %bitcast.47), channel_id=1, source_target_pairs={{1,0},{2,1},{3,2},{4,3},{5,4},{6,5},{7,6},{9,8},{10,9},{11,10},{12... | collective-permute-start | bytes 18440 | tf_op jit(solution)/shard_map/ppermute | solution.py:26
  255.0 4.4 copy-start.22
  259.6 10.8 %collective-permute-start.24 = (f32[6,16,16]{0,2,1:T(8,128)S(1)}, f32[6,16,16]{0,2,1:T(8,128)S(1)}, u32[]{:S(2)}, u32[]{:S(2)}) collective-permute-start(f32[6,16,16]{0,2,1:T(8,128)S(1)} %bitcast.282), channel_id=1, source_target_pairs={{0,1},{1,2},{2,3},{3,4},{4,5},{5,6},{6,7},{8,9},{9,10},{10,11},{11... | collective-permute-start | bytes 18440 | tf_op jit(solution)/shard_map/ppermute | solution.py:24
  264.8 12.9 %collective-permute-start.19 = (f32[20,6,16]{0,2,1:T(8,128)S(1)}, f32[20,6,16]{0,2,1:T(8,128)S(1)}, u32[]{:S(2)}, u32[]{:S(2)}) collective-permute-start(f32[20,6,16]{0,2,1:T(8,128)S(1)} %get-tuple-element.631), channel_id=1, source_target_pairs={{8,0},{16,8},{24,16},{32,24},{40,32},{48,40},{56,48},{64,56},{72,6... | collective-permute-start | bytes 23048 | tf_op jit(solution)/shard_map/ppermute | solution.py:26
  266.9 10.9 %collective-permute-start.18 = (f32[20,6,16]{0,2,1:T(8,128)S(1)}, f32[20,6,16]{0,2,1:T(8,128)S(1)}, u32[]{:S(2)}, u32[]{:S(2)}) collective-permute-start(f32[20,6,16]{0,2,1:T(8,128)S(1)} %get-tuple-element.630), channel_id=1, source_target_pairs={{0,8},{8,16},{16,24},{24,32},{32,40},{40,48},{48,56},{56,64},{64,7... | collective-permute-start | bytes 23048 | tf_op jit(solution)/shard_map/ppermute | solution.py:24
  272.0 8.0 %collective-permute-start.27 = (f32[20,6,16]{0,2,1:T(8,128)}, f32[20,6,16]{0,2,1:T(8,128)S(1)}, u32[]{:S(2)}, u32[]{:S(2)}) collective-permute-start(f32[20,6,16]{0,2,1:T(8,128)} %get-tuple-element.629), channel_id=1, source_target_pairs={{8,0},{16,8},{24,16},{32,24},{40,32},{48,40},{56,48},{64,56},{72,6... | collective-permute-start | bytes 23048 | tf_op jit(solution)/shard_map/ppermute | solution.py:26
  273.9 6.1 %collective-permute-start.26 = (f32[20,6,16]{0,2,1:T(8,128)S(1)}, f32[20,6,16]{0,2,1:T(8,128)S(1)}, u32[]{:S(2)}, u32[]{:S(2)}) collective-permute-start(f32[20,6,16]{0,2,1:T(8,128)S(1)} %get-tuple-element.628), channel_id=1, source_target_pairs={{0,8},{8,16},{16,24},{24,32},{32,40},{40,48},{48,56},{56,64},{64,7... | collective-permute-start | bytes 23048 | tf_op jit(solution)/shard_map/ppermute | solution.py:24
  280.0 4.0 copy-start.7
  336.6 2.6 copy-start.9
  338.1 2.8 copy-start.21
  547.8 36.9 %all-to-all-start = ((f32[8,32,3072]{2,1,0:T(8,128)}), f32[8,32,3072]{2,1,0:T(8,128)S(1)}, u32[]{:S(2)}, u32[]{:S(2)}) async-start(f32[8,32,3072]{2,1,0:T(8,128)} %broadcast_in_dim.136), calls=%async_computation | async-start | bytes 6291456 | tf_op jit(solution)/shard_map/all_to_all | solution.py:35
  554.1 33.2 %copy-start.1 = (bf16[8,16,1024]{2,1,0:T(8,128)(2,1)S(1)}, bf16[8,16,1024]{2,1,0:T(8,128)(2,1)}, u32[]{:S(2)}) copy-start(bf16[8,16,1024]{2,1,0:T(8,128)(2,1)} %param.11) | copy-start | bytes 786436
Sparse Core Ops, SparseCore 0:
  10.8 98.4 all-gather.1
  360.1 184.6 reduce-scatter.3
where the time goes:
time: 602 us; the launch traced here: 594 us
  waiting for transfers between devices  267 us (44%)
  local copies, waits for them, and re-layouts  131 us (22%)
  starting transfers between devices  86.8 us (14%)
  matrix products  51.4 us (9%)
  other arithmetic  25.5 us (4%)
  loops' own time  16.7 us (3%)
  between operations  15.8 us (3%)
    reduce_scatter x1, waiting for transfers between devices, local(): lax.psum_scatter(lax.dot_general(flat, grads, (((0,), (0,)), ((), ())), p...  185 us
    ppermute x14, starting transfers between devices, padded_2(): lax.ppermute(tail, axis, [(i, (i + 1) % count) for i in range(ends)])  55.1 us
    all_gather x1, waiting for transfers between devices, local(): full_weight = lax.all_gather(qkv_weight, 'wide', axis=0, tiled=True)  54.3 us
    dynamic_slice x72, local copies, waits for them, and re-layouts, by_single(): lax.dynamic_slice_in_dim(array, number * group * unit, group * unit, 2)  38.9 us
    ppermute x14, starting transfers between devices, padded_2(): lax.ppermute(head, axis, [((i + 1) % count, i) for i in range(ends)])  27.7 us
    gather x12, local copies, waits for them, and re-layouts, regions_single(): piece = lax.dynamic_slice(padded, start, (region, region) + trailing)  26.3 us
    all_to_all x1, waiting for transfers between devices, copy_for_each(): lax.all_to_all(jnp.broadcast_to(array[None], (peers, *array.shape)), axis...  24.5 us
    unnamed x79, local copies, waits for them, and re-layouts  19.5 us
  transfers between devices with their start and end apart: 31, of which 5 were waited for; matrix products, arithmetic and copies ran while one was open for 21% of the time, Pallas kernels for 0%

commit v1 on v0

v1 whole, which is shorter than its diff:
```python
import functools
import math

import jax
import jax.numpy as jnp
from jax import lax
from jax.experimental import pallas as pl
from jax.experimental.pallas import tpu as pltpu
from jax.sharding import PartitionSpec as P

MESH = pl.DeviceIdType.MESH
F32 = jnp.float32
BF16 = jnp.bfloat16
RADIUS = 6
NEGATIVE = -1e30
HUGE = 1e30
SCALE = 0.125
VMEM_LIMIT = 60 * 1024 * 1024
ANY = pl.BlockSpec(memory_space=pl.ANY)
VM = pl.BlockSpec(memory_space=pltpu.VMEM)

ROWS = {-1: (0, 6, 14), 0: (0, 8, 6), 1: (2, 6, 0)}


def place():
    wide = lax.axis_index("wide")
    narrow = lax.axis_index("narrow")
    return narrow, wide // 2, wide % 2


def device(narrow, chip, core):
    return {"wide": lax.rem(chip, 16) * 2 + core, "narrow": lax.rem(narrow, 8)}


def remote(src, dst, send, recv, to):
    return pltpu.make_async_remote_copy(
        src_ref=src, dst_ref=dst, send_sem=send, recv_sem=recv, device_id=to, device_id_type=MESH
    )


def greet(devices):
    barrier = pltpu.get_barrier_semaphore()
    for to in devices:
        pl.semaphore_signal(barrier, inc=1, device_id=to, device_id_type=MESH)
    pl.semaphore_wait(barrier, len(devices))


def half_of(core):
    return pl.ds(pl.multiple_of(core * 512, 512), 512)


def gather_kernel(
    x_ref, g_ref, w_ref, act_ref, xr_ref, gr_ref, wg_ref, acts_ref,
    h_send, h_recv, h_local, s_send, s_recv, a_send, a_recv, a_local,
    w_send, w_recv, w_local, p_send, p_recv, r_send, r_recv,
):
    n, chip, core = place()
    other = 1 - core
    z = lax.rem(chip, 8)
    xh = chip // 8
    step = 2 * core - 1
    side_chip = chip + step + 16
    up = device(n, xh * 8 + lax.rem(z + 1, 8), core)
    down = device(n, xh * 8 + lax.rem(z + 7, 8), core)
    partner = device(n, (1 - xh) * 8 + z, core)
    sibling = device(n, chip, other)

    peers = [up, down, partner, sibling]
    for dn in (-1, 0, 1):
        for dc in (-1, 0, 1):
            for c in (0, 1):
                if (dn, dc) != (0, 0):
                    peers.append(device(n + dn + 8, chip + dc + 16, c))
    greet(peers)

    sends = []
    own = []
    for t in range(3):
        here = wg_ref.at[t, xh, z, core]
        cp = pltpu.make_async_copy(
            w_ref.at[:, pl.ds(pl.multiple_of(t * 1024 + core * 512, 512), 512)], here, w_local.at[t]
        )
        cp.start()
        own.append(cp)
        cp = remote(
            w_ref.at[:, pl.ds(pl.multiple_of(t * 1024 + other * 512, 512), 512)],
            here, w_send.at[t], w_recv.at[t], sibling,
        )
        cp.start()
        sends.append(cp)

    tensors = ((g_ref, lambda c: gr_ref), (x_ref, lambda c: xr_ref.at[c]))
    locals_ = []
    for i, (src, dst) in enumerate(tensors):
        for dn in (-1, 0, 1):
            lo, count, at = ROWS[dn]
            for side in (0, 1):
                for rel in (0, 1):
                    c = core if rel == 0 else other
                    if side == 0:
                        source = src.at[pl.ds(lo, count), :, :, half_of(c)]
                        target = dst(c).at[pl.ds(at, count), pl.ds(1 + 2 * core, 2)]
                        slot = core
                        to = device(n + dn + 8, chip, c)
                    else:
                        source = src.at[pl.ds(lo, count), pl.ds(core, 1), :, half_of(c)]
                        target = dst(c).at[pl.ds(at, count), pl.ds(5 * other, 1)]
                        slot = 3 - core
                        to = device(n + dn + 8, side_chip, c)
                    if dn == 0 and side == 0 and rel == 0:
                        cp = pltpu.make_async_copy(source, target, h_local.at[i])
                        locals_.append(cp)
                    else:
                        cp = remote(
                            source, target, h_send.at[i, dn + 1, side, rel],
                            h_recv.at[i, dn + 1, slot], to,
                        )
                        sends.append(cp)
                    cp.start()

    act_copy = pltpu.make_async_copy(act_ref, acts_ref.at[core], a_local)
    act_copy.start()
    act_send = remote(act_ref, acts_ref.at[core], a_send, a_recv, sibling)
    act_send.start()
    sends.append(act_send)

    for t in range(3):
        own[t].wait()
        remote(
            w_ref.at[:, pl.ds(0, 512)], wg_ref.at[t, xh, z, other],
            w_send.at[t], w_recv.at[t], sibling,
        ).wait_recv()
    hops = {(0, 0): 4, (0, 1): 3, (1, 0): 3, (1, 1): 4}

    def slab(s, index):
        return wg_ref.at[:, xh if s == 0 else 1 - xh, lax.rem(index + 16, 8)]

    def forward(s, d, k):
        moved = slab(s, z - k if d == 0 else z + k)
        cp = remote(
            moved, moved, r_send.at[s, d, k], r_recv.at[s, d, k], up if d == 0 else down
        )
        cp.start()
        sends.append(cp)

    def arrived(s, d, k):
        landed = slab(s, z - 1 - k if d == 0 else z + 1 + k)
        remote(landed, landed, r_send.at[s, d, k], r_recv.at[s, d, k], up).wait_recv()

    mine = slab(0, z)
    cp = remote(mine, mine, p_send, p_recv, partner)
    cp.start()
    sends.append(cp)
    forward(0, 0, 0)
    forward(0, 1, 0)
    theirs = slab(1, z)
    remote(theirs, theirs, p_send, p_recv, partner).wait_recv()
    forward(1, 0, 0)
    forward(1, 1, 0)

    def finish_region(i, dst):
        locals_[i].wait()
        for dn in (-1, 0, 1):
            lo, count, at = ROWS[dn]
            for piece in range(4):
                if piece < 2:
                    if dn == 0 and piece == 1:
                        continue
                    slot = other if dn == 0 else piece
                    landed = dst.at[pl.ds(at, count), pl.ds(1 + 2 * slot, 2)]
                else:
                    slot = piece
                    landed = dst.at[pl.ds(at, count), pl.ds(0 if piece == 2 else 5, 1)]
                remote(
                    landed, landed, h_send.at[i, dn + 1, 0, 0], h_recv.at[i, dn + 1, slot], sibling
                ).wait_recv()

    for k in range(1, 5):
        for s in range(2):
            for d in range(2):
                if k <= hops[s, d]:
                    arrived(s, d, k - 1)
                if k < hops[s, d]:
                    forward(s, d, k)
        if k == 2:
            finish_region(1, xr_ref.at[core])
            cp = remote(xr_ref.at[core], xr_ref.at[core], s_send, s_recv, sibling)
            cp.start()
            sends.append(cp)
    finish_region(0, gr_ref)
    act_copy.wait()
    remote(act_ref, acts_ref.at[other], a_send, a_recv, sibling).wait_recv()
    remote(xr_ref.at[other], xr_ref.at[other], s_send, s_recv, sibling).wait_recv()
    for cp in sends:
        cp.wait_send()


def gather_all(x4, g4, weight, act):
    dma = pltpu.SemaphoreType.DMA
    return pl.pallas_call(
        gather_kernel,
        out_shape=(
            jax.ShapeDtypeStruct((2, 20, 6, 8, 512), BF16),
            jax.ShapeDtypeStruct((20, 6, 8, 512), BF16),
            jax.ShapeDtypeStruct((3, 2, 8, 2, 32, 512), BF16),
            jax.ShapeDtypeStruct((2, 128, 128), F32),
        ),
        in_specs=[VM] * 4,
        out_specs=(ANY,) * 4,
        scratch_shapes=[
            dma((2, 3, 2, 2)), dma((2, 3, 4)), dma((2,)), dma, dma, dma, dma, dma,
            dma((3,)), dma((3,)), dma((3,)), dma, dma, dma((2, 2, 4)), dma((2, 2, 4)),
        ],
        compiler_params=pltpu.CompilerParams(collective_id=0, has_side_effects=True),
        name="gather_all",
    )(x4, g4, weight, act)


def window_bias(hf):
    n, chip, _ = place()
    shape = (128, 640)
    inner = lax.broadcasted_iota(jnp.int32, shape, 0)
    outer = lax.broadcasted_iota(jnp.int32, shape, 1)
    row, col = outer // 32, outer % 32
    down = row - RADIUS - inner // 16
    across = col - 8 - inner % 16
    grid_row = n * 8 - RADIUS + row
    grid_col = chip * 32 - 8 + 16 * hf + col
    ok = (jnp.abs(down) <= RADIUS) & (jnp.abs(across) <= RADIUS)
    ok = ok & (grid_row >= 0) & (grid_row < 64) & (grid_col >= 0) & (grid_col < 512)
    return jnp.where(ok, 0.0, NEGATIVE)


def nt(a, b):
    return lax.dot_general(a, b, (((1,), (1,)), ((), ())), preferred_element_type=F32)


def nn(a, b):
    return jnp.dot(a, b, preferred_element_type=F32)


def tn(a, b):
    return lax.dot_general(a, b, (((0,), (0,)), ((), ())), preferred_element_type=F32)


def lanes_of(hp):
    return pl.ds(pl.multiple_of(hp * 128, 128), 128)


def head_masks():
    lane = lax.broadcasted_iota(jnp.int32, (128, 128), 1)
    low = lane < 64
    return low, (low.astype(F32).astype(BF16), (1.0 - low.astype(F32)).astype(BF16)), lane


def query_kernel(
    xr_ref, gr_ref, wg_ref, acts_ref,
    attn_ref, dq_ref, ld_ref, qr_ref, grs_ref, kown_ref, vown_ref, xown_ref,
    acc, kr, vr, qown, gown, ldacc, bias,
):
    def own_of(values, hf):
        return values[6:14, 1 + 2 * hf : 3 + 2 * hf].reshape(128, 512)

    for t, region in enumerate((qr_ref, kr, vr)):

        def chunk(i, carry, t=t, region=region):
            rows = pl.ds(pl.multiple_of(i * 192, 192), 192)
            out = nn(xr_ref[0, pl.ds(4 * i, 4)].reshape(192, 512), wg_ref[t, :512])
            out += nn(xr_ref[1, pl.ds(4 * i, 4)].reshape(192, 512), wg_ref[t, 512:])
            acc[pl.ds(4 * i, 4)] = out.reshape(4, 6, 8, 512)
            region[pl.ds(4 * i, 4)] = out.astype(BF16).reshape(4, 48, 512)
            return carry

        lax.fori_loop(0, 5, chunk, 0)
        for hf in range(2):
            own = acc[6:14, 1 + 2 * hf : 3 + 2 * hf].reshape(128, 512).astype(BF16)
            if t == 0:
                qown[hf] = own * SCALE
            elif t == 1:
                kown_ref[hf] = own * SCALE
            else:
                vown_ref[hf] = own

    def regroup(i, carry):
        rows = gr_ref[pl.ds(4 * i, 4)].astype(F32).reshape(192, 512)
        grs_ref[pl.ds(4 * i, 4)] = rows.astype(BF16).reshape(4, 48, 512)
        return carry

    lax.fori_loop(0, 5, regroup, 0)
    for hf in range(2):
        groups = pl.ds(1 + 2 * hf, 2)
        gown[hf] = gr_ref[6:14, groups].astype(F32).reshape(128, 512).astype(BF16)
        for c in range(2):
            xown_ref[hf, :, c * 512 : c * 512 + 512] = (
                xr_ref[c, 6:14, groups].astype(F32).reshape(128, 512).astype(BF16)
            )
        bias[...] = window_bias(hf)
        ldacc[...] = jnp.zeros_like(ldacc)

        def pair(hp, carry, hf=hf):
            lanes = lanes_of(hp)
            low, masks, lane = head_masks()
            keys = kr[:, 16 * hf : 16 * hf + 32, lanes].reshape(640, 128)
            values = vr[:, 16 * hf : 16 * hf + 32, lanes].reshape(640, 128)
            query = qown[hf, :, lanes]
            grad = gown[hf, :, lanes]
            active = acts_ref[hf]
            outs, dqs = [], []
            ld = ldacc[...]
            for j in range(2):
                s = nt(query * masks[j], keys) + bias[...]
                top = jnp.max(s, axis=1, keepdims=True)
                e = jnp.exp(s - top)
                total = jnp.sum(e, axis=1, keepdims=True)
                p = e * (1.0 / total)
                lse = top + jnp.log(total)
                out = nn(p.astype(BF16), values)
                out = out.astype(BF16).astype(F32)
                gm = grad * masks[j]
                delta = jnp.sum(gm.astype(F32) * out, axis=1, keepdims=True)
                dp = nt(gm, values)
                ds = (p * (dp - delta) * SCALE).astype(BF16)
                dqs.append(nn(ds, keys))
                outs.append(out)
                on = active > 0.0
                head = 2 * hp + j
                ld = jnp.where(lane == head, jnp.where(on, lse, HUGE), ld)
                ld = jnp.where(lane == head + 8, jnp.where(on, delta, 0.0), ld)
            ldacc[...] = ld
            attn_ref[hf, :, lanes] = (jnp.where(low, outs[0], outs[1]) * active).astype(BF16)
            dq_ref[hf, :, lanes] = (jnp.where(low, dqs[0], dqs[1]) * active).astype(BF16)
            return carry

        lax.fori_loop(0, 4, pair, 0)
        ld_ref[:, 2 * hf : 2 * hf + 2] = ldacc[...].reshape(8, 2, 8, 128)


def query_side(xr, gr, wg, acts):
    shape = jax.ShapeDtypeStruct
    return pl.pallas_call(
        query_kernel,
        out_shape=(
            shape((2, 128, 512), BF16), shape((2, 128, 512), BF16), shape((8, 4, 8, 128), F32),
            shape((20, 48, 512), BF16), shape((20, 48, 512), BF16),
            shape((2, 128, 512), BF16), shape((2, 128, 512), BF16), shape((2, 128, 1024), BF16),
        ),
        in_specs=[VM] * 4,
        out_specs=(VM,) * 8,
        scratch_shapes=[
            pltpu.VMEM((20, 6, 8, 512), F32), pltpu.VMEM((20, 48, 512), BF16),
            pltpu.VMEM((20, 48, 512), BF16), pltpu.VMEM((2, 128, 512), BF16),
            pltpu.VMEM((2, 128, 512), BF16), pltpu.VMEM((128, 128), F32),
            pltpu.VMEM((128, 640), F32),
        ],
        compiler_params=pltpu.CompilerParams(vmem_limit_bytes=VMEM_LIMIT),
        name="query_side",
    )(xr, gr, wg, acts)


def halo_kernel(ld_ref, out_ref, send, recv, local):
    n, chip, core = place()
    near = [(dn, dc) for dn in (-1, 0, 1) for dc in (-1, 0, 1) if (dn, dc) != (0, 0)]
    greet([device(n + dn + 8, chip + dc + 16, core) for dn, dc in near])
    columns = {-1: (0, 1, 5), 0: (0, 4, 1), 1: (3, 1, 0)}
    copies = []
    for dn, dc in near:
        lo, count, at = ROWS[dn]
        first, width, to = columns[dc]
        cp = remote(
            ld_ref.at[pl.ds(lo, count), pl.ds(first, width)],
            out_ref.at[pl.ds(at, count), pl.ds(to, width)],
            send.at[dn + 1, dc + 1], recv.at[dn + 1, dc + 1],
            device(n + dn + 8, chip + dc + 16, core),
        )
        cp.start()
        copies.append(cp)
    own = pltpu.make_async_copy(ld_ref, out_ref.at[pl.ds(6, 8), pl.ds(1, 4)], local)
    own.start()
    own.wait()
    for cp in copies:
        cp.wait()


def halo(ld):
    dma = pltpu.SemaphoreType.DMA
    return pl.pallas_call(
        halo_kernel,
        out_shape=jax.ShapeDtypeStruct((20, 6, 8, 128), F32),
        in_specs=[VM],
        out_specs=ANY,
        scratch_shapes=[dma((3, 3)), dma((3, 3)), dma],
        compiler_params=pltpu.CompilerParams(collective_id=1, has_side_effects=True),
        name="halo",
    )(ld)


def key_kernel(
    qr_ref, gr_ref, kown_ref, vown_ref, ldr_ref, dq_ref, xown_ref, wg_ref,
    gx_ref, gw_ref, dk, dv, lds, bias,
):
    for hf in range(2):
        bias[...] = window_bias(hf)
        for i in range(5):
            part = ldr_ref[4 * i : 4 * i + 4, 2 * hf : 2 * hf + 4].reshape(128, 128)
            lds[:, 128 * i : 128 * i + 128] = part.T

        def pair(hp, carry, hf=hf):
            lanes = lanes_of(hp)
            low, masks, _ = head_masks()
            query = qr_ref[:, 16 * hf : 16 * hf + 32, lanes].reshape(640, 128)
            grad = gr_ref[:, 16 * hf : 16 * hf + 32, lanes].reshape(640, 128)
            keys = kown_ref[hf, :, lanes]
            values = vown_ref[hf, :, lanes]
            dks, dvs = [], []
            for j in range(2):
                head = 2 * hp + j
                s = nt(keys * masks[j], query) + bias[...]
                p = jnp.exp(s - lds[pl.ds(head, 1), :])
                dvs.append(nn(p.astype(BF16), grad))
                dp = nt(values * masks[j], grad)
                ds = (p * (dp - lds[pl.ds(head + 8, 1), :]) * SCALE).astype(BF16)
                dks.append(nn(ds, query))
            dk[pl.ds(128 * hf, 128), lanes] = jnp.where(low, dks[0], dks[1]).astype(BF16)
            dv[pl.ds(128 * hf, 128), lanes] = jnp.where(low, dvs[0], dvs[1]).astype(BF16)
            return carry

        lax.fori_loop(0, 4, pair, 0)

    def columns(i, carry):
        at = pl.ds(pl.multiple_of(i * 128, 128), 128)
        tokens = xown_ref[:, :, at].reshape(256, 128)
        dq = dq_ref[...].reshape(256, 512)
        total = nt(dq, wg_ref[0, at]) + nt(dk[...], wg_ref[1, at]) + nt(dv[...], wg_ref[2, at])
        gx_ref[:, :, at] = total.reshape(2, 128, 128)
        gw_ref[0, at] = tn(tokens, dq)
        gw_ref[1, at] = tn(tokens, dk[...])
        gw_ref[2, at] = tn(tokens, dv[...])
        return carry

    lax.fori_loop(0, 8, columns, 0)


def key_side(qr, gr, kown, vown, ldr, dq, xown, wg):
    shape = jax.ShapeDtypeStruct
    return pl.pallas_call(
        key_kernel,
        out_shape=(shape((2, 128, 1024), F32), shape((3, 1024, 512), F32)),
        in_specs=[VM] * 8,
        out_specs=(VM,) * 2,
        scratch_shapes=[
            pltpu.VMEM((256, 512), BF16), pltpu.VMEM((256, 512), BF16),
            pltpu.VMEM((128, 640), F32), pltpu.VMEM((128, 640), F32),
        ],
        compiler_params=pltpu.CompilerParams(vmem_limit_bytes=VMEM_LIMIT),
        name="key_side",
    )(qr, gr, kown, vown, ldr, dq, xown, wg)


XPEERS = ((0, 1), (1, 0), (1, 1))


def reduce_kernel(
    p_ref, attn_ref, gx_ref, arx_ref, grx_ref, gw_ref,
    yb, xb, rb, ks, vs, qs, xb2, yb2, qxb, qx, qyb, kv, zb, fin,
    c_send, c_recv, y_send, y_recv, x_send, x_recv, r_send, r_recv,
    x2_send, x2_recv, y2_send, y2_recv, qx_send, qx_recv, qy_send, qy_recv,
    z_send, z_recv, f_send, f_recv, f_local,
):
    n, chip, core = place()
    other = 1 - core
    z = lax.rem(chip, 8)
    xh = chip // 8
    y = n // 2
    xl = lax.rem(n, 2)

    def at(xh_, z_, core_, y_, xl_):
        return device(y_ * 2 + xl_, xh_ * 8 + z_, core_)

    def ypeer(d):
        return lax.rem(y + d, 4)

    def zpeer(d):
        return lax.rem(z + d + 8, 8)

    def flip(value, by):
        return 1 - value if by else value

    peers = [at(xh, zpeer(d), core, y, xl) for d in range(1, 8)]
    peers += [at(1 - xh, z, core, y, flip(xl, b)) for b in (0, 1)]
    for c in (0, 1):
        for d in range(4):
            for b in (0, 1):
                if (c, d, b) != (0, 0, 0):
                    peers.append(at(xh, z, flip(core, c), ypeer(d), flip(xl, b)))
    greet(peers)

    sends = []

    def go(src, dst, send, recv, to):
        cp = remote(src, dst, send, recv, to)
        cp.start()
        sends.append(cp)

    def came(dst, send, recv):
        remote(dst, dst, send, recv, at(xh, z, other, y, xl)).wait_recv()

    def quarter(index):
        return pl.ds(pl.multiple_of(index * 128, 128), 128)

    def ring_chunk(zd, d, s):
        return p_ref.at[0, s, zd, :, :, pl.ds(256 * d, 256)]

    def ring_to(d):
        return at(xh, zpeer(1 if d == 0 else -1), core, y, xl)

    for s in range(2):
        for d in range(2):
            first = zpeer(-1 if d == 0 else 1)
            go(ring_chunk(first, d, s), rb.at[d, 0, s], r_send.at[d, 0, s], r_recv.at[d, 0, s], ring_to(d))
    for d in (1, 3, 2):
        go(
            p_ref.at[1, :, :, :, :, quarter(ypeer(d))], yb.at[d - 1],
            y_send.at[d - 1], y_recv.at[d - 1], at(xh, z, core, ypeer(d), xl),
        )
    for i, (a, b) in enumerate(XPEERS):
        go(
            p_ref.at[2, flip(xh, a), :, flip(xl, b)], xb.at[i], x_send.at[i], x_recv.at[i],
            at(flip(xh, a), z, core, y, flip(xl, b)),
        )
    sibling = at(xh, z, other, y, xl)
    go(attn_ref.at[other], arx_ref, c_send.at[0], c_recv.at[0], sibling)
    go(gx_ref.at[other], grx_ref, c_send.at[1], c_recv.at[1], sibling)

    def first_sums():
        for d in range(3):
            came(yb.at[d], y_send.at[d], y_recv.at[d])

        def add_k(i, carry):
            a, b = i // 8, lax.rem(i, 8)
            total = p_ref[1, a, b, :, :, quarter(y)] + yb[0, a, b]
            ks[a, b] = total + yb[1, a, b] + yb[2, a, b]
            return carry

        lax.fori_loop(0, 16, add_k, 0)
        for i, (a, b) in enumerate(XPEERS):
            go(
                ks.at[flip(xh, a), :, flip(xl, b)], xb2.at[i], x2_send.at[i], x2_recv.at[i],
                at(flip(xh, a), z, core, y, flip(xl, b)),
            )
        for i in range(3):
            came(xb.at[i], x_send.at[i], x_recv.at[i])

        def add_v(i, carry):
            vs[i] = p_ref[2, xh, i, xl] + xb[0, i] + xb[1, i] + xb[2, i]
            return carry

        lax.fori_loop(0, 8, add_v, 0)
        for d in (1, 3, 2):
            go(
                vs.at[:, :, quarter(ypeer(d))], yb2.at[d - 1], y2_send.at[d - 1], y2_recv.at[d - 1],
                at(xh, z, core, ypeer(d), xl),
            )

    for k in range(1, 8):
        for s in range(2):
            for d in range(2):
                came(rb.at[d, k - 1, s], r_send.at[d, k - 1, s], r_recv.at[d, k - 1, s])
                dest = zpeer(-1 - k if d == 0 else k + 1 - 8)
                cols = pl.ds(256 * d, 256)
                if k < 7:
                    rb[d, k - 1, s] = rb[d, k - 1, s] + p_ref[0, s, dest, :, :, cols]
                    go(
                        rb.at[d, k - 1, s], rb.at[d, k, s],
                        r_send.at[d, k, s], r_recv.at[d, k, s], ring_to(d),
                    )
                else:
                    qs[s, :, :, 256 * d : 256 * d + 256] = (
                        rb[d, k - 1, s] + p_ref[0, s, z, :, :, cols]
                    )
        if k == 5:
            first_sums()
    for i, (a, b) in enumerate(XPEERS):
        go(
            qs.at[flip(xh, a), flip(xl, b)], qxb.at[i], qx_send.at[i], qx_recv.at[i],
            at(flip(xh, a), z, core, y, flip(xl, b)),
        )
    for i in range(3):
        came(xb2.at[i], x2_send.at[i], x2_recv.at[i])
        came(yb2.at[i], y2_send.at[i], y2_recv.at[i])
    for i in range(8):
        kv[i, 0] = ks[xh, i, xl] + xb2[0, i] + xb2[1, i] + xb2[2, i]
        kv[i, 1] = vs[i, :, quarter(y)] + yb2[0, i] + yb2[1, i] + yb2[2, i]
    for d in (4, 3, 5, 2, 6, 1, 7):
        go(
            kv.at[zpeer(d)], zb.at[d - 1], z_send.at[d - 1], z_recv.at[d - 1],
            at(xh, zpeer(d), core, y, xl),
        )
    for i in range(3):
        came(qxb.at[i], qx_send.at[i], qx_recv.at[i])
    qx[...] = qs[xh, xl] + qxb[0] + qxb[1] + qxb[2]
    for d in (2, 1, 3):
        go(
            qx.at[:, quarter(ypeer(d))], qyb.at[d - 1], qy_send.at[d - 1], qy_recv.at[d - 1],
            at(xh, z, core, ypeer(d), xl),
        )
    for d in range(7):
        came(zb.at[d], z_send.at[d], z_recv.at[d])
    total = kv[z]
    for d in range(7):
        total = total + zb[d]
    fin[pl.ds(1, 2)] = total
    for d in range(3):
        came(qyb.at[d], qy_send.at[d], qy_recv.at[d])
    fin[0] = qx[:, quarter(y)] + qyb[0] + qyb[1] + qyb[2]

    for d in (2, 1, 3):
        for b in (0, 1):
            go(
                fin, gw_ref.at[core, y], f_send.at[d, b], f_recv.at[core, y],
                at(xh, z, xl, ypeer(d), flip(xl, b)),
            )
    go(fin, gw_ref.at[core, y], f_send.at[0, 1], f_recv.at[core, y], at(xh, z, xl, y, 1 - xl))
    last = remote(fin, gw_ref.at[core, y], f_send.at[0, 0], f_recv.at[core, y], at(xh, z, xl, y, xl))
    keep = pltpu.make_async_copy(fin, gw_ref.at[core, y], f_local)

    @pl.when(core == xl)
    def _():
        keep.start()
        keep.wait()

    @pl.when(core != xl)
    def _():
        last.start()
        last.wait_send()

    for c in range(2):
        for d in range(4):
            if (c, d) == (0, 0):
                @pl.when(core != xl)
                def _():
                    came(gw_ref.at[core, y], f_send.at[0, 0], f_recv.at[core, y])
            else:
                cc = flip(core, c)
                came(gw_ref.at[cc, ypeer(d)], f_send.at[0, 0], f_recv.at[cc, ypeer(d)])
    came(arx_ref, c_send.at[0], c_recv.at[0])
    came(grx_ref, c_send.at[1], c_recv.at[1])
    for cp in sends:
        cp.wait_send()


def reduce_all(partial, attn, gx):
    dma = pltpu.SemaphoreType.DMA
    vmem = lambda *shape: pltpu.VMEM(shape, F32)
    shape = jax.ShapeDtypeStruct
    return pl.pallas_call(
        reduce_kernel,
        out_shape=(
            shape((128, 512), BF16), shape((128, 1024), F32), shape((2, 4, 3, 32, 128), F32)
        ),
        in_specs=[VM] * 3,
        out_specs=(ANY,) * 3,
        scratch_shapes=[
            vmem(3, 2, 8, 2, 32, 128), vmem(3, 8, 32, 512), vmem(2, 7, 2, 2, 32, 256),
            vmem(2, 8, 2, 32, 128), vmem(8, 32, 512), vmem(2, 2, 32, 512),
            vmem(3, 8, 32, 128), vmem(3, 8, 32, 128), vmem(3, 32, 512), vmem(32, 512),
            vmem(3, 32, 128), vmem(8, 2, 32, 128), vmem(7, 2, 32, 128), vmem(3, 32, 128),
            dma((2,)), dma((2,)), dma((3,)), dma((3,)), dma((3,)), dma((3,)),
            dma((2, 7, 2)), dma((2, 7, 2)),
            dma((3,)), dma((3,)), dma((3,)), dma((3,)), dma((3,)), dma((3,)), dma((3,)), dma((3,)),
            dma((7,)), dma((7,)), dma((4, 2)), dma((2, 4)), dma,
        ],
        compiler_params=pltpu.CompilerParams(
            collective_id=2, has_side_effects=True, vmem_limit_bytes=VMEM_LIMIT
        ),
        name="reduce_all",
    )(partial, attn, gx)


def local(image_tokens, qkv_weight, block_list, block_count, out_grad):
    core = lax.axis_index("wide") % 2
    slots = block_list[0]
    live = jnp.arange(2, dtype=jnp.int32) < block_count[0, 0]
    on = jnp.any((slots[:, None] == jnp.arange(2, dtype=jnp.int32)[None]) & live[:, None], axis=0)
    on = on.astype(F32)
    act = jnp.broadcast_to(on[None, :, None, None], (8, 2, 8, 128)).reshape(128, 128)
    xr, gr, wg, acts = gather_all(
        image_tokens.reshape(8, 2, 8, 1024), out_grad.reshape(8, 2, 8, 1024), qkv_weight, act
    )
    wg = wg.reshape(3, 1024, 512)
    attn, dq, ld, qr, grs, kown, vown, xown = query_side(xr, gr, wg, acts)
    ldr = halo(ld)
    gx, partial = key_side(qr, grs, kown, vown, ldr, dq, xown, wg)
    arx, grx, gw = reduce_all(partial.reshape(3, 2, 8, 2, 32, 512), attn, gx)
    mine = lax.dynamic_index_in_dim(attn, core, 0, keepdims=False)
    attn_out = jnp.where(
        core == 0, jnp.concatenate([mine, arx], axis=-1), jnp.concatenate([arx, mine], axis=-1)
    )
    grad_x = (lax.dynamic_index_in_dim(gx, core, 0, keepdims=False) + grx).astype(BF16)
    factor = 1.0 / math.sqrt(32768.0)
    grad_w = jnp.transpose(gw, (3, 2, 0, 1, 4)).reshape(32, 3072) * factor
    return attn_out.reshape(8, 16, 1024), grad_x.reshape(8, 16, 1024), grad_w


def solution(mesh):
    placed = (
        P("narrow", "wide", None),
        P("wide", None),
        P("narrow", "wide"),
        P("narrow", "wide"),
        P("narrow", "wide", None),
    )
    return jax.shard_map(
        local,
        mesh=mesh,
        in_specs=placed,
        out_specs=(P("narrow", "wide", None), P("narrow", "wide", None), P("wide", None)),
        check_vma=False,
    )
```

time: 602 us -> 186 us (0.31); the launches traced: 594 us -> 185 us
  waiting for transfers between devices: 267 us -> 0 us
  Pallas kernels: 0 us -> 177 us
  local copies, waits for them, and re-layouts: 131 us -> 2.07 us
  starting transfers between devices: 86.8 us -> 0 us
  matrix products: 51.4 us -> 0 us
  other arithmetic: 25.5 us -> 4.43 us
  loops' own time: 16.7 us -> 0 us
  between operations: 15.8 us -> 1.36 us
    reduce_scatter x1 -> x0, waiting for transfers between devices: 185 us -> none  [local(): lax.psum_scatter(lax.dot_general(flat, grads, (((0,), (0,)), ((), ())), p...]
    pallas_call x0 -> x5, Pallas kernels: none -> 177 us  [the longest x1 70.4 us: gather_all(): pl.pallas_call(gather_kernel, out_shape=(jax.ShapeDtypeStruct((2, 20, 6,...]
    ppermute x28 -> x0, starting transfers between devices: 82.7 us -> none  [the longest x14 55.1 us: padded_2(): lax.ppermute(tail, axis, [(i, (i + 1) % count) for i in range(ends)])]
    all_gather x1 -> x0, waiting for transfers between devices: 54.3 us -> none  [local(): full_weight = lax.all_gather(qkv_weight, 'wide', axis=0, tiled=True)]
    dot_general x51 -> x0, matrix products: 51.4 us -> none  [the longest x8 8.65 us: query_kernel(): jnp.einsum('bhqk,bkhd->bqhd', dscores, keys, preferred_element_type=jnp.f...]
    dynamic_slice x88 -> x1, local copies, waits for them, and re-layouts: 48.2 us -> 0.01 us  [local(): mine = lax.dynamic_index_in_dim(attn, core, 0, keepdims=False)]
    gather x26 -> x0, local copies, waits for them, and re-layouts: 33.5 us -> none  [the longest x12 26.3 us: regions_single(): piece = lax.dynamic_slice(padded, start, (region, region) + trailing)]
    all_to_all x1 -> x0, waiting for transfers between devices: 24.5 us -> none  [copy_for_each(): lax.all_to_all(jnp.broadcast_to(array[None], (peers, *array.shape)), axis...]
  transfers between devices with their start and end apart: 31 -> 0, of which waited for: 5 -> 0; matrix products, arithmetic and copies ran while one was open for 21% -> 0% of each run, Pallas kernels for 0% -> 0%
where the time goes in v1:
time: 186 us; the launch traced here: 185 us
  Pallas kernels  177 us (95%)
  other arithmetic  4.43 us (2%)
  local copies, waits for them, and re-layouts  2.07 us (1%)
    pallas_call x1, Pallas kernels, gather_all(): pl.pallas_call(gather_kernel, out_shape=(jax.ShapeDtypeStruct((2, 20, 6,...  70.4 us
    pallas_call x1, Pallas kernels, reduce_all(): pl.pallas_call(reduce_kernel, out_shape=(shape((128, 512), BF16), shape((...  57.2 us
    pallas_call x1, Pallas kernels, query_side(): pl.pallas_call(query_kernel, out_shape=(shape((2, 128, 512), BF16), shape...  22.1 us
    pallas_call x1, Pallas kernels, key_side(): pl.pallas_call(key_kernel, out_shape=(shape((2, 128, 1024), F32), shape((...  17.8 us
    pallas_call x1, Pallas kernels, halo(): pl.pallas_call(halo_kernel, out_shape=jax.ShapeDtypeStruct((20, 6, 8, 128...  10 us

profile of v1, /device:TPU:1, one launch (start us, length us, event | category | flops | bytes accessed | tf_op | source)
XLA Modules:
  0.0 185.4 jit_solution(13884143475931754070)
XLA Ops:
  1.3 0.7 and_reduce_fusion
  2.0 0.1 broadcast_in_dim.12
  2.1 0.1 broadcast_in_dim.13
  2.2 0.7 broadcast_in_dim.14.act_ref
  2.9 70.4 %gather_all.1 = (bf16[2,20,6,8,512]{4,3,2,1,0:T(8,128)(2,1)}, bf16[20,6,8,512]{3,2,1,0:T(8,128)(2,1)}, bf16[3,2,8,2,32,512]{5,4,3,2,1,0:T(8,128)(2,1)}, f32[2,128,128]{2,1,0:T(8,128)}) custom-call(bf16[8,2,8,1024]{3,2,1,0:T(8,128)(2,1)} %bitcast.20, bf16[8,2,8,1024]{3,2,1,0:T(8,128)(2,1)} %bitcast.21, bf16[32,3072]{1,0:T(8,128)(2,1)} %w_ref.1, ...), custom_call_target="tpu_custom_call" | custom-call | tf_op jit(solution)/shard_map/gather_all/pallas_call | solution.py:200
  73.4 22.1 %query_side.1 = (bf16[2,128,512]{2,1,0:T(8,128)(2,1)}, bf16[2,128,512]{2,1,0:T(8,128)(2,1)}, f32[8,4,8,128]{3,2,1,0:T(8,128)}, bf16[20,48,512]{2,1,0:T(8,128)(2,...) custom-call(bf16[2,20,6,8,512]{4,3,2,1,0:T(8,128)(2,1)} %get-tuple-e, ...), custom_call_target="tpu_custom_call" | custom-call | tf_op jit(solution)/shard_map/query_side/pallas_call | solution.py:340
  95.5 10.0 %halo.1.ldr_ref = f32[20,6,8,128]{3,2,1,0:T(8,128)} custom-call(f32[8,4,8,128]{3,2,1,0:T(8,128)} %get-tuple-element.29.ld_ref), custom_call_target="tpu_custom_call" | custom-call | tf_op jit(solution)/shard_map/halo/pallas_call | solution.py:386
  105.5 17.8 %key_side.1 = (f32[2,128,1024]{2,1,0:T(8,128)}, f32[3,1024,512]{2,1,0:T(8,128)}) custom-call(bf16[20,48,512]{2,1,0:T(8,128)(2,1)} %get-tuple-element.25.qr_ref, bf16[20,48,512]{2,1,0:T(8,128)(2,1)} %get-tuple-element.26.gr_ref, bf16[2,128,512]{2,1,0:T(8,128)(2,1)} %get-tuple-element.27.kown_ref, bf16[2,128,512]{2,1,0:T(8,128)(2,1)} %get-tuple-element.28.vown_ref, ...), custom_call_target="tpu_custom_call" | custom-call | tf_op jit(solution)/shard_map/key_side/pallas_call | solution.py:445
  123.3 0.0 copy-start
  123.3 57.2 %reduce_all.1 = (bf16[128,512]{1,0:T(8,128)(2,1)}, f32[128,1024]{1,0:T(8,128)}, f32[2,4,3,32,128]{4,3,2,1,0:T(8,128)}) custom-call(f32[3,2,8,2,32,512]{5,4,3,2,1,0:T(8,128)} %bitcast.18, bf16[2,128,512]{2,1,0:T(8,128)(2,1)} %get-tuple-element.24.attn_ref, f32[2,128,1024]{2,1,0:T(8,128)} %get-tuple-element.33.gx_ref), custom_call_target="tpu_custom_call" | custom-call | tf_op jit(solution)/shard_map/reduce_all/pallas_call | solution.py:655
  180.5 0.0 copy-start.1
  180.5 0.0 copy-start.2
  180.5 1.1 multiply_bitcast_fusion
  181.6 0.3 copy.9
  181.8 0.9 mul.15
  182.7 0.0 copy-done
  182.7 1.8 fusion
  184.5 0.0 copy-done.1
  184.6 0.0 copy-done.2
  184.6 0.8 maximum_select_fusion
  (3 shorter events, 0.0 us)
Async XLA Ops:
  123.3 59.4 %copy-start = (f32[2,128,1024]{2,1,0:T(8,128)S(1)}, f32[2,128,1024]{2,1,0:T(8,128)}, u32[]{:S(2)}) copy-start(f32[2,128,1024]{2,1,0:T(8,128)} %get-tuple-element.33.gx_ref) | copy-start | bytes 3145732
  180.5 4.1 %copy-start.1 = (bf16[2,128,512]{2,1,0:T(8,128)(2,1)S(1)}, bf16[2,128,512]{2,1,0:T(8,128)(2,1)}, u32[]{:S(2)}) copy-start(bf16[2,128,512]{2,1,0:T(8,128)(2,1)} %get-tuple-element.24.attn_ref) | copy-start | bytes 786436
  180.5 4.1 %copy-start.2 = (bf16[128,512]{1,0:T(8,128)(2,1)S(1)}, bf16[128,512]{1,0:T(8,128)(2,1)}, u32[]{:S(2)}) copy-start(bf16[128,512]{1,0:T(8,128)(2,1)} %get-tuple-element.34) | copy-start | bytes 393220

commit v2 on v1

v2 whole, which is shorter than its diff:
```python
import functools
import math

import jax
import jax.numpy as jnp
from jax import lax
from jax.experimental import pallas as pl
from jax.experimental.pallas import tpu as pltpu
from jax.sharding import PartitionSpec as P

MESH = pl.DeviceIdType.MESH
F32 = jnp.float32
BF16 = jnp.bfloat16
RADIUS = 6
NEGATIVE = -1e30
HUGE = 1e30
SCALE = 0.125
VMEM_LIMIT = 60 * 1024 * 1024
ANY = pl.BlockSpec(memory_space=pl.ANY)
VM = pl.BlockSpec(memory_space=pltpu.VMEM)

ROWS = {-1: (0, 6, 14), 0: (0, 8, 6), 1: (2, 6, 0)}


def place():
    wide = lax.axis_index("wide")
    narrow = lax.axis_index("narrow")
    return narrow, wide // 2, wide % 2


def device(narrow, chip, core):
    return {"wide": lax.rem(chip, 16) * 2 + core, "narrow": lax.rem(narrow, 8)}


def remote(src, dst, send, recv, to):
    return pltpu.make_async_remote_copy(
        src_ref=src, dst_ref=dst, send_sem=send, recv_sem=recv, device_id=to, device_id_type=MESH
    )


def greet(devices):
    barrier = pltpu.get_barrier_semaphore()
    for to in devices:
        pl.semaphore_signal(barrier, inc=1, device_id=to, device_id_type=MESH)
    pl.semaphore_wait(barrier, len(devices))


def half_of(core):
    return pl.ds(pl.multiple_of(core * 512, 512), 512)


def gather_kernel(
    x_ref, g_ref, w_ref, act_ref, xr_ref, gr_ref, wg_ref, acts_ref,
    h_send, h_recv, h_local, s_send, s_recv, a_send, a_recv, a_local,
    w_send, w_recv, w_local, p_send, p_recv, r_send, r_recv,
):
    n, chip, core = place()
    other = 1 - core
    z = lax.rem(chip, 8)
    xh = chip // 8
    step = 2 * core - 1
    side_chip = chip + step + 16
    up = device(n, xh * 8 + lax.rem(z + 1, 8), core)
    down = device(n, xh * 8 + lax.rem(z + 7, 8), core)
    partner = device(n + 1 - 2 * lax.rem(n, 2), (1 - xh) * 8 + z, core)
    sibling = device(n, chip, other)

    peers = [up, down, partner, sibling]
    for dn in (-1, 0, 1):
        for dc in (-1, 0, 1):
            for c in (0, 1):
                if (dn, dc) != (0, 0):
                    peers.append(device(n + dn + 8, chip + dc + 16, c))
    greet(peers)

    sends = []
    own = []
    for t in range(3):
        here = wg_ref.at[t, xh, z, core]
        cp = pltpu.make_async_copy(
            w_ref.at[:, pl.ds(pl.multiple_of(t * 1024 + core * 512, 512), 512)], here, w_local.at[t]
        )
        cp.start()
        own.append(cp)
        cp = remote(
            w_ref.at[:, pl.ds(pl.multiple_of(t * 1024 + other * 512, 512), 512)],
            here, w_send.at[t], w_recv.at[t], sibling,
        )
        cp.start()
        sends.append(cp)

    for t in range(3):
        own[t].wait()
        remote(
            w_ref.at[:, pl.ds(0, 512)], wg_ref.at[t, xh, z, other],
            w_send.at[t], w_recv.at[t], sibling,
        ).wait_recv()
    hops = {(0, 0): 4, (0, 1): 3, (1, 0): 3, (1, 1): 4}

    def slab(s, index):
        return wg_ref.at[:, xh if s == 0 else 1 - xh, lax.rem(index + 16, 8)]

    def forward(s, d, k):
        moved = slab(s, z - k if d == 0 else z + k)
        cp = remote(
            moved, moved, r_send.at[s, d, k], r_recv.at[s, d, k], up if d == 0 else down
        )
        cp.start()
        sends.append(cp)

    def arrived(s, d, k):
        landed = slab(s, z - 1 - k if d == 0 else z + 1 + k)
        remote(landed, landed, r_send.at[s, d, k], r_recv.at[s, d, k], up).wait_recv()

    mine = slab(0, z)
    cp = remote(mine, mine, p_send, p_recv, partner)
    cp.start()
    sends.append(cp)
    forward(0, 0, 0)
    forward(0, 1, 0)
    tensors = ((g_ref, lambda c: gr_ref), (x_ref, lambda c: xr_ref.at[c]))
    locals_ = []
    for i, (src, dst) in enumerate(tensors):
        for dn in (-1, 0, 1):
            lo, count, at = ROWS[dn]
            for side in (0, 1):
                for rel in (0, 1):
                    c = core if rel == 0 else other
                    if side == 0:
                        source = src.at[pl.ds(lo, count), :, :, half_of(c)]
                        target = dst(c).at[pl.ds(at, count), pl.ds(1 + 2 * core, 2)]
                        slot = core
                        to = device(n + dn + 8, chip, c)
                    else:
                        source = src.at[pl.ds(lo, count), pl.ds(core, 1), :, half_of(c)]
                        target = dst(c).at[pl.ds(at, count), pl.ds(5 * other, 1)]
                        slot = 3 - core
                        to = device(n + dn + 8, side_chip, c)
                    if dn == 0 and side == 0 and rel == 0:
                        cp = pltpu.make_async_copy(source, target, h_local.at[i])
                        locals_.append(cp)
                    else:
                        cp = remote(
                            source, target, h_send.at[i, dn + 1, side, rel],
                            h_recv.at[i, dn + 1, slot], to,
                        )
                        sends.append(cp)
                    cp.start()

    act_copy = pltpu.make_async_copy(act_ref, acts_ref.at[core], a_local)
    act_copy.start()
    act_send = remote(act_ref, acts_ref.at[core], a_send, a_recv, sibling)
    act_send.start()
    sends.append(act_send)

    theirs = slab(1, z)
    remote(theirs, theirs, p_send, p_recv, partner).wait_recv()
    forward(1, 0, 0)
    forward(1, 1, 0)

    def finish_region(i, dst):
        locals_[i].wait()
        for dn in (-1, 0, 1):
            lo, count, at = ROWS[dn]
            for piece in range(4):
                if piece < 2:
                    if dn == 0 and piece == 1:
                        continue
                    slot = other if dn == 0 else piece
                    landed = dst.at[pl.ds(at, count), pl.ds(1 + 2 * slot, 2)]
                else:
                    slot = piece
                    landed = dst.at[pl.ds(at, count), pl.ds(0 if piece == 2 else 5, 1)]
                remote(
                    landed, landed, h_send.at[i, dn + 1, 0, 0], h_recv.at[i, dn + 1, slot], sibling
                ).wait_recv()

    for k in range(1, 5):
        for s in range(2):
            for d in range(2):
                if k <= hops[s, d]:
                    arrived(s, d, k - 1)
                if k < hops[s, d]:
                    forward(s, d, k)
        if k == 2:
            finish_region(1, xr_ref.at[core])
            cp = remote(xr_ref.at[core], xr_ref.at[core], s_send, s_recv, sibling)
            cp.start()
            sends.append(cp)
    finish_region(0, gr_ref)
    act_copy.wait()
    remote(act_ref, acts_ref.at[other], a_send, a_recv, sibling).wait_recv()
    remote(xr_ref.at[other], xr_ref.at[other], s_send, s_recv, sibling).wait_recv()
    for cp in sends:
        cp.wait_send()


def gather_all(x4, g4, weight, act):
    dma = pltpu.SemaphoreType.DMA
    return pl.pallas_call(
        gather_kernel,
        out_shape=(
            jax.ShapeDtypeStruct((2, 20, 6, 8, 512), BF16),
            jax.ShapeDtypeStruct((20, 6, 8, 512), BF16),
            jax.ShapeDtypeStruct((3, 2, 8, 2, 32, 512), BF16),
            jax.ShapeDtypeStruct((2, 128, 128), F32),
        ),
        in_specs=[VM] * 4,
        out_specs=(ANY,) * 4,
        scratch_shapes=[
            dma((2, 3, 2, 2)), dma((2, 3, 4)), dma((2,)), dma, dma, dma, dma, dma,
            dma((3,)), dma((3,)), dma((3,)), dma, dma, dma((2, 2, 4)), dma((2, 2, 4)),
        ],
        compiler_params=pltpu.CompilerParams(collective_id=0, has_side_effects=True),
        name="gather_all",
    )(x4, g4, weight, act)


def window_bias(hf):
    n, chip, _ = place()
    shape = (128, 640)
    inner = lax.broadcasted_iota(jnp.int32, shape, 0)
    outer = lax.broadcasted_iota(jnp.int32, shape, 1)
    row, col = outer // 32, outer % 32
    down = row - RADIUS - inner // 16
    across = col - 8 - inner % 16
    grid_row = n * 8 - RADIUS + row
    grid_col = chip * 32 - 8 + 16 * hf + col
    ok = (jnp.abs(down) <= RADIUS) & (jnp.abs(across) <= RADIUS)
    ok = ok & (grid_row >= 0) & (grid_row < 64) & (grid_col >= 0) & (grid_col < 512)
    return jnp.where(ok, 0.0, NEGATIVE)


def nt(a, b):
    return lax.dot_general(a, b, (((1,), (1,)), ((), ())), preferred_element_type=F32)


def nn(a, b):
    return jnp.dot(a, b, preferred_element_type=F32)


def tn(a, b):
    return lax.dot_general(a, b, (((0,), (0,)), ((), ())), preferred_element_type=F32)


def lanes_of(hp):
    return pl.ds(pl.multiple_of(hp * 128, 128), 128)


def head_masks():
    lane = lax.broadcasted_iota(jnp.int32, (128, 128), 1)
    low = lane < 64
    return low, (low.astype(F32).astype(BF16), (1.0 - low.astype(F32)).astype(BF16)), lane


def query_kernel(
    xr_ref, gr_ref, wg_ref, acts_ref,
    attn_ref, dq_ref, ld_ref, qr_ref, grs_ref, kown_ref, vown_ref, xt_ref,
    acc, kr, vr, qown, gown, ldacc, ldall, bias,
):
    def own_of(values, hf):
        return values[6:14, 1 + 2 * hf : 3 + 2 * hf].reshape(128, 512)

    for t, region in enumerate((qr_ref, kr, vr)):

        def chunk(i, carry, t=t, region=region):
            rows = pl.ds(pl.multiple_of(i * 192, 192), 192)
            out = nn(xr_ref[0, pl.ds(4 * i, 4)].reshape(192, 512), wg_ref[t, :512])
            out += nn(xr_ref[1, pl.ds(4 * i, 4)].reshape(192, 512), wg_ref[t, 512:])
            acc[pl.ds(4 * i, 4)] = out.reshape(4, 6, 8, 512)
            region[pl.ds(4 * i, 4)] = out.astype(BF16).reshape(4, 48, 512)
            return carry

        lax.fori_loop(0, 5, chunk, 0)
        for hf in range(2):
            own = acc[6:14, 1 + 2 * hf : 3 + 2 * hf].reshape(128, 512).astype(BF16)
            if t == 0:
                qown[hf] = own * SCALE
            elif t == 1:
                kown_ref[hf] = own * SCALE
            else:
                vown_ref[hf] = own

    def regroup(i, carry):
        rows = gr_ref[pl.ds(4 * i, 4)].astype(F32).reshape(192, 512)
        grs_ref[pl.ds(4 * i, 4)] = rows.astype(BF16).reshape(4, 48, 512)
        return carry

    lax.fori_loop(0, 5, regroup, 0)
    for hf in range(2):
        groups = pl.ds(1 + 2 * hf, 2)
        gown[hf] = gr_ref[6:14, groups].astype(F32).reshape(128, 512).astype(BF16)
        for c in range(2):
            tokens = xr_ref[c, 6:14, groups].astype(F32).reshape(128, 512)
            for i in range(4):
                xt_ref[512 * c + 128 * i : 512 * c + 128 * i + 128, 128 * hf : 128 * hf + 128] = (
                    tokens[:, 128 * i : 128 * i + 128].T.astype(BF16)
                )
        bias[...] = window_bias(hf)
        ldacc[...] = jnp.zeros_like(ldacc)

        def pair(hp, carry, hf=hf):
            lanes = lanes_of(hp)
            low, masks, lane = head_masks()
            keys = kr[:, 16 * hf : 16 * hf + 32, lanes].reshape(640, 128)
            values = vr[:, 16 * hf : 16 * hf + 32, lanes].reshape(640, 128)
            query = qown[hf, :, lanes]
            grad = gown[hf, :, lanes]
            active = acts_ref[hf]
            outs, dqs = [], []
            ld = ldacc[...]
            for j in range(2):
                s = nt(query * masks[j], keys) + bias[...]
                top = jnp.max(s, axis=1, keepdims=True)
                e = jnp.exp(s - top)
                total = jnp.sum(e, axis=1, keepdims=True)
                p = e * (1.0 / total)
                lse = top + jnp.log(total)
                out = nn(p.astype(BF16), values)
                out = out.astype(BF16).astype(F32)
                gm = grad * masks[j]
                delta = jnp.sum(gm.astype(F32) * out, axis=1, keepdims=True)
                dp = nt(gm, values)
                ds = (p * (dp - delta) * SCALE).astype(BF16)
                dqs.append(nn(ds, keys))
                outs.append(out)
                on = active > 0.0
                head = 2 * hp + j
                ld = jnp.where(lane == head, jnp.where(on, lse, HUGE), ld)
                ld = jnp.where(lane == head + 8, jnp.where(on, delta, 0.0), ld)
            ldacc[...] = ld
            attn_ref[hf, :, lanes] = (jnp.where(low, outs[0], outs[1]) * active).astype(BF16)
            dq_ref[hf, :, lanes] = (jnp.where(low, dqs[0], dqs[1]) * active).astype(BF16)
            return carry

        lax.fori_loop(0, 4, pair, 0)
        ldall[:, 16 * hf : 16 * hf + 16, :] = ldacc[...].reshape(8, 16, 128)
    for i in range(2):
        ld_ref[:, 128 * i : 128 * i + 128] = ldall[4 * i : 4 * i + 4].reshape(128, 128).T[:16]


def query_side(xr, gr, wg, acts):
    shape = jax.ShapeDtypeStruct
    return pl.pallas_call(
        query_kernel,
        out_shape=(
            shape((2, 128, 512), BF16), shape((2, 128, 512), BF16), shape((16, 256), F32),
            shape((20, 48, 512), BF16), shape((20, 48, 512), BF16),
            shape((2, 128, 512), BF16), shape((2, 128, 512), BF16), shape((1024, 256), BF16),
        ),
        in_specs=[VM] * 4,
        out_specs=(VM,) * 8,
        scratch_shapes=[
            pltpu.VMEM((20, 6, 8, 512), F32), pltpu.VMEM((20, 48, 512), BF16),
            pltpu.VMEM((20, 48, 512), BF16), pltpu.VMEM((2, 128, 512), BF16),
            pltpu.VMEM((2, 128, 512), BF16), pltpu.VMEM((128, 128), F32),
            pltpu.VMEM((8, 32, 128), F32), pltpu.VMEM((128, 640), F32),
        ],
        compiler_params=pltpu.CompilerParams(vmem_limit_bytes=VMEM_LIMIT),
        name="query_side",
    )(xr, gr, wg, acts)


XPEERS = ((0, 1), (1, 0), (1, 1))
NEAR = tuple((dn, dc) for dn in (-1, 0, 1) for dc in (-1, 0, 1) if (dn, dc) != (0, 0))
FIRST = ["x", "y", "z", "z"] + ["y", "x"] * 4
SLOT = [FIRST[:b].count(FIRST[b]) for b in range(12)]
LATE = [b for b in range(12) if FIRST[b] != "z"]
BATCHES = (LATE[:6], LATE[6:])


def block_of(t, hp):
    return hp if t == 0 else 4 + 2 * hp + (t - 1)


def back_kernel(
    qr_ref, gr_ref, kown_ref, vown_ref, ld_ref, dq_ref, xt_ref, wg_ref, attn_ref,
    attn_out, gx_out, gw_out,
    p, sx, sy, sz, rx, ry, rz, rx2, ry2, mz, rzx, rzy, cz, rc, fin,
    dk, dv, lds, ldb, bias, gx, gxr, gxo, wv,
    ld_send, ld_recv, w_sem, o_sem, a_send, a_recv, g_send, g_recv,
    x_send, x_recv, y_send, y_recv, z_send, z_recv,
    x2_send, x2_recv, y2_send, y2_recv, zx_send, zx_recv, zy_send, zy_recv,
    c_send, c_recv, f_send, f_recv, f_local,
):
    n, chip, core = place()
    other = 1 - core
    z = lax.rem(chip, 8)
    xh = chip // 8
    y = n // 2
    xl = lax.rem(n, 2)

    def at(xh_, z_, core_, y_, xl_):
        return device(y_ * 2 + xl_, xh_ * 8 + z_, core_)

    def ypeer(d):
        return lax.rem(y + d, 4)

    def zpeer(d):
        return lax.rem(z + d + 8, 8)

    def flip(value, by):
        return 1 - value if by else value

    sibling = at(xh, z, other, y, xl)
    peers = [device(n + dn + 8, chip + dc + 16, core) for dn, dc in NEAR]
    peers += [at(xh, zpeer(d), core, y, xl) for d in range(1, 8)]
    peers += [at(1 - xh, z, core, y, flip(xl, b)) for b in (0, 1)]
    for c in (0, 1):
        for d in range(4):
            for b in (0, 1):
                if (c, d, b) != (0, 0, 0):
                    peers.append(at(xh, z, flip(core, c), ypeer(d), flip(xl, b)))
    greet(peers)

    sends = []

    def go(src, dst, send, recv, to):
        cp = remote(src, dst, send, recv, to)
        cp.start()
        sends.append(cp)

    def came(dst, send, recv):
        remote(dst, dst, send, recv, sibling).wait_recv()

    def xpeer(i):
        a, b = XPEERS[i]
        return flip(xh, a), flip(xl, b), at(flip(xh, a), z, core, y, flip(xl, b))

    for dn, dc in NEAR:
        go(
            ld_ref, ldb.at[1 - dn, 1 - dc], ld_send.at[dn + 1, dc + 1], ld_recv.at[1 - dn, 1 - dc],
            device(n + dn + 8, chip + dc + 16, core),
        )
    weights = pltpu.make_async_copy(wg_ref, wv, w_sem)
    weights.start()

    def first(b):
        i = SLOT[b]
        if FIRST[b] == "x":
            for d in (2, 0, 1):
                a, l, to = xpeer(d)
                go(p.at[b, a, :, l], rx.at[i, d], x_send.at[i, d], x_recv.at[i, d], to)
        elif FIRST[b] == "y":
            for d in (2, 1, 3):
                to = at(xh, z, core, ypeer(d), xl)
                go(
                    p.at[b, :, :, :, ypeer(d)], ry.at[i, d - 1],
                    y_send.at[i, d - 1], y_recv.at[i, d - 1], to,
                )
        else:
            for d in (4, 3, 5, 2, 6, 1, 7):
                to = at(xh, zpeer(d), core, y, xl)
                go(
                    p.at[b, :, zpeer(d)], rz.at[i, d - 1],
                    z_send.at[i, d - 1], z_recv.at[i, d - 1], to,
                )

    def second(b):
        i = SLOT[b]
        if FIRST[b] == "x":
            for d in range(3):
                came(rx.at[i, d], x_send.at[i, d], x_recv.at[i, d])

            def add_x(j, carry):
                sx[i, j] = p[b, xh, j, xl] + rx[i, 0, j] + rx[i, 1, j] + rx[i, 2, j]
                return carry

            lax.fori_loop(0, 8, add_x, 0)
            for d in (2, 1, 3):
                go(
                    sx.at[i, :, ypeer(d)], ry2.at[i, d - 1], y2_send.at[i, d - 1],
                    y2_recv.at[i, d - 1], at(xh, z, core, ypeer(d), xl),
                )
        elif FIRST[b] == "y":
            for d in range(3):
                came(ry.at[i, d], y_send.at[i, d], y_recv.at[i, d])

            def add_y(j, carry):
                for a in range(2):
                    total = p[b, a, j, :, y] + ry[i, 0, a, j]
                    sy[i, a, j] = total + ry[i, 1, a, j] + ry[i, 2, a, j]
                return carry

            lax.fori_loop(0, 8, add_y, 0)
            for d in (2, 0, 1):
                a, l, to = xpeer(d)
                go(sy.at[i, a, :, l], rx2.at[i, d], x2_send.at[i, d], x2_recv.at[i, d], to)
        else:
            for d in range(7):
                came(rz.at[i, d], z_send.at[i, d], z_recv.at[i, d])
            for a in range(2):
                for l in range(2):
                    total = p[b, a, z, l]
                    for d in range(7):
                        total = total + rz[i, d, a, l]
                    sz[i, a, l] = total
            for d in (2, 0, 1):
                a, l, to = xpeer(d)
                go(sz.at[i, a, l], rzx.at[i, d], zx_send.at[i, d], zx_recv.at[i, d], to)

    def third(b):
        i = SLOT[b]
        if FIRST[b] == "x":
            for d in range(3):
                came(ry2.at[i, d], y2_send.at[i, d], y2_recv.at[i, d])
            for j in range(8):
                cz[j, LATE.index(b)] = sx[i, j, y] + ry2[i, 0, j] + ry2[i, 1, j] + ry2[i, 2, j]
        elif FIRST[b] == "y":
            for d in range(3):
                came(rx2.at[i, d], x2_send.at[i, d], x2_recv.at[i, d])
            for j in range(8):
                cz[j, LATE.index(b)] = sy[i, xh, j, xl] + rx2[i, 0, j] + rx2[i, 1, j] + rx2[i, 2, j]
        else:
            for d in range(3):
                came(rzx.at[i, d], zx_send.at[i, d], zx_recv.at[i, d])
            mz[i] = sz[i, xh, xl] + rzx[i, 0] + rzx[i, 1] + rzx[i, 2]
            for d in (2, 1, 3):
                go(
                    mz.at[i, ypeer(d)], rzy.at[i, d - 1], zy_send.at[i, d - 1],
                    zy_recv.at[i, d - 1], at(xh, z, core, ypeer(d), xl),
                )

    def spread(h):
        lo, count = LATE.index(BATCHES[h][0]), len(BATCHES[h])
        for d in (4, 3, 5, 2, 6, 1, 7):
            go(
                cz.at[zpeer(d), pl.ds(lo, count)], rc.at[d - 1, pl.ds(lo, count)],
                c_send.at[h, d - 1], c_recv.at[h, d - 1], at(xh, zpeer(d), core, y, xl),
            )

    factor = 1.0 / math.sqrt(32768.0)

    def keep(b, total):
        t, hp = (0, b) if b < 4 else ((b - 4) % 2 + 1, (b - 4) // 2)
        fin[t, :, 128 * hp : 128 * hp + 128] = total * factor

    def last(h):
        lo, count = LATE.index(BATCHES[h][0]), len(BATCHES[h])
        for d in range(7):
            landed = rc.at[d, pl.ds(lo, count)]
            came(landed, c_send.at[h, d], c_recv.at[h, d])
        for b in BATCHES[h]:
            i = LATE.index(b)
            total = cz[z, i]
            for d in range(7):
                total = total + rc[d, i]
            keep(b, total)

    def last_z(b):
        i = SLOT[b]
        for d in range(3):
            came(rzy.at[i, d], zy_send.at[i, d], zy_recv.at[i, d])
        keep(b, mz[i, y] + rzy[i, 0] + rzy[i, 1] + rzy[i, 2])

    def product(blocks, columns):
        def rows(i, carry):
            out = nn(xt_ref[pl.ds(pl.multiple_of(i * 256, 256), 256), :], columns)
            out = out.reshape(4, 2, 4, 8, 128 * len(blocks))
            for j, b in enumerate(blocks):
                p[b, i // 2, pl.ds(4 * lax.rem(i, 2), 4)] = out[..., 128 * j : 128 * j + 128]
            return carry

        lax.fori_loop(0, 4, rows, 0)

    dq = dq_ref[...].reshape(256, 512)
    for half in range(2):
        product((2 * half, 2 * half + 1), dq[:, 256 * half : 256 * half + 256])
        first(2 * half)
        first(2 * half + 1)
    go(attn_ref.at[other], attn_out.at[:, half_of(core)], a_send, a_recv, sibling)
    attn_own = pltpu.make_async_copy(attn_ref.at[core], attn_out.at[:, half_of(core)], o_sem.at[0])
    attn_own.start()

    for hf in range(2):
        bias[hf] = window_bias(hf)
    ldb[1, 1] = ld_ref[...]
    for dn, dc in NEAR:
        came(ldb.at[1 - dn, 1 - dc], ld_send.at[dn + 1, dc + 1], ld_recv.at[1 - dn, 1 - dc])
    column = lax.rem(lax.broadcasted_iota(jnp.int32, (16, 256), 1), 32)
    for hf in range(2):
        parts = []
        for r in range(3):
            left, mid, right = ldb[r, 0], ldb[r, 1], ldb[r, 2]
            if hf == 0:
                part = jnp.where(column < 8, pltpu.roll(left, 232, 1), pltpu.roll(mid, 8, 1))
            else:
                part = jnp.where(column < 24, pltpu.roll(mid, 248, 1), pltpu.roll(right, 24, 1))
            parts.append(part)
        lds[hf] = pltpu.roll(jnp.concatenate(parts, axis=1), 768 - 64, 1)[:, :640]

    low, masks, _ = head_masks()
    for hp in range(4):
        lanes = slice(128 * hp, 128 * hp + 128)

        def side(hf, carry, hp=hp, lanes=lanes):
            window = pl.ds(pl.multiple_of(16 * hf, 16), 32)
            query = qr_ref[:, window, lanes].reshape(640, 128)
            grad = gr_ref[:, window, lanes].reshape(640, 128)
            keys = kown_ref[hf, :, lanes]
            values = vown_ref[hf, :, lanes]
            dks, dvs = [], []
            for j in range(2):
                head = 2 * hp + j
                s = nt(keys * masks[j], query) + bias[hf]
                e = jnp.exp(s - lds[hf, head : head + 1, :])
                dvs.append(nn(e.astype(BF16), grad))
                dp = nt(values * masks[j], grad)
                ds = (e * (dp - lds[hf, head + 8 : head + 9, :]) * SCALE).astype(BF16)
                dks.append(nn(ds, query))
            dk[hp, hf] = jnp.where(low, dks[0], dks[1]).astype(BF16)
            dv[hp, hf] = jnp.where(low, dvs[0], dvs[1]).astype(BF16)
            return carry

        lax.fori_loop(0, 2, side, 0)
        both = jnp.concatenate([dk[hp].reshape(256, 128), dv[hp].reshape(256, 128)], axis=1)
        blocks = (block_of(1, hp), block_of(2, hp))
        product(blocks, both)
        first(blocks[0])
        first(blocks[1])
        if hp == 1:
            second(0)
            second(1)
        if hp == 2:
            second(block_of(1, 0))
            second(block_of(2, 0))
            second(2)
            second(3)
            third(0)
            third(1)

    weights.wait()

    def gradients(t):
        source = dk if t == 1 else dv
        return jnp.concatenate([source[h].reshape(256, 128) for h in range(4)], axis=1)

    all_k, all_v = gradients(1), gradients(2)

    def input_columns(i, carry):
        rows = pl.ds(pl.multiple_of(i * 256, 256), 256)
        total = nt(dq, wv[0, rows]) + nt(all_k, wv[1, rows]) + nt(all_v, wv[2, rows])
        gx[:, :, rows] = total.reshape(2, 128, 256)
        return carry

    lax.fori_loop(0, 4, input_columns, 0)
    go(gx.at[other], gxr, g_send, g_recv, sibling)

    second(block_of(1, 1))
    second(block_of(2, 1))
    third(block_of(1, 0))
    third(block_of(2, 0))
    third(2)
    third(3)
    third(block_of(1, 1))
    third(block_of(2, 1))
    spread(0)
    came(gxr, g_send, g_recv)
    gxo[...] = (gx[core] + gxr[...]).astype(BF16)
    gx_own = pltpu.make_async_copy(gxo, gx_out, o_sem.at[1])
    gx_own.start()
    second(block_of(1, 2))
    second(block_of(2, 2))
    second(block_of(1, 3))
    second(block_of(2, 3))
    last_z(2)
    last_z(3)
    third(block_of(1, 2))
    third(block_of(2, 2))
    last(0)
    third(block_of(1, 3))
    third(block_of(2, 3))
    spread(1)
    last(1)

    mine = pl.ds(pl.multiple_of(8 * y, 8), 8)

    def columns(t, c):
        return pl.ds(pl.multiple_of(t * 1024 + c * 512, 512), 512)

    for t in range(3):
        spot = gw_out.at[mine, columns(t, core)]
        for d in (2, 1, 3):
            for b in (0, 1):
                go(
                    fin.at[t], spot, f_send.at[d, b, t], f_recv.at[core, y, t],
                    at(xh, z, xl, ypeer(d), flip(xl, b)),
                )
        go(fin.at[t], spot, f_send.at[0, 1, t], f_recv.at[core, y, t], at(xh, z, xl, y, 1 - xl))
        away = remote(
            fin.at[t], spot, f_send.at[0, 0, t], f_recv.at[core, y, t], at(xh, z, xl, y, xl)
        )
        here = pltpu.make_async_copy(fin.at[t], spot, f_local.at[t])

        @pl.when(core == xl)
        def _():
            here.start()
            here.wait()

        @pl.when(core != xl)
        def _():
            away.start()
            away.wait_send()

    attn_own.wait()
    gx_own.wait()
    came(attn_out.at[:, half_of(other)], a_send, a_recv)
    for t in range(3):
        for c in range(2):
            for d in range(4):
                cc, yy = flip(core, c), ypeer(d)
                spot = gw_out.at[pl.ds(pl.multiple_of(8 * yy, 8), 8), columns(t, cc)]
                if (c, d) == (0, 0):

                    @pl.when(core != xl)
                    def _():
                        came(spot, f_send.at[0, 0, t], f_recv.at[cc, yy, t])
                else:
                    came(spot, f_send.at[0, 0, t], f_recv.at[cc, yy, t])
    for cp in sends:
        cp.wait_send()


def back(qr, gr, kown, vown, ld, dq, xt, wg, attn):
    dma = pltpu.SemaphoreType.DMA
    vmem = lambda *shape: pltpu.VMEM(shape, F32)
    shape = jax.ShapeDtypeStruct
    nx, ny, nz, nl = FIRST.count("x"), FIRST.count("y"), FIRST.count("z"), len(LATE)
    return pl.pallas_call(
        back_kernel,
        out_shape=(
            shape((128, 1024), BF16), shape((128, 1024), BF16), shape((32, 3072), F32),
        ),
        in_specs=[VM] * 7 + [ANY, VM],
        out_specs=(ANY,) * 3,
        scratch_shapes=[
            vmem(12, 2, 8, 2, 4, 8, 128),
            vmem(nx, 8, 4, 8, 128), vmem(ny, 2, 8, 2, 8, 128), vmem(nz, 2, 2, 4, 8, 128),
            vmem(nx, 3, 8, 4, 8, 128), vmem(ny, 3, 2, 8, 2, 8, 128), vmem(nz, 7, 2, 2, 4, 8, 128),
            vmem(ny, 3, 8, 8, 128), vmem(nx, 3, 8, 8, 128),
            vmem(nz, 4, 8, 128), vmem(nz, 3, 4, 8, 128), vmem(nz, 3, 8, 128),
            vmem(8, nl, 8, 128), vmem(7, nl, 8, 128), vmem(3, 8, 512),
            pltpu.VMEM((4, 2, 128, 128), BF16), pltpu.VMEM((4, 2, 128, 128), BF16),
            vmem(2, 16, 640), vmem(3, 3, 16, 256), vmem(2, 128, 640),
            vmem(2, 128, 1024), vmem(128, 1024), pltpu.VMEM((128, 1024), BF16),
            pltpu.VMEM((3, 1024, 512), BF16),
            dma((3, 3)), dma((3, 3)), dma, dma((2,)), dma, dma, dma, dma,
            dma((nx, 3)), dma((nx, 3)), dma((ny, 3)), dma((ny, 3)), dma((nz, 7)), dma((nz, 7)),
            dma((ny, 3)), dma((ny, 3)), dma((nx, 3)), dma((nx, 3)),
            dma((nz, 3)), dma((nz, 3)), dma((nz, 3)), dma((nz, 3)),
            dma((2, 7)), dma((2, 7)), dma((4, 2, 3)), dma((2, 4, 3)), dma((3,)),
        ],
        compiler_params=pltpu.CompilerParams(
            collective_id=2, has_side_effects=True, vmem_limit_bytes=VMEM_LIMIT
        ),
        name="back",
    )(qr, gr, kown, vown, ld, dq, xt, wg, attn)


def local(image_tokens, qkv_weight, block_list, block_count, out_grad):
    slots = block_list[0]
    live = jnp.arange(2, dtype=jnp.int32) < block_count[0, 0]
    on = jnp.any((slots[:, None] == jnp.arange(2, dtype=jnp.int32)[None]) & live[:, None], axis=0)
    on = on.astype(F32)
    act = jnp.broadcast_to(on[None, :, None, None], (8, 2, 8, 128)).reshape(128, 128)
    xr, gr, wg, acts = gather_all(
        image_tokens.reshape(8, 2, 8, 1024), out_grad.reshape(8, 2, 8, 1024), qkv_weight, act
    )
    wg = wg.reshape(3, 1024, 512)
    attn, dq, ld, qr, grs, kown, vown, xt = query_side(xr, gr, wg, acts)
    attn_out, grad_x, grad_w = back(qr, grs, kown, vown, ld, dq, xt, wg, attn)
    return attn_out.reshape(8, 16, 1024), grad_x.reshape(8, 16, 1024), grad_w


def solution(mesh):
    placed = (
        P("narrow", "wide", None),
        P("wide", None),
        P("narrow", "wide"),
        P("narrow", "wide"),
        P("narrow", "wide", None),
    )
    return jax.shard_map(
        local,
        mesh=mesh,
        in_specs=placed,
        out_specs=(P("narrow", "wide", None), P("narrow", "wide", None), P("wide", None)),
        check_vma=False,
    )
```

time: 186 us -> 152 us (0.82)
  Pallas kernels: 177 us -> 143 us
  local copies, waits for them, and re-layouts: 2.07 us -> 5.99 us
  other arithmetic: 4.43 us -> 0.76 us
    pallas_call x3 -> x1, Pallas kernels: 85 us -> 65.4 us  [back(): pl.pallas_call(back_kernel, out_shape=(shape((128, 1024), BF16), shape((1...]
    pallas_call x1, Pallas kernels: 70.4 us -> 55.8 us  [gather_all(): pl.pallas_call(gather_kernel, out_shape=(jax.ShapeDtypeStruct((2, 20, 6,...]
    unnamed x6 -> x3, local copies, waits for them, and re-layouts: 0.01 us -> 5.1 us
where the time goes in v2:
time: 152 us; the launch traced here: 151 us
  Pallas kernels  143 us (94%)
  local copies, waits for them, and re-layouts  5.99 us (4%)
    pallas_call x1, Pallas kernels, back(): pl.pallas_call(back_kernel, out_shape=(shape((128, 1024), BF16), shape((1...  65.4 us
    pallas_call x1, Pallas kernels, gather_all(): pl.pallas_call(gather_kernel, out_shape=(jax.ShapeDtypeStruct((2, 20, 6,...  55.8 us
    pallas_call x1, Pallas kernels, query_side(): pl.pallas_call(query_kernel, out_shape=(shape((2, 128, 512), BF16), shape...  22.1 us
    unnamed x3, local copies, waits for them, and re-layouts  5.1 us

profile of v2, /device:TPU:1, one launch (start us, length us, event | category | flops | bytes accessed | tf_op | source)
XLA Modules:
  0.0 151.3 jit_solution(7977596693274226509)
XLA Ops:
  1.3 0.7 and_reduce_fusion
  2.0 0.1 broadcast_in_dim.12
  2.1 0.1 broadcast_in_dim.13
  2.2 0.7 broadcast_in_dim.14.act_ref
  2.9 55.8 %gather_all.1 = (bf16[2,20,6,8,512]{4,3,2,1,0:T(8,128)(2,1)}, bf16[20,6,8,512]{3,2,1,0:T(8,128)(2,1)}, bf16[3,2,8,2,32,512]{5,4,3,2,1,0:T(8,128)(2,1)}, f32[2,128,128]{2,1,0:T(8,128)}) custom-call(bf16[8,2,8,1024]{3,2,1,0:T(8,128)(2,1)} %bitcast.10, bf16[8,2,8,1024]{3,2,1,0:T(8,128)(2,1)} %bitcast.11, bf16[32,3072]{1,0:T(8,128)(2,1)} %w_ref.1, ...), custom_call_target="tpu_custom_call" | custom-call | tf_op jit(solution)/shard_map/gather_all/pallas_call | solution.py:200
  58.8 22.1 %query_side.1 = (bf16[2,128,512]{2,1,0:T(8,128)(2,1)}, bf16[2,128,512]{2,1,0:T(8,128)(2,1)}, f32[16,256]{1,0:T(8,128)}, bf16[20,48,512]{2,1,0:T(8,128)(2,1)}, bf...) custom-call(bf16[2,20,6,8,512]{4,3,2,1,0:T(8,128)(2,1)} %get-tuple-e, ...), custom_call_target="tpu_custom_call" | custom-call | tf_op jit(solution)/shard_map/query_side/pallas_call | solution.py:344
  80.9 65.4 %back.1 = (bf16[128,1024]{1,0:T(8,128)(2,1)}, bf16[128,1024]{1,0:T(8,128)(2,1)}, f32[32,3072]{1,0:T(8,128)}) custom-call(bf16[20,48,512]{2,1,0:T(8,128)(2,1)} %get-tuple-element.22.qr_ref, bf16[20,48,512]{2,1,0:T(8,128)(2,1)} %get-tuple-element.23.gr_ref, bf16[2,128,512]{2,1,0:T(8,128)(2,1)} %get-tuple-element.24.kown_ref, ...), custom_call_target="tpu_custom_call" | custom-call | tf_op jit(solution)/shard_map/back/pallas_call | solution.py:729
  146.2 1.7 %copy.12 = bf16[8,16,1024]{2,1,0:T(8,128)(2,1)} copy(bf16[8,16,1024]{2,1,0:T(8,128)(2,1)} %bitcast.13) | data formatting | bytes 524288
  147.9 1.7 %copy.13 = bf16[8,16,1024]{2,1,0:T(8,128)(2,1)} copy(bf16[8,16,1024]{2,1,0:T(8,128)(2,1)} %bitcast.12) | data formatting | bytes 524288
  149.6 1.8 %copy.14 = f32[32,3072]{1,0:T(8,128)} copy(f32[32,3072]{1,0:T(8,128)} %get-tuple-element.38) | data formatting | bytes 786432
  (2 shorter events, 0.0 us)

commit v3 on v2

v3 whole, which is shorter than its diff:
```python
import functools
import math

import jax
import jax.numpy as jnp
from jax import lax
from jax.experimental import pallas as pl
from jax.experimental.pallas import tpu as pltpu
from jax.sharding import PartitionSpec as P

MESH = pl.DeviceIdType.MESH
F32 = jnp.float32
BF16 = jnp.bfloat16
RADIUS = 6
NEGATIVE = -1e30
HUGE = 1e30
SCALE = 0.125
VMEM_LIMIT = 60 * 1024 * 1024
ANY = pl.BlockSpec(memory_space=pl.ANY)
VM = pl.BlockSpec(memory_space=pltpu.VMEM)

ROWS = {-1: (0, 6, 14), 0: (0, 8, 6), 1: (2, 6, 0)}


def place():
    wide = lax.axis_index("wide")
    narrow = lax.axis_index("narrow")
    return narrow, wide // 2, wide % 2


def device(narrow, chip, core):
    return {"wide": lax.rem(chip, 16) * 2 + core, "narrow": lax.rem(narrow, 8)}


def remote(src, dst, send, recv, to):
    return pltpu.make_async_remote_copy(
        src_ref=src, dst_ref=dst, send_sem=send, recv_sem=recv, device_id=to, device_id_type=MESH
    )


def greet(devices):
    barrier = pltpu.get_barrier_semaphore()
    for to in devices:
        pl.semaphore_signal(barrier, inc=1, device_id=to, device_id_type=MESH)
    pl.semaphore_wait(barrier, len(devices))


def half_of(core):
    return pl.ds(pl.multiple_of(core * 512, 512), 512)


def gather_kernel(
    x_ref, g_ref, w_ref, act_ref, xr_ref, gr_ref, wg_ref, acts_ref, xall_ref,
    h_send, h_recv, h_local, s_send, s_recv, a_send, a_recv, a_local,
    w_send, w_recv, w_local, p_send, p_recv, r_send, r_recv, e_send, e_recv,
):
    n, chip, core = place()
    other = 1 - core
    z = lax.rem(chip, 8)
    xh = chip // 8
    step = 2 * core - 1
    side_chip = chip + step + 16
    up = device(n, xh * 8 + lax.rem(z + 1, 8), core)
    down = device(n, xh * 8 + lax.rem(z + 7, 8), core)
    partner = device(n + 1 - 2 * lax.rem(n, 2), (1 - xh) * 8 + z, core)
    sibling = device(n, chip, other)

    peers = [up, down, partner, sibling]
    for dn in (-1, 0, 1):
        for dc in (-1, 0, 1):
            for c in (0, 1):
                if (dn, dc) != (0, 0):
                    peers.append(device(n + dn + 8, chip + dc + 16, c))
    for d in (1, 2, 3):
        for c in (0, 1):
            peers.append(device(n + 2 * d, chip, c))
    greet(peers)

    sends = []
    own = []
    for t in range(3):
        here = wg_ref.at[t, xh, z, core]
        cp = pltpu.make_async_copy(
            w_ref.at[:, pl.ds(pl.multiple_of(t * 1024 + core * 512, 512), 512)], here, w_local.at[t]
        )
        cp.start()
        own.append(cp)
        cp = remote(
            w_ref.at[:, pl.ds(pl.multiple_of(t * 1024 + other * 512, 512), 512)],
            here, w_send.at[t], w_recv.at[t], sibling,
        )
        cp.start()
        sends.append(cp)

    for t in range(3):
        own[t].wait()
        remote(
            w_ref.at[:, pl.ds(0, 512)], wg_ref.at[t, xh, z, other],
            w_send.at[t], w_recv.at[t], sibling,
        ).wait_recv()
    hops = {(0, 0): 4, (0, 1): 3, (1, 0): 3, (1, 1): 4}

    def slab(t, s, index):
        return wg_ref.at[t, xh if s == 0 else 1 - xh, lax.rem(index + 16, 8)]

    def forward(s, d, k, t):
        moved = slab(t, s, z - k if d == 0 else z + k)
        cp = remote(
            moved, moved, r_send.at[s, d, k, t], r_recv.at[s, d, k, t], up if d == 0 else down
        )
        cp.start()
        sends.append(cp)

    def arrived(s, d, k, t):
        landed = slab(t, s, z - 1 - k if d == 0 else z + 1 + k)
        remote(landed, landed, r_send.at[s, d, k, t], r_recv.at[s, d, k, t], up).wait_recv()

    for t in range(3):
        mine = slab(t, 0, z)
        cp = remote(mine, mine, p_send.at[t], p_recv.at[t], partner)
        cp.start()
        sends.append(cp)
        forward(0, 0, 0, t)
        forward(0, 1, 0, t)
    tensors = ((g_ref, lambda c: gr_ref), (x_ref, lambda c: xr_ref.at[c]))
    locals_ = []
    for i, (src, dst) in enumerate(tensors):
        for dn in (-1, 0, 1):
            lo, count, at = ROWS[dn]
            for side in (0, 1):
                for rel in (0, 1):
                    c = core if rel == 0 else other
                    if side == 0:
                        source = src.at[pl.ds(lo, count), :, :, half_of(c)]
                        target = dst(c).at[pl.ds(at, count), pl.ds(1 + 2 * core, 2)]
                        slot = core
                        to = device(n + dn + 8, chip, c)
                    else:
                        source = src.at[pl.ds(lo, count), pl.ds(core, 1), :, half_of(c)]
                        target = dst(c).at[pl.ds(at, count), pl.ds(5 * other, 1)]
                        slot = 3 - core
                        to = device(n + dn + 8, side_chip, c)
                    if dn == 0 and side == 0 and rel == 0:
                        cp = pltpu.make_async_copy(source, target, h_local.at[i])
                        locals_.append(cp)
                    else:
                        cp = remote(
                            source, target, h_send.at[i, dn + 1, side, rel],
                            h_recv.at[i, dn + 1, slot], to,
                        )
                        sends.append(cp)
                    cp.start()

    act_copy = pltpu.make_async_copy(act_ref, acts_ref.at[core], a_local)
    act_copy.start()
    act_send = remote(act_ref, acts_ref.at[core], a_send, a_recv, sibling)
    act_send.start()
    sends.append(act_send)

    for t in range(3):
        theirs = slab(t, 1, z)
        remote(theirs, theirs, p_send.at[t], p_recv.at[t], partner).wait_recv()
        forward(1, 0, 0, t)
        forward(1, 1, 0, t)

    for d in (2, 1, 3):
        want = lax.rem(n // 2 + d, 4) // 2
        for rel in (0, 1):
            cp = remote(
                x_ref.at[:, :, :, half_of(want)], xall_ref.at[3 - d, core],
                e_send.at[d - 1, rel], e_recv.at[3 - d, core],
                device(n + 2 * d, chip, core if rel == 0 else other),
            )
            cp.start()
            sends.append(cp)

    def finish_region(i, dst):
        locals_[i].wait()
        for dn in (-1, 0, 1):
            lo, count, at = ROWS[dn]
            for piece in range(4):
                if piece < 2:
                    if dn == 0 and piece == 1:
                        continue
                    slot = other if dn == 0 else piece
                    landed = dst.at[pl.ds(at, count), pl.ds(1 + 2 * slot, 2)]
                else:
                    slot = piece
                    landed = dst.at[pl.ds(at, count), pl.ds(0 if piece == 2 else 5, 1)]
                remote(
                    landed, landed, h_send.at[i, dn + 1, 0, 0], h_recv.at[i, dn + 1, slot], sibling
                ).wait_recv()

    for k in range(1, 5):
        for s in range(2):
            for t in range(3):
                for d in range(2):
                    if k <= hops[s, d]:
                        arrived(s, d, k - 1, t)
                    if k < hops[s, d]:
                        forward(s, d, k, t)
        if k == 2:
            finish_region(1, xr_ref.at[core])
            cp = remote(xr_ref.at[core], xr_ref.at[core], s_send, s_recv, sibling)
            cp.start()
            sends.append(cp)
    finish_region(0, gr_ref)
    act_copy.wait()
    remote(act_ref, acts_ref.at[other], a_send, a_recv, sibling).wait_recv()
    remote(xr_ref.at[other], xr_ref.at[other], s_send, s_recv, sibling).wait_recv()
    for r in range(3):
        for c in range(2):
            landed = xall_ref.at[r, c]
            remote(landed, landed, e_send.at[r, c], e_recv.at[r, c], sibling).wait_recv()
    for cp in sends:
        cp.wait_send()


def gather_all(x4, g4, weight, act):
    dma = pltpu.SemaphoreType.DMA
    return pl.pallas_call(
        gather_kernel,
        out_shape=(
            jax.ShapeDtypeStruct((2, 20, 6, 8, 512), BF16),
            jax.ShapeDtypeStruct((20, 6, 8, 512), BF16),
            jax.ShapeDtypeStruct((3, 2, 8, 2, 32, 512), BF16),
            jax.ShapeDtypeStruct((2, 128, 128), F32),
            jax.ShapeDtypeStruct((3, 2, 8, 2, 8, 512), BF16),
        ),
        in_specs=[VM] * 4,
        out_specs=(ANY,) * 5,
        scratch_shapes=[
            dma((2, 3, 2, 2)), dma((2, 3, 4)), dma((2,)), dma, dma, dma, dma, dma,
            dma((3,)), dma((3,)), dma((3,)), dma((3,)), dma((3,)),
            dma((2, 2, 4, 3)), dma((2, 2, 4, 3)), dma((3, 2)), dma((3, 2)),
        ],
        compiler_params=pltpu.CompilerParams(collective_id=0, has_side_effects=True),
        name="gather_all",
    )(x4, g4, weight, act)


def window_bias(hf):
    n, chip, _ = place()
    shape = (128, 640)
    inner = lax.broadcasted_iota(jnp.int32, shape, 0)
    outer = lax.broadcasted_iota(jnp.int32, shape, 1)
    row, col = outer // 32, outer % 32
    down = row - RADIUS - inner // 16
    across = col - 8 - inner % 16
    grid_row = n * 8 - RADIUS + row
    grid_col = chip * 32 - 8 + 16 * hf + col
    ok = (jnp.abs(down) <= RADIUS) & (jnp.abs(across) <= RADIUS)
    ok = ok & (grid_row >= 0) & (grid_row < 64) & (grid_col >= 0) & (grid_col < 512)
    return jnp.where(ok, 0.0, NEGATIVE)


def nt(a, b):
    return lax.dot_general(a, b, (((1,), (1,)), ((), ())), preferred_element_type=F32)


def nn(a, b):
    return jnp.dot(a, b, preferred_element_type=F32)


def tn(a, b):
    return lax.dot_general(a, b, (((0,), (0,)), ((), ())), preferred_element_type=F32)


def lanes_of(hp):
    return pl.ds(pl.multiple_of(hp * 128, 128), 128)


def head_masks():
    lane = lax.broadcasted_iota(jnp.int32, (128, 128), 1)
    low = lane < 64
    return low, (low.astype(F32).astype(BF16), (1.0 - low.astype(F32)).astype(BF16)), lane


def query_kernel(
    xr_ref, gr_ref, wg_ref, acts_ref, xall_ref,
    attn_ref, dq_ref, ld_ref, qr_ref, grs_ref, kown_ref, vown_ref, xt_ref,
    acc, kr, vr, qown, gown, ldacc, ldall, bias,
):
    row_half = lax.axis_index("narrow") // 4

    for t, region in enumerate((qr_ref, kr, vr)):

        def chunk(i, carry, t=t, region=region):
            out = nn(xr_ref[0, pl.ds(4 * i, 4)].reshape(192, 512), wg_ref[t, :512])
            out += nn(xr_ref[1, pl.ds(4 * i, 4)].reshape(192, 512), wg_ref[t, 512:])
            acc[pl.ds(4 * i, 4)] = out.reshape(4, 6, 8, 512)
            region[pl.ds(4 * i, 4)] = out.astype(BF16).reshape(4, 48, 512)
            return carry

        lax.fori_loop(0, 5, chunk, 0)
        for hf in range(2):
            own = acc[6:14, 1 + 2 * hf : 3 + 2 * hf].reshape(128, 512).astype(BF16)
            if t == 0:
                qown[hf] = own * SCALE
            elif t == 1:
                kown_ref[hf] = own * SCALE
            else:
                vown_ref[hf] = own

    def regroup(i, carry):
        rows = gr_ref[pl.ds(4 * i, 4)].astype(F32).reshape(192, 512)
        grs_ref[pl.ds(4 * i, 4)] = rows.astype(BF16).reshape(4, 48, 512)
        return carry

    lax.fori_loop(0, 5, regroup, 0)
    for hf in range(2):
        groups = pl.ds(1 + 2 * hf, 2)
        gown[hf] = gr_ref[6:14, groups].astype(F32).reshape(128, 512).astype(BF16)
        for r in range(4):
            if r == 0:
                tokens = xr_ref[row_half, 6:14, groups]
            else:
                tokens = xall_ref[r - 1, hf]
            tokens = tokens.astype(F32).reshape(128, 512)
            at = 256 * r + 128 * hf
            for i in range(4):
                xt_ref[128 * i : 128 * i + 128, at : at + 128] = (
                    tokens[:, 128 * i : 128 * i + 128].T.astype(BF16)
                )
        bias[...] = window_bias(hf)
        ldacc[...] = jnp.zeros_like(ldacc)

        def pair(hp, carry, hf=hf):
            lanes = lanes_of(hp)
            low, masks, lane = head_masks()
            keys = kr[:, 16 * hf : 16 * hf + 32, lanes].reshape(640, 128)
            values = vr[:, 16 * hf : 16 * hf + 32, lanes].reshape(640, 128)
            query = qown[hf, :, lanes]
            grad = gown[hf, :, lanes]
            active = acts_ref[hf]
            outs, dqs = [], []
            ld = ldacc[...]
            for j in range(2):
                s = nt(query * masks[j], keys) + bias[...]
                top = jnp.max(s, axis=1, keepdims=True)
                e = jnp.exp(s - top)
                total = jnp.sum(e, axis=1, keepdims=True)
                p = e * (1.0 / total)
                lse = top + jnp.log(total)
                out = nn(p.astype(BF16), values)
                out = out.astype(BF16).astype(F32)
                gm = grad * masks[j]
                delta = jnp.sum(gm.astype(F32) * out, axis=1, keepdims=True)
                dp = nt(gm, values)
                ds = (p * (dp - delta) * SCALE).astype(BF16)
                dqs.append(nn(ds, keys))
                outs.append(out)
                on = active > 0.0
                head = 2 * hp + j
                ld = jnp.where(lane == head, jnp.where(on, lse, HUGE), ld)
                ld = jnp.where(lane == head + 8, jnp.where(on, delta, 0.0), ld)
            ldacc[...] = ld
            attn_ref[hf, :, lanes] = (jnp.where(low, outs[0], outs[1]) * active).astype(BF16)
            dq_ref[hp, hf] = (jnp.where(low, dqs[0], dqs[1]) * active).astype(BF16)
            return carry

        lax.fori_loop(0, 4, pair, 0)
        ldall[:, 16 * hf : 16 * hf + 16, :] = ldacc[...].reshape(8, 16, 128)
    for i in range(2):
        ld_ref[:, 128 * i : 128 * i + 128] = ldall[4 * i : 4 * i + 4].reshape(128, 128).T[:16]


def query_side(xr, gr, wg, acts, xall):
    shape = jax.ShapeDtypeStruct
    return pl.pallas_call(
        query_kernel,
        out_shape=(
            shape((2, 128, 512), BF16), shape((4, 2, 128, 128), BF16), shape((16, 256), F32),
            shape((20, 48, 512), BF16), shape((20, 48, 512), BF16),
            shape((2, 128, 512), BF16), shape((2, 128, 512), BF16), shape((512, 1024), BF16),
        ),
        in_specs=[VM] * 5,
        out_specs=(VM,) * 8,
        scratch_shapes=[
            pltpu.VMEM((20, 6, 8, 512), F32), pltpu.VMEM((20, 48, 512), BF16),
            pltpu.VMEM((20, 48, 512), BF16), pltpu.VMEM((2, 128, 512), BF16),
            pltpu.VMEM((2, 128, 512), BF16), pltpu.VMEM((128, 128), F32),
            pltpu.VMEM((8, 32, 128), F32), pltpu.VMEM((128, 640), F32),
        ],
        compiler_params=pltpu.CompilerParams(vmem_limit_bytes=VMEM_LIMIT),
        name="query_side",
    )(xr, gr, wg, acts, xall)


XPEERS = ((0, 1), (1, 0), (1, 1))
NEAR = tuple((dn, dc) for dn in (-1, 0, 1) for dc in (-1, 0, 1) if (dn, dc) != (0, 0))


def back_kernel(
    qr_ref, gr_ref, kown_ref, vown_ref, ld_ref, dq_ref, xt_ref, wg_ref, attn_ref,
    attn_out, gx_out, gw_out,
    gall, p, rx, cz, rc, fin_q, fin_kv, kv, lds, ldb, bias, gx, gxr, gxo, wv,
    ld_send, ld_recv, w_sem, o_sem, a_send, a_recv, g_send, g_recv,
    q_send, q_recv, k_send, k_recv, x_send, x_recv, c_send, c_recv, f_send, f_recv, f_local,
):
    n, chip, core = place()
    other = 1 - core
    z = lax.rem(chip, 8)
    xh = chip // 8
    y = n // 2
    xl = lax.rem(n, 2)
    row_half = y // 2
    col_half = lax.rem(y, 2)

    def at(xh_, z_, core_, y_, xl_):
        return device(y_ * 2 + xl_, xh_ * 8 + z_, core_)

    def ypeer(d):
        return lax.rem(y + d, 4)

    def zpeer(d):
        return lax.rem(z + d + 8, 8)

    def flip(value, by):
        return 1 - value if by else value

    sibling = at(xh, z, other, y, xl)
    peers = [device(n + dn + 8, chip + dc + 16, core) for dn, dc in NEAR]
    peers += [at(xh, zpeer(d), core, y, xl) for d in range(1, 8)]
    for a in (0, 1):
        for c in (0, 1):
            for d in range(4):
                for b in (0, 1):
                    if (a, c, d, b) != (0, 0, 0, 0):
                        peers.append(at(flip(xh, a), z, flip(core, c), ypeer(d), flip(xl, b)))
    greet(peers)

    sends = []

    def go(src, dst, send, recv, to):
        cp = remote(src, dst, send, recv, to)
        cp.start()
        sends.append(cp)

    def came(dst, send, recv):
        remote(dst, dst, send, recv, sibling).wait_recv()

    for dn, dc in NEAR:
        go(
            ld_ref, ldb.at[1 - dn, 1 - dc], ld_send.at[dn + 1, dc + 1], ld_recv.at[1 - dn, 1 - dc],
            device(n + dn + 8, chip + dc + 16, core),
        )
    for d in (2, 1, 3):
        go(
            dq_ref.at[pl.ds(2 * lax.rem(ypeer(d), 2), 2)], gall.at[4 - d, pl.ds(0, 2)],
            q_send.at[d - 1], q_recv.at[3 - d], at(xh, z, core, ypeer(d), xl),
        )
    weights = pltpu.make_async_copy(wg_ref, wv, w_sem)
    weights.start()
    go(attn_ref.at[other], attn_out.at[:, half_of(core)], a_send, a_recv, sibling)
    attn_own = pltpu.make_async_copy(attn_ref.at[core], attn_out.at[:, half_of(core)], o_sem.at[0])
    attn_own.start()

    def share(hp):
        for d in (2, 1, 3):
            go(
                kv.at[hp, lax.rem(ypeer(d), 2)], gall.at[4 - d, 2 + hp],
                k_send.at[hp, d - 1], k_recv.at[hp, 3 - d], at(xh, z, core, ypeer(d), xl),
            )

    def product(first, count):
        if count == 2:
            columns = jnp.concatenate(
                [gall[:, first + j].reshape(1024, 128) for j in range(count)], axis=1
            )
        else:
            columns = gall[:, first].reshape(1024, 128)

        def rows(i, carry):
            out = nn(xt_ref[pl.ds(pl.multiple_of(i * 128, 128), 128), :], columns)
            out = out.reshape(2, 2, 2, 2, 8, 128 * count)
            for j in range(count):
                p[first + j, pl.ds(2 * i, 2)] = out[..., 128 * j : 128 * j + 128]
            return carry

        lax.fori_loop(0, 4, rows, 0)
        for b in range(first, first + count):
            for i in (2, 0, 1):
                a, l = flip(xh, XPEERS[i][0]), flip(xl, XPEERS[i][1])
                go(
                    p.at[b, :, l, a], rx.at[b, i], x_send.at[b, i], x_recv.at[b, i],
                    at(a, z, core, y, l),
                )

    def product_q():
        for r in range(3):
            came(gall.at[r + 1, pl.ds(0, 2)], q_send.at[r], q_recv.at[r])
        for j in range(2):
            gall[0, j] = dq_ref[2 * col_half + j]
        product(0, 2)

    def product_kv(hp):
        for r in range(3):
            came(gall.at[r + 1, 2 + hp], k_send.at[hp, r], k_recv.at[hp, r])
        gall[0, 2 + hp] = kv[hp, col_half]
        product(2 + hp, 1)

    def sum_x(b):
        for i in range(3):
            came(rx.at[b, i], x_send.at[b, i], x_recv.at[b, i])
        for j in range(8):
            cz[j, b] = p[b, j, xl, xh] + rx[b, 0, j] + rx[b, 1, j] + rx[b, 2, j]

    batches = ((0, 4), (4, 2))

    def spread(h):
        lo, count = batches[h]
        for d in (4, 3, 5, 2, 6, 1, 7):
            go(
                cz.at[zpeer(d), pl.ds(lo, count)], rc.at[d - 1, pl.ds(lo, count)],
                c_send.at[h, d - 1], c_recv.at[h, d - 1], at(xh, zpeer(d), core, y, xl),
            )

    factor = 1.0 / math.sqrt(32768.0)

    def sum_z(h):
        lo, count = batches[h]
        for d in range(7):
            came(rc.at[d, pl.ds(lo, count)], c_send.at[h, d], c_recv.at[h, d])
        for b in range(lo, lo + count):
            total = cz[z, b]
            for d in range(7):
                total = total + rc[d, b]
            total = total.reshape(16, 128) * factor
            if b < 2:
                fin_q[:, 128 * b : 128 * b + 128] = total
            else:
                fin_kv[:, 128 * (b - 2) : 128 * (b - 1)] = total

    for hf in range(2):
        bias[hf] = window_bias(hf)
    ldb[1, 1] = ld_ref[...]
    for dn, dc in NEAR:
        came(ldb.at[1 - dn, 1 - dc], ld_send.at[dn + 1, dc + 1], ld_recv.at[1 - dn, 1 - dc])
    column = lax.rem(lax.broadcasted_iota(jnp.int32, (16, 256), 1), 32)
    for hf in range(2):
        parts = []
        for r in range(3):
            left, mid, right = ldb[r, 0], ldb[r, 1], ldb[r, 2]
            if hf == 0:
                part = jnp.where(column < 8, pltpu.roll(left, 232, 1), pltpu.roll(mid, 8, 1))
            else:
                part = jnp.where(column < 24, pltpu.roll(mid, 248, 1), pltpu.roll(right, 24, 1))
            parts.append(part)
        lds[hf] = pltpu.roll(jnp.concatenate(parts, axis=1), 768 - 64, 1)[:, :640]

    low, masks, _ = head_masks()

    def key_side(hp):
        lanes = slice(128 * hp, 128 * hp + 128)

        def side(hf, carry):
            window = pl.ds(pl.multiple_of(16 * hf, 16), 32)
            query = qr_ref[:, window, lanes].reshape(640, 128)
            grad = gr_ref[:, window, lanes].reshape(640, 128)
            keys = kown_ref[hf, :, lanes]
            values = vown_ref[hf, :, lanes]
            dks, dvs = [], []
            for j in range(2):
                head = 2 * hp + j
                s = nt(keys * masks[j], query) + bias[hf]
                e = jnp.exp(s - lds[hf, head : head + 1, :])
                dvs.append(nn(e.astype(BF16), grad))
                dp = nt(values * masks[j], grad)
                ds = (e * (dp - lds[hf, head + 8 : head + 9, :]) * SCALE).astype(BF16)
                dks.append(nn(ds, query))
            kv[hp, 0, hf] = jnp.where(low, dks[0], dks[1]).astype(BF16)
            kv[hp, 1, hf] = jnp.where(low, dvs[0], dvs[1]).astype(BF16)
            return carry

        lax.fori_loop(0, 2, side, 0)
        share(hp)

    key_side(0)
    product_q()
    key_side(1)
    product_kv(0)
    key_side(2)
    product_kv(1)
    sum_x(0)
    sum_x(1)
    key_side(3)
    product_kv(2)
    sum_x(2)
    sum_x(3)
    spread(0)

    weights.wait()
    all_q = jnp.concatenate([dq_ref[h].reshape(256, 128) for h in range(4)], axis=1)
    all_k = jnp.concatenate([kv[h, 0].reshape(256, 128) for h in range(4)], axis=1)
    all_v = jnp.concatenate([kv[h, 1].reshape(256, 128) for h in range(4)], axis=1)

    def input_columns(i, carry):
        rows = pl.ds(pl.multiple_of(i * 256, 256), 256)
        total = nt(all_q, wv[0, rows]) + nt(all_k, wv[1, rows]) + nt(all_v, wv[2, rows])
        gx[:, :, rows] = total.reshape(2, 128, 256)
        return carry

    product_kv(3)
    lax.fori_loop(0, 4, input_columns, 0)
    go(gx.at[other], gxr, g_send, g_recv, sibling)
    sum_x(4)
    sum_x(5)
    spread(1)
    came(gxr, g_send, g_recv)
    gxo[...] = (gx[core] + gxr[...]).astype(BF16)
    gx_own = pltpu.make_async_copy(gxo, gx_out, o_sem.at[1])
    gx_own.start()
    sum_z(0)
    sum_z(1)

    def spots(c, part, a):
        rows = pl.ds(pl.multiple_of(16 * a, 16), 16)
        q_at = pl.multiple_of(c * 512 + part * 256, 256)
        kv_at = pl.multiple_of((1 + part) * 1024 + c * 512, 512)
        return gw_out.at[rows, pl.ds(q_at, 256)], gw_out.at[rows, pl.ds(kv_at, 512)]

    mine = spots(core, col_half, xh)
    for i, fin in enumerate((fin_q, fin_kv)):
        recv = f_recv.at[i, core, col_half, xh]
        for d in (2, 1, 3):
            for b in (0, 1):
                go(fin, mine[i], f_send.at[i, d, b], recv, at(row_half, z, xl, ypeer(d), flip(xl, b)))
        go(fin, mine[i], f_send.at[i, 0, 1], recv, at(row_half, z, xl, y, 1 - xl))
        away = remote(fin, mine[i], f_send.at[i, 0, 0], recv, at(row_half, z, xl, y, xl))
        here = pltpu.make_async_copy(fin, mine[i], f_local.at[i])
        is_here = (core == xl) & (row_half == xh)

        @pl.when(is_here)
        def _():
            here.start()
            here.wait()

        @pl.when(jnp.logical_not(is_here))
        def _():
            away.start()
            away.wait_send()

    attn_own.wait()
    gx_own.wait()
    came(attn_out.at[:, half_of(other)], a_send, a_recv)
    for c in range(2):
        for part in range(2):
            for a in range(2):
                landed = spots(c, part, a)
                own = (
                    (c == core) & (part == col_half) & (a == xh) & (row_half == xh) & (xl == core)
                )
                for i in range(2):

                    @pl.when(jnp.logical_not(own))
                    def _():
                        came(landed[i], f_send.at[i, 0, 0], f_recv.at[i, c, part, a])

    for cp in sends:
        cp.wait_send()


def back(qr, gr, kown, vown, ld, dq, xt, wg, attn):
    dma = pltpu.SemaphoreType.DMA
    vmem = lambda *shape: pltpu.VMEM(shape, F32)
    half = lambda *shape: pltpu.VMEM(shape, BF16)
    shape = jax.ShapeDtypeStruct
    return pl.pallas_call(
        back_kernel,
        out_shape=(
            shape((128, 1024), BF16), shape((128, 1024), BF16), shape((32, 3072), F32),
        ),
        in_specs=[VM] * 7 + [ANY, VM],
        out_specs=(ANY,) * 3,
        scratch_shapes=[
            half(4, 6, 2, 128, 128), vmem(6, 8, 2, 2, 2, 8, 128), vmem(6, 3, 8, 2, 8, 128),
            vmem(8, 6, 2, 8, 128), vmem(7, 6, 2, 8, 128), vmem(16, 256), vmem(16, 512),
            half(4, 2, 2, 128, 128), vmem(2, 16, 640), vmem(3, 3, 16, 256), vmem(2, 128, 640),
            vmem(2, 128, 1024), vmem(128, 1024), half(128, 1024), half(3, 1024, 512),
            dma((3, 3)), dma((3, 3)), dma, dma((2,)), dma, dma, dma, dma,
            dma((3,)), dma((3,)), dma((4, 3)), dma((4, 3)), dma((6, 3)), dma((6, 3)),
            dma((2, 7)), dma((2, 7)), dma((2, 4, 2)), dma((2, 2, 2, 2)), dma((2,)),
        ],
        compiler_params=pltpu.CompilerParams(
            collective_id=2, has_side_effects=True, vmem_limit_bytes=VMEM_LIMIT
        ),
        name="back",
    )(qr, gr, kown, vown, ld, dq, xt, wg, attn)


def local(image_tokens, qkv_weight, block_list, block_count, out_grad):
    slots = block_list[0]
    live = jnp.arange(2, dtype=jnp.int32) < block_count[0, 0]
    on = jnp.any((slots[:, None] == jnp.arange(2, dtype=jnp.int32)[None]) & live[:, None], axis=0)
    on = on.astype(F32)
    act = jnp.broadcast_to(on[None, :, None, None], (8, 2, 8, 128)).reshape(128, 128)
    xr, gr, wg, acts, xall = gather_all(
        image_tokens.reshape(8, 2, 8, 1024), out_grad.reshape(8, 2, 8, 1024), qkv_weight, act
    )
    wg = wg.reshape(3, 1024, 512)
    attn, dq, ld, qr, grs, kown, vown, xt = query_side(xr, gr, wg, acts, xall)
    attn_out, grad_x, grad_w = back(qr, grs, kown, vown, ld, dq, xt, wg, attn)
    return attn_out.reshape(8, 16, 1024), grad_x.reshape(8, 16, 1024), grad_w


def solution(mesh):
    placed = (
        P("narrow", "wide", None),
        P("wide", None),
        P("narrow", "wide"),
        P("narrow", "wide"),
        P("narrow", "wide", None),
    )
    return jax.shard_map(
        local,
        mesh=mesh,
        in_specs=placed,
        out_specs=(P("narrow", "wide", None), P("narrow", "wide", None), P("wide", None)),
        check_vma=False,
    )
```

time: 152 us -> 136 us (0.89)
  Pallas kernels: 143 us -> 128 us
    pallas_call x1, Pallas kernels: 65.4 us -> 49.7 us  [back(): pl.pallas_call(back_kernel, out_shape=(shape((128, 1024), BF16), shape((1...]
where the time goes in v3:
time: 136 us
  Pallas kernels  128 us (94%)
  local copies, waits for them, and re-layouts  5.99 us (4%)
    pallas_call x1, Pallas kernels, gather_all(): pl.pallas_call(gather_kernel, out_shape=(jax.ShapeDtypeStruct((2, 20, 6,...  55.2 us
    pallas_call x1, Pallas kernels, back(): pl.pallas_call(back_kernel, out_shape=(shape((128, 1024), BF16), shape((1...  49.7 us
    pallas_call x1, Pallas kernels, query_side(): pl.pallas_call(query_kernel, out_shape=(shape((2, 128, 512), BF16), shape...  22.6 us
    unnamed x3, local copies, waits for them, and re-layouts  5.1 us

profile of v3, /device:TPU:1, one launch (start us, length us, event | category | flops | bytes accessed | tf_op | source)
XLA Modules:
  0.0 135.6 jit_solution(12123974860639161363)
XLA Ops:
  1.3 0.7 and_reduce_fusion
  2.0 0.1 broadcast_in_dim.12
  2.1 0.1 broadcast_in_dim.13
  2.2 0.7 broadcast_in_dim.14.act_ref
  2.9 55.2 %gather_all.1 = (bf16[2,20,6,8,512]{4,3,2,1,0:T(8,128)(2,1)}, bf16[20,6,8,512]{3,2,1,0:T(8,128)(2,1)}, bf16[3,2,8,2,32,512]{5,4,3,2,1,0:T(8,128)(2,1)}, f32[2,12...) custom-call(bf16[8,2,8,1024]{3,2,1,0:T(8,128)(2,1)} %bitcast.10, bf16[8,2,8,1024]{3,2,1,0:T(8,128)(2,1)} %bitcast.11, ...), custom_call_target="tpu_custom_call" | custom-call | tf_op jit(solution)/shard_map/gather_all/pallas_call | solution.py:221
  58.2 22.6 %query_side.1 = (bf16[2,128,512]{2,1,0:T(8,128)(2,1)}, bf16[4,2,128,128]{3,2,1,0:T(8,128)(2,1)}, f32[16,256]{1,0:T(8,128)}, bf16[20,48,512]{2,1,0:T(8,128)(2,1)}...) custom-call(bf16[2,20,6,8,512]{4,3,2,1,0:T(8,128)(2,1)} %get-tuple-e, ...), custom_call_target="tpu_custom_call" | custom-call | tf_op jit(solution)/shard_map/query_side/pallas_call | solution.py:370
  80.7 49.7 %back.1 = (bf16[128,1024]{1,0:T(8,128)(2,1)}, bf16[128,1024]{1,0:T(8,128)(2,1)}, f32[32,3072]{1,0:T(8,128)}) custom-call(bf16[20,48,512]{2,1,0:T(8,128)(2,1)} %get-tuple-element.24.qr_ref, bf16[20,48,512]{2,1,0:T(8,128)(2,1)} %get-tuple-element.25.gr_ref, bf16[2,128,512]{2,1,0:T(8,128)(2,1)} %get-tuple-element.26.kown_ref, ...), custom_call_target="tpu_custom_call" | custom-call | tf_op jit(solution)/shard_map/back/pallas_call | solution.py:669
  130.5 1.7 %copy.12 = bf16[8,16,1024]{2,1,0:T(8,128)(2,1)} copy(bf16[8,16,1024]{2,1,0:T(8,128)(2,1)} %bitcast.13) | data formatting | bytes 524288
  132.2 1.7 %copy.13 = bf16[8,16,1024]{2,1,0:T(8,128)(2,1)} copy(bf16[8,16,1024]{2,1,0:T(8,128)(2,1)} %bitcast.12) | data formatting | bytes 524288
  133.8 1.8 %copy.14 = f32[32,3072]{1,0:T(8,128)} copy(f32[32,3072]{1,0:T(8,128)} %get-tuple-element.40) | data formatting | bytes 786432
  (2 shorter events, 0.0 us)

commit v4 on v3

v4 whole, which is shorter than its diff:
```python
import functools
import math

import jax
import jax.numpy as jnp
from jax import lax
from jax.experimental import pallas as pl
from jax.experimental.pallas import tpu as pltpu
from jax.sharding import PartitionSpec as P

MESH = pl.DeviceIdType.MESH
F32 = jnp.float32
BF16 = jnp.bfloat16
RADIUS = 6
NEGATIVE = -1e30
HUGE = 1e30
SCALE = 0.125
VMEM_LIMIT = 60 * 1024 * 1024
ANY = pl.BlockSpec(memory_space=pl.ANY)
VM = pl.BlockSpec(memory_space=pltpu.VMEM)

ROWS = {-1: (0, 6, 14), 0: (0, 8, 6), 1: (2, 6, 0)}


def place():
    wide = lax.axis_index("wide")
    narrow = lax.axis_index("narrow")
    return narrow, wide // 2, wide % 2


def device(narrow, chip, core):
    return {"wide": lax.rem(chip, 16) * 2 + core, "narrow": lax.rem(narrow, 8)}


def remote(src, dst, send, recv, to):
    return pltpu.make_async_remote_copy(
        src_ref=src, dst_ref=dst, send_sem=send, recv_sem=recv, device_id=to, device_id_type=MESH
    )


def greet(devices):
    barrier = pltpu.get_barrier_semaphore()
    for to in devices:
        pl.semaphore_signal(barrier, inc=1, device_id=to, device_id_type=MESH)
    pl.semaphore_wait(barrier, len(devices))


def half_of(core):
    return pl.ds(pl.multiple_of(core * 512, 512), 512)


def window_bias(hf):
    n, chip, _ = place()
    shape = (128, 640)
    inner = lax.broadcasted_iota(jnp.int32, shape, 0)
    outer = lax.broadcasted_iota(jnp.int32, shape, 1)
    row, col = outer // 32, outer % 32
    down = row - RADIUS - inner // 16
    across = col - 8 - inner % 16
    grid_row = n * 8 - RADIUS + row
    grid_col = chip * 32 - 8 + 16 * hf + col
    ok = (jnp.abs(down) <= RADIUS) & (jnp.abs(across) <= RADIUS)
    ok = ok & (grid_row >= 0) & (grid_row < 64) & (grid_col >= 0) & (grid_col < 512)
    return jnp.where(ok, 0.0, NEGATIVE)


def nt(a, b):
    return lax.dot_general(a, b, (((1,), (1,)), ((), ())), preferred_element_type=F32)


def nn(a, b):
    return jnp.dot(a, b, preferred_element_type=F32)


def tn(a, b):
    return lax.dot_general(a, b, (((0,), (0,)), ((), ())), preferred_element_type=F32)


def lanes_of(hp):
    return pl.ds(pl.multiple_of(hp * 128, 128), 128)


def head_masks():
    lane = lax.broadcasted_iota(jnp.int32, (128, 128), 1)
    low = lane < 64
    return low, (low.astype(F32).astype(BF16), (1.0 - low.astype(F32)).astype(BF16)), lane


XPEERS = ((0, 1), (1, 0), (1, 1))
NEAR = tuple((dn, dc) for dn in (-1, 0, 1) for dc in (-1, 0, 1) if (dn, dc) != (0, 0))


def layer_kernel(
    x_ref, g_ref, w_ref, list_ref, count_ref,
    attn_out, gx_out, gw_out,
    xr_ref, gr_ref, wg_ref, xall_ref, acts,
    acc, qr_ref, kr, vr, grs_ref, qown, kown_ref, vown_ref, gown, ldacc, ldall, ld_ref,
    dq_ref, attn_ref, xt_ref,
    gall, p, rx, cz, rc, fin_q, fin_kv, kv, lds, ldb, bias, gx, gxr, gxo,
    h_send, h_recv, h_local, s_send, s_recv, act_send, act_recv,
    w_send, w_recv, w_local, p_send, p_recv, r_send, r_recv, e_send, e_recv,
    ld_send, ld_recv, o_sem, a_send, a_recv, g_send, g_recv,
    q_send, q_recv, k_send, k_recv, x_send, x_recv, c_send, c_recv, f_send, f_recv, f_local,
):
    n, chip, core = place()
    other = 1 - core
    z = lax.rem(chip, 8)
    xh = chip // 8
    y = n // 2
    xl = lax.rem(n, 2)
    row_half = y // 2
    col_half = lax.rem(y, 2)

    def at(xh_, z_, core_, y_, xl_):
        return device(y_ * 2 + xl_, xh_ * 8 + z_, core_)

    def ypeer(d):
        return lax.rem(y + d, 4)

    def zpeer(d):
        return lax.rem(z + d + 8, 8)

    def flip(value, by):
        return 1 - value if by else value

    for block in range(2):
        on = jnp.float32(0.0)
        for i in range(2):
            hit = (count_ref[0, 0] > i) & (list_ref[0, i] == block)
            on = jnp.maximum(on, jnp.where(hit, 1.0, 0.0))
        acts[core, block : block + 1, :] = jnp.full((1, 128), on, F32)

    sibling = at(xh, z, other, y, xl)
    up = at(xh, zpeer(1), core, y, xl)
    down = at(xh, zpeer(-1), core, y, xl)
    partner = at(1 - xh, z, core, y, 1 - xl)
    peers = [device(n + dn + 8, chip + dc + 16, c) for dn, dc in NEAR for c in (0, 1)]
    peers += [at(xh, zpeer(d), core, y, xl) for d in range(1, 8)]
    for a in (0, 1):
        for c in (0, 1):
            for d in range(4):
                for b in (0, 1):
                    if (a, c, d, b) != (0, 0, 0, 0):
                        peers.append(at(flip(xh, a), z, flip(core, c), ypeer(d), flip(xl, b)))
    greet(peers)

    sends = []

    def go(src, dst, send, recv, to):
        cp = remote(src, dst, send, recv, to)
        cp.start()
        sends.append(cp)

    def came(dst, send, recv):
        remote(dst, dst, send, recv, sibling).wait_recv()

    own = []
    for t in range(3):
        here = wg_ref.at[t, xh, z, core]
        go(
            w_ref.at[:, pl.ds(pl.multiple_of(t * 1024 + other * 512, 512), 512)],
            here, w_send.at[t], w_recv.at[t], sibling,
        )
        cp = pltpu.make_async_copy(
            w_ref.at[:, pl.ds(pl.multiple_of(t * 1024 + core * 512, 512), 512)], here, w_local.at[t]
        )
        cp.start()
        own.append(cp)
    go(acts.at[core], acts.at[core], act_send, act_recv, sibling)

    hops = {(0, 0): 4, (0, 1): 3, (1, 0): 3, (1, 1): 4}

    def slab(t, s, index):
        return wg_ref.at[t, xh if s == 0 else 1 - xh, lax.rem(index + 16, 8)]

    def forward(s, d, k, t):
        moved = slab(t, s, z - k if d == 0 else z + k)
        go(moved, moved, r_send.at[s, d, k, t], r_recv.at[s, d, k, t], up if d == 0 else down)

    def arrived(s, d, k, t):
        came(
            slab(t, s, z - 1 - k if d == 0 else z + 1 + k),
            r_send.at[s, d, k, t], r_recv.at[s, d, k, t],
        )

    for t in range(3):
        own[t].wait()
        came(wg_ref.at[t, xh, z, other], w_send.at[t], w_recv.at[t])
        mine = slab(t, 0, z)
        go(mine, mine, p_send.at[t], p_recv.at[t], partner)
        forward(0, 0, 0, t)
        forward(0, 1, 0, t)

    side_chip = chip + 2 * core - 1 + 16
    tensors = ((x_ref, lambda c: xr_ref.at[c]), (g_ref, lambda c: gr_ref))
    locals_ = []

    def send_region(i, dns):
        src, dst = tensors[i]
        for dn in dns:
            lo, count, to_row = ROWS[dn]
            for side in (0, 1):
                for rel in (0, 1):
                    c = core if rel == 0 else other
                    if side == 0:
                        source = src.at[pl.ds(lo, count), :, :, half_of(c)]
                        target = dst(c).at[pl.ds(to_row, count), pl.ds(1 + 2 * core, 2)]
                        slot = core
                        to = device(n + dn + 8, chip, c)
                    else:
                        source = src.at[pl.ds(lo, count), pl.ds(core, 1), :, half_of(c)]
                        target = dst(c).at[pl.ds(to_row, count), pl.ds(5 * other, 1)]
                        slot = 3 - core
                        to = device(n + dn + 8, side_chip, c)
                    if dn == 0 and side == 0 and rel == 0:
                        cp = pltpu.make_async_copy(source, target, h_local.at[i])
                        cp.start()
                        locals_.append(cp)
                    else:
                        go(
                            source, target, h_send.at[i, dn + 1, side, rel],
                            h_recv.at[i, dn + 1, slot], to,
                        )

    def region_came(i, dst, dn, piece):
        lo, count, to_row = ROWS[dn]
        if piece < 2:
            slot = other if dn == 0 else piece
            landed = dst.at[pl.ds(to_row, count), pl.ds(1 + 2 * slot, 2)]
        else:
            slot = piece
            landed = dst.at[pl.ds(to_row, count), pl.ds(0 if piece == 2 else 5, 1)]
        came(landed, h_send.at[i, dn + 1, 0, 0], h_recv.at[i, dn + 1, slot])

    pieces = [(dn, piece) for dn in (-1, 0, 1) for piece in range(4) if (dn, piece) != (0, 1)]
    send_region(0, (-1, 1, 0))
    for t in range(3):
        came(slab(t, 1, z), p_send.at[t], p_recv.at[t])
        forward(1, 0, 0, t)
        forward(1, 1, 0, t)
    send_region(1, (0,))
    for d in (2, 1, 3):
        want = ypeer(d) // 2
        for rel in (0, 1):
            go(
                x_ref.at[:, :, :, half_of(want)], xall_ref.at[3 - d, core],
                e_send.at[d - 1, rel], e_recv.at[3 - d, core],
                at(xh, z, core if rel == 0 else other, ypeer(d), xl),
            )

    def project(part, first):
        for t, region in enumerate((qr_ref, kr, vr)):

            def chunk(i, carry, t=t, region=region):
                rows = pl.ds(4 * i, 4)
                out = nn(xr_ref[part, rows].reshape(192, 512), wg_ref[t, part].reshape(512, 512))
                if first:
                    acc[t, rows] = out.reshape(4, 6, 8, 512)
                else:
                    out = out.reshape(4, 6, 8, 512) + acc[t, rows]
                    acc[t, rows] = out
                    region[rows] = out.astype(BF16).reshape(4, 48, 512)
                return carry

            lax.fori_loop(0, 5, chunk, 0)

    def hop(s, k):
        for t in range(3):
            for d in range(2):
                if k <= hops[s, d]:
                    arrived(s, d, k - 1, t)
                if k < hops[s, d]:
                    forward(s, d, k, t)

    hop(0, 1)
    hop(1, 1)
    hop(0, 2)
    locals_[0].wait()
    for dn, piece in pieces:
        region_came(0, xr_ref.at[core], dn, piece)
    go(xr_ref.at[core], xr_ref.at[core], s_send, s_recv, sibling)
    hop(1, 2)
    send_region(1, (-1, 1))
    hop(0, 3)
    hop(1, 3)
    hop(0, 4)
    for hf in range(2):
        bias[hf] = window_bias(hf)
    came(xr_ref.at[other], s_send, s_recv)
    project(xh, True)
    hop(1, 4)
    project(1 - xh, False)
    for t in range(3):
        for hf in range(2):
            own_t = acc[t, 6:14, 1 + 2 * hf : 3 + 2 * hf].reshape(128, 512).astype(BF16)
            if t == 0:
                qown[hf] = own_t * SCALE
            elif t == 1:
                kown_ref[hf] = own_t * SCALE
            else:
                vown_ref[hf] = own_t

    locals_[1].wait()
    region_came(1, gr_ref, 0, 0)
    came(acts.at[other], act_send, act_recv)
    inner = lax.broadcasted_iota(jnp.int32, (128, 128), 0)
    for hf in range(2):
        groups = pl.ds(1 + 2 * hf, 2)
        gown[hf] = gr_ref[6:14, groups].astype(F32).reshape(128, 512).astype(BF16)
        ldacc[...] = jnp.zeros_like(ldacc)
        active = jnp.where(lax.rem(inner, 16) < 8, acts[hf, 0:1, :], acts[hf, 1:2, :])

        def pair(hp, carry, hf=hf, active=active):
            lanes = lanes_of(hp)
            low, masks, lane = head_masks()
            keys = kr[:, 16 * hf : 16 * hf + 32, lanes].reshape(640, 128)
            values = vr[:, 16 * hf : 16 * hf + 32, lanes].reshape(640, 128)
            query = qown[hf, :, lanes]
            grad = gown[hf, :, lanes]
            outs, dqs = [], []
            ld = ldacc[...]
            for j in range(2):
                s = nt(query * masks[j], keys) + bias[hf]
                top = jnp.max(s, axis=1, keepdims=True)
                e = jnp.exp(s - top)
                total = jnp.sum(e, axis=1, keepdims=True)
                p = e * (1.0 / total)
                lse = top + jnp.log(total)
                out = nn(p.astype(BF16), values)
                out = out.astype(BF16).astype(F32)
                gm = grad * masks[j]
                delta = jnp.sum(gm.astype(F32) * out, axis=1, keepdims=True)
                dp = nt(gm, values)
                ds = (p * (dp - delta) * SCALE).astype(BF16)
                dqs.append(nn(ds, keys))
                outs.append(out)
                on = active > 0.0
                head = 2 * hp + j
                ld = jnp.where(lane == head, jnp.where(on, lse, HUGE), ld)
                ld = jnp.where(lane == head + 8, jnp.where(on, delta, 0.0), ld)
            ldacc[...] = ld
            attn_ref[hf, :, lanes] = (jnp.where(low, outs[0], outs[1]) * active).astype(BF16)
            dq_ref[hp, hf] = (jnp.where(low, dqs[0], dqs[1]) * active).astype(BF16)
            return carry

        lax.fori_loop(0, 4, pair, 0)
        ldall[:, 16 * hf : 16 * hf + 16, :] = ldacc[...].reshape(8, 16, 128)
    for i in range(2):
        ld_ref[:, 128 * i : 128 * i + 128] = ldall[4 * i : 4 * i + 4].reshape(128, 128).T[:16]

    for dn, dc in NEAR:
        go(
            ld_ref, ldb.at[1 - dn, 1 - dc], ld_send.at[dn + 1, dc + 1], ld_recv.at[1 - dn, 1 - dc],
            device(n + dn + 8, chip + dc + 16, core),
        )
    for d in (2, 1, 3):
        go(
            dq_ref.at[pl.ds(2 * lax.rem(ypeer(d), 2), 2)], gall.at[4 - d, pl.ds(0, 2)],
            q_send.at[d - 1], q_recv.at[3 - d], at(xh, z, core, ypeer(d), xl),
        )
    go(attn_ref.at[other], attn_out.at[:, half_of(core)], a_send, a_recv, sibling)
    attn_own = pltpu.make_async_copy(attn_ref.at[core], attn_out.at[:, half_of(core)], o_sem.at[0])
    attn_own.start()

    def share(hp):
        for d in (2, 1, 3):
            go(
                kv.at[hp, lax.rem(ypeer(d), 2)], gall.at[4 - d, 2 + hp],
                k_send.at[hp, d - 1], k_recv.at[hp, 3 - d], at(xh, z, core, ypeer(d), xl),
            )

    def product(first, count):
        if count == 2:
            columns = jnp.concatenate(
                [gall[:, first + j].reshape(1024, 128) for j in range(count)], axis=1
            )
        else:
            columns = gall[:, first].reshape(1024, 128)

        def rows(i, carry):
            out = nn(xt_ref[pl.ds(pl.multiple_of(i * 128, 128), 128), :], columns)
            out = out.reshape(2, 2, 2, 2, 8, 128 * count)
            for j in range(count):
                p[first + j, pl.ds(2 * i, 2)] = out[..., 128 * j : 128 * j + 128]
            return carry

        lax.fori_loop(0, 4, rows, 0)
        for b in range(first, first + count):
            for i in (2, 0, 1):
                a, l = flip(xh, XPEERS[i][0]), flip(xl, XPEERS[i][1])
                go(
                    p.at[b, :, l, a], rx.at[b, i], x_send.at[b, i], x_recv.at[b, i],
                    at(a, z, core, y, l),
                )

    def product_q():
        for r in range(3):
            came(gall.at[r + 1, pl.ds(0, 2)], q_send.at[r], q_recv.at[r])
        for j in range(2):
            gall[0, j] = dq_ref[2 * col_half + j]
        product(0, 2)

    def product_kv(hp):
        for r in range(3):
            came(gall.at[r + 1, 2 + hp], k_send.at[hp, r], k_recv.at[hp, r])
        gall[0, 2 + hp] = kv[hp, col_half]
        product(2 + hp, 1)

    def sum_x(b):
        for i in range(3):
            came(rx.at[b, i], x_send.at[b, i], x_recv.at[b, i])
        for j in range(8):
            cz[j, b] = p[b, j, xl, xh] + rx[b, 0, j] + rx[b, 1, j] + rx[b, 2, j]

    batches = ((0, 4), (4, 2))

    def spread(h):
        lo, count = batches[h]
        for d in (4, 3, 5, 2, 6, 1, 7):
            go(
                cz.at[zpeer(d), pl.ds(lo, count)], rc.at[d - 1, pl.ds(lo, count)],
                c_send.at[h, d - 1], c_recv.at[h, d - 1], at(xh, zpeer(d), core, y, xl),
            )

    factor = 1.0 / math.sqrt(32768.0)

    def sum_z(h):
        lo, count = batches[h]
        for d in range(7):
            came(rc.at[d, pl.ds(lo, count)], c_send.at[h, d], c_recv.at[h, d])
        for b in range(lo, lo + count):
            total = cz[z, b]
            for d in range(7):
                total = total + rc[d, b]
            total = total.reshape(16, 128) * factor
            if b < 2:
                fin_q[:, 128 * b : 128 * b + 128] = total
            else:
                fin_kv[:, 128 * (b - 2) : 128 * (b - 1)] = total

    for dn, piece in pieces:
        if (dn, piece) != (0, 0):
            region_came(1, gr_ref, dn, piece)

    def regroup(i, carry):
        rows = gr_ref[pl.ds(4 * i, 4)].astype(F32).reshape(192, 512)
        grs_ref[pl.ds(4 * i, 4)] = rows.astype(BF16).reshape(4, 48, 512)
        return carry

    lax.fori_loop(0, 5, regroup, 0)
    for r in range(3):
        for c in range(2):
            came(xall_ref.at[r, c], e_send.at[r, c], e_recv.at[r, c])
    for hf in range(2):
        groups = pl.ds(1 + 2 * hf, 2)
        for r in range(4):
            if r == 0:
                tokens = xr_ref[row_half, 6:14, groups]
            else:
                tokens = xall_ref[r - 1, hf]
            tokens = tokens.astype(F32).reshape(128, 512)
            to_lane = 256 * r + 128 * hf
            for i in range(4):
                xt_ref[128 * i : 128 * i + 128, to_lane : to_lane + 128] = (
                    tokens[:, 128 * i : 128 * i + 128].T.astype(BF16)
                )
    ldb[1, 1] = ld_ref[...]
    for dn, dc in NEAR:
        came(ldb.at[1 - dn, 1 - dc], ld_send.at[dn + 1, dc + 1], ld_recv.at[1 - dn, 1 - dc])
    column = lax.rem(lax.broadcasted_iota(jnp.int32, (16, 256), 1), 32)
    for hf in range(2):
        parts = []
        for r in range(3):
            left, mid, right = ldb[r, 0], ldb[r, 1], ldb[r, 2]
            if hf == 0:
                part = jnp.where(column < 8, pltpu.roll(left, 232, 1), pltpu.roll(mid, 8, 1))
            else:
                part = jnp.where(column < 24, pltpu.roll(mid, 248, 1), pltpu.roll(right, 24, 1))
            parts.append(part)
        lds[hf] = pltpu.roll(jnp.concatenate(parts, axis=1), 768 - 64, 1)[:, :640]

    low, masks, _ = head_masks()

    def key_side(hp):
        lanes = slice(128 * hp, 128 * hp + 128)

        def side(hf, carry):
            window = pl.ds(pl.multiple_of(16 * hf, 16), 32)
            query = qr_ref[:, window, lanes].reshape(640, 128)
            grad = grs_ref[:, window, lanes].reshape(640, 128)
            keys = kown_ref[hf, :, lanes]
            values = vown_ref[hf, :, lanes]
            dks, dvs = [], []
            for j in range(2):
                head = 2 * hp + j
                s = nt(keys * masks[j], query) + bias[hf]
                e = jnp.exp(s - lds[hf, head : head + 1, :])
                dvs.append(nn(e.astype(BF16), grad))
                dp = nt(values * masks[j], grad)
                ds = (e * (dp - lds[hf, head + 8 : head + 9, :]) * SCALE).astype(BF16)
                dks.append(nn(ds, query))
            kv[hp, 0, hf] = jnp.where(low, dks[0], dks[1]).astype(BF16)
            kv[hp, 1, hf] = jnp.where(low, dvs[0], dvs[1]).astype(BF16)
            return carry

        lax.fori_loop(0, 2, side, 0)
        share(hp)

    key_side(0)
    product_q()
    key_side(1)
    product_kv(0)
    key_side(2)
    product_kv(1)
    sum_x(0)
    sum_x(1)
    key_side(3)
    product_kv(2)
    sum_x(2)
    sum_x(3)
    spread(0)

    all_q = jnp.concatenate([dq_ref[h].reshape(256, 128) for h in range(4)], axis=1)
    all_k = jnp.concatenate([kv[h, 0].reshape(256, 128) for h in range(4)], axis=1)
    all_v = jnp.concatenate([kv[h, 1].reshape(256, 128) for h in range(4)], axis=1)

    def input_columns(i, carry):
        rows = pl.ds(pl.multiple_of(i * 256, 256), 256)
        part = [wg_ref[t, i // 2, pl.ds(4 * lax.rem(i, 2), 4)].reshape(256, 512) for t in range(3)]
        total = nt(all_q, part[0]) + nt(all_k, part[1]) + nt(all_v, part[2])
        gx[:, :, rows] = total.reshape(2, 128, 256)
        return carry

    product_kv(3)
    lax.fori_loop(0, 4, input_columns, 0)
    go(gx.at[other], gxr, g_send, g_recv, sibling)
    sum_x(4)
    sum_x(5)
    spread(1)
    came(gxr, g_send, g_recv)
    gxo[...] = (gx[core] + gxr[...]).astype(BF16)
    gx_own = pltpu.make_async_copy(gxo, gx_out, o_sem.at[1])
    gx_own.start()
    sum_z(0)
    sum_z(1)

    def spots(c, part, a):
        rows = pl.ds(pl.multiple_of(16 * a, 16), 16)
        q_at = pl.multiple_of(c * 512 + part * 256, 256)
        kv_at = pl.multiple_of((1 + part) * 1024 + c * 512, 512)
        return gw_out.at[rows, pl.ds(q_at, 256)], gw_out.at[rows, pl.ds(kv_at, 512)]

    mine = spots(core, col_half, xh)
    for i, fin in enumerate((fin_q, fin_kv)):
        recv = f_recv.at[i, core, col_half, xh]
        for d in (2, 1, 3):
            for b in (0, 1):
                go(fin, mine[i], f_send.at[i, d, b], recv, at(row_half, z, xl, ypeer(d), flip(xl, b)))
        go(fin, mine[i], f_send.at[i, 0, 1], recv, at(row_half, z, xl, y, 1 - xl))
        away = remote(fin, mine[i], f_send.at[i, 0, 0], recv, at(row_half, z, xl, y, xl))
        here = pltpu.make_async_copy(fin, mine[i], f_local.at[i])
        is_here = (core == xl) & (row_half == xh)

        @pl.when(is_here)
        def _():
            here.start()
            here.wait()

        @pl.when(jnp.logical_not(is_here))
        def _():
            away.start()
            away.wait_send()

    attn_own.wait()
    gx_own.wait()
    came(attn_out.at[:, half_of(other)], a_send, a_recv)
    for c in range(2):
        for part in range(2):
            for a in range(2):
                landed = spots(c, part, a)
                own = (
                    (c == core) & (part == col_half) & (a == xh) & (row_half == xh) & (xl == core)
                )
                for i in range(2):

                    @pl.when(jnp.logical_not(own))
                    def _():
                        came(landed[i], f_send.at[i, 0, 0], f_recv.at[i, c, part, a])

    for cp in sends:
        cp.wait_send()


def layer(x4, g4, weight, block_list, block_count):
    dma = pltpu.SemaphoreType.DMA
    vmem = lambda *shape: pltpu.VMEM(shape, F32)
    half = lambda *shape: pltpu.VMEM(shape, BF16)
    shape = jax.ShapeDtypeStruct
    smem = pl.BlockSpec(memory_space=pltpu.SMEM)
    return pl.pallas_call(
        layer_kernel,
        out_shape=(
            shape((128, 1024), BF16), shape((128, 1024), BF16), shape((32, 3072), F32),
        ),
        in_specs=[VM] * 3 + [smem] * 2,
        out_specs=(ANY,) * 3,
        scratch_shapes=[
            half(2, 20, 6, 8, 512), half(20, 6, 8, 512), half(3, 2, 8, 2, 32, 512),
            half(3, 2, 8, 2, 8, 512), vmem(2, 8, 128),
            vmem(3, 20, 6, 8, 512), half(20, 48, 512), half(20, 48, 512), half(20, 48, 512),
            half(20, 48, 512), half(2, 128, 512), half(2, 128, 512), half(2, 128, 512),
            half(2, 128, 512), vmem(128, 128), vmem(8, 32, 128), vmem(16, 256),
            half(4, 2, 128, 128), half(2, 128, 512), half(512, 1024),
            half(4, 6, 2, 128, 128), vmem(6, 8, 2, 2, 2, 8, 128), vmem(6, 3, 8, 2, 8, 128),
            vmem(8, 6, 2, 8, 128), vmem(7, 6, 2, 8, 128), vmem(16, 256), vmem(16, 512),
            half(4, 2, 2, 128, 128), vmem(2, 16, 640), vmem(3, 3, 16, 256), vmem(2, 128, 640),
            vmem(2, 128, 1024), vmem(128, 1024), half(128, 1024),
            dma((2, 3, 2, 2)), dma((2, 3, 4)), dma((2,)), dma, dma, dma, dma,
            dma((3,)), dma((3,)), dma((3,)), dma((3,)), dma((3,)),
            dma((2, 2, 4, 3)), dma((2, 2, 4, 3)), dma((3, 2)), dma((3, 2)),
            dma((3, 3)), dma((3, 3)), dma((2,)), dma, dma, dma, dma,
            dma((3,)), dma((3,)), dma((4, 3)), dma((4, 3)), dma((6, 3)), dma((6, 3)),
            dma((2, 7)), dma((2, 7)), dma((2, 4, 2)), dma((2, 2, 2, 2)), dma((2,)),
        ],
        compiler_params=pltpu.CompilerParams(
            collective_id=0, has_side_effects=True, vmem_limit_bytes=VMEM_LIMIT
        ),
        name="layer",
    )(x4, g4, weight, block_list, block_count)


def local(image_tokens, qkv_weight, block_list, block_count, out_grad):
    attn_out, grad_x, grad_w = layer(
        image_tokens.reshape(8, 2, 8, 1024), out_grad.reshape(8, 2, 8, 1024), qkv_weight,
        block_list, block_count,
    )
    return attn_out.reshape(8, 16, 1024), grad_x.reshape(8, 16, 1024), grad_w


def solution(mesh):
    placed = (
        P("narrow", "wide", None),
        P("wide", None),
        P("narrow", "wide"),
        P("narrow", "wide"),
        P("narrow", "wide", None),
    )
    return jax.shard_map(
        local,
        mesh=mesh,
        in_specs=placed,
        out_specs=(P("narrow", "wide", None), P("narrow", "wide", None), P("wide", None)),
        check_vma=False,
    )
```

time: 136 us -> 123 us (0.904)
  Pallas kernels: 128 us -> 119 us
  local copies, waits for them, and re-layouts: 5.99 us -> 3.19 us
    pallas_call x3 -> x1, Pallas kernels: 128 us -> 119 us  [layer(): pl.pallas_call(layer_kernel, out_shape=(shape((128, 1024), BF16), shape((...]
    unnamed x3 -> x7, local copies, waits for them, and re-layouts: 5.1 us -> 3.19 us
where the time goes in v4:
time: 123 us
  Pallas kernels  119 us (97%)
  local copies, waits for them, and re-layouts  3.19 us (3%)
  between operations  1.3 us (1%)
    pallas_call x1, Pallas kernels, layer(): pl.pallas_call(layer_kernel, out_shape=(shape((128, 1024), BF16), shape((...  119 us
    unnamed x7, local copies, waits for them, and re-layouts  3.19 us

profile of v4, /device:TPU:1, one launch (start us, length us, event | category | flops | bytes accessed | tf_op | source)
XLA Modules:
  0.0 123.1 jit_solution(4574608253156072351)
XLA Ops:
  1.3 118.6 %layer.1 = (bf16[128,1024]{1,0:T(8,128)(2,1)}, bf16[128,1024]{1,0:T(8,128)(2,1)}, f32[32,3072]{1,0:T(8,128)}) custom-call(bf16[8,2,8,1024]{3,2,1,0:T(8,128)(2,1)} %bitcast.4, bf16[8,2,8,1024]{3,2,1,0:T(8,128)(2,1)} %bitcast.5, bf16[32,3072]{1,0:T(8,128)(2,1)} %w_ref.1, s32[1,2]{1,0:T(1,128)} %list_ref.1, s32[1,1]{1,0:T(1,128)S(6)} %copy.11.count_ref), custom_call_target="tpu_custom_call" | custom-call | tf_op jit(solution)/shard_map/layer/pallas_call | solution.py:600
  119.9 0.0 copy-start.1
  119.9 0.0 copy-start
  119.9 1.7 %copy.12 = bf16[8,16,1024]{2,1,0:T(8,128)(2,1)} copy(bf16[8,16,1024]{2,1,0:T(8,128)(2,1)} %bitcast.7) | data formatting | bytes 524288
  121.6 0.0 copy-done.1
  121.7 0.7 copy.13
  122.4 0.0 copy-done
  122.4 0.7 copy.14
Async XLA Ops:
  119.9 1.8 %copy-start.1 = (bf16[128,1024]{1,0:T(8,128)(2,1)S(1)}, bf16[128,1024]{1,0:T(8,128)(2,1)}, u32[]{:S(2)}) copy-start(bf16[128,1024]{1,0:T(8,128)(2,1)} %get-tuple-element.7) | copy-start | bytes 786436
  119.9 2.5 %copy-start = (f32[32,3072]{1,0:T(8,128)S(1)}, f32[32,3072]{1,0:T(8,128)}, u32[]{:S(2)}) copy-start(f32[32,3072]{1,0:T(8,128)} %get-tuple-element.14) | copy-start | bytes 1179652

commit v5 on v4

--- a/solution.py
+++ b/solution.py
@@ -76,8 +76,8 @@
     return lax.dot_general(a, b, (((0,), (0,)), ((), ())), preferred_element_type=F32)
 
 
-def lanes_of(hp):
-    return pl.ds(pl.multiple_of(hp * 128, 128), 128)
+def stacked(pair, masks):
+    return jnp.concatenate([pair * masks[0], pair * masks[1]], axis=0)
 
 
 def head_masks():
@@ -90,11 +90,15 @@
 NEAR = tuple((dn, dc) for dn in (-1, 0, 1) for dc in (-1, 0, 1) if (dn, dc) != (0, 0))
 
 
+Q_BLOCKS = (0, 3)
+KV_BLOCKS = (1, 2, 4, 5)
+
+
 def layer_kernel(
     x_ref, g_ref, w_ref, list_ref, count_ref,
     attn_out, gx_out, gw_out,
     xr_ref, gr_ref, wg_ref, xall_ref, acts,
-    acc, qr_ref, kr, vr, grs_ref, qown, kown_ref, vown_ref, gown, ldacc, ldall, ld_ref,
+    acc, qr_ref, kr, vr, grs_ref, qown, kown_ref, vown_ref, gown, on_tokens, ldall, ld_ref,
     dq_ref, attn_ref, xt_ref,
     gall, p, rx, cz, rc, fin_q, fin_kv, kv, lds, ldb, bias, gx, gxr, gxo,
     h_send, h_recv, h_local, s_send, s_recv, act_send, act_recv,
@@ -307,104 +311,96 @@
     for hf in range(2):
         groups = pl.ds(1 + 2 * hf, 2)
         gown[hf] = gr_ref[6:14, groups].astype(F32).reshape(128, 512).astype(BF16)
-        ldacc[...] = jnp.zeros_like(ldacc)
-        active = jnp.where(lax.rem(inner, 16) < 8, acts[hf, 0:1, :], acts[hf, 1:2, :])
-
-        def pair(hp, carry, hf=hf, active=active):
-            lanes = lanes_of(hp)
-            low, masks, lane = head_masks()
-            keys = kr[:, 16 * hf : 16 * hf + 32, lanes].reshape(640, 128)
-            values = vr[:, 16 * hf : 16 * hf + 32, lanes].reshape(640, 128)
+        on_tokens[hf] = jnp.where(lax.rem(inner, 16) < 8, acts[hf, 0:1, :], acts[hf, 1:2, :])
+
+    low, masks, lane = head_masks()
+
+    def query_side(hp):
+        lanes = slice(128 * hp, 128 * hp + 128)
+
+        def side(hf, carry):
+            window = pl.ds(pl.multiple_of(16 * hf, 16), 32)
+            keys = kr[:, window, lanes].reshape(640, 128)
+            values = vr[:, window, lanes].reshape(640, 128)
             query = qown[hf, :, lanes]
             grad = gown[hf, :, lanes]
-            outs, dqs = [], []
-            ld = ldacc[...]
+            active = on_tokens[hf]
+            on = active > 0.0
+            s = nt(stacked(query, masks), keys)
+            s = (s.reshape(2, 128, 640) + bias[hf]).reshape(256, 640)
+            top = jnp.max(s, axis=1, keepdims=True)
+            e = jnp.exp(s - top)
+            total = jnp.sum(e, axis=1, keepdims=True)
+            e = e * (1.0 / total)
+            lse = top + jnp.log(total)
+            out = nn(e.astype(BF16), values).astype(BF16).astype(F32)
+            gm = stacked(grad, masks)
+            delta = jnp.sum(gm.astype(F32) * out, axis=1, keepdims=True)
+            dp = nt(gm, values)
+            ds = (e * (dp - delta) * SCALE).astype(BF16)
+            dqs = nn(ds, keys)
+            ld = jnp.zeros((128, 128), F32)
             for j in range(2):
-                s = nt(query * masks[j], keys) + bias[hf]
-                top = jnp.max(s, axis=1, keepdims=True)
-                e = jnp.exp(s - top)
-                total = jnp.sum(e, axis=1, keepdims=True)
-                p = e * (1.0 / total)
-                lse = top + jnp.log(total)
-                out = nn(p.astype(BF16), values)
-                out = out.astype(BF16).astype(F32)
-                gm = grad * masks[j]
-                delta = jnp.sum(gm.astype(F32) * out, axis=1, keepdims=True)
-                dp = nt(gm, values)
-                ds = (p * (dp - delta) * SCALE).astype(BF16)
-                dqs.append(nn(ds, keys))
-                outs.append(out)
-                on = active > 0.0
-                head = 2 * hp + j
-                ld = jnp.where(lane == head, jnp.where(on, lse, HUGE), ld)
-                ld = jnp.where(lane == head + 8, jnp.where(on, delta, 0.0), ld)
-            ldacc[...] = ld
-            attn_ref[hf, :, lanes] = (jnp.where(low, outs[0], outs[1]) * active).astype(BF16)
-            dq_ref[hp, hf] = (jnp.where(low, dqs[0], dqs[1]) * active).astype(BF16)
+                rows = slice(128 * j, 128 * j + 128)
+                ld = jnp.where(lane == j, jnp.where(on, lse[rows], HUGE), ld)
+                ld = jnp.where(lane == j + 2, jnp.where(on, delta[rows], 0.0), ld)
+            ldall[:, pl.ds(pl.multiple_of(16 * hf, 16), 16), :] = ld.reshape(8, 16, 128)
+            attn_ref[hf, :, lanes] = (jnp.where(low, out[:128], out[128:]) * active).astype(BF16)
+            dq_ref[hp, hf] = (jnp.where(low, dqs[:128], dqs[128:]) * active).astype(BF16)
             return carry
 
-        lax.fori_loop(0, 4, pair, 0)
-        ldall[:, 16 * hf : 16 * hf + 16, :] = ldacc[...].reshape(8, 16, 128)
-    for i in range(2):
-        ld_ref[:, 128 * i : 128 * i + 128] = ldall[4 * i : 4 * i + 4].reshape(128, 128).T[:16]
-
-    for dn, dc in NEAR:
-        go(
-            ld_ref, ldb.at[1 - dn, 1 - dc], ld_send.at[dn + 1, dc + 1], ld_recv.at[1 - dn, 1 - dc],
-            device(n + dn + 8, chip + dc + 16, core),
-        )
-    for d in (2, 1, 3):
-        go(
-            dq_ref.at[pl.ds(2 * lax.rem(ypeer(d), 2), 2)], gall.at[4 - d, pl.ds(0, 2)],
-            q_send.at[d - 1], q_recv.at[3 - d], at(xh, z, core, ypeer(d), xl),
-        )
-    go(attn_ref.at[other], attn_out.at[:, half_of(core)], a_send, a_recv, sibling)
-    attn_own = pltpu.make_async_copy(attn_ref.at[core], attn_out.at[:, half_of(core)], o_sem.at[0])
-    attn_own.start()
+        lax.fori_loop(0, 2, side, 0)
+        for i in range(2):
+            ld_ref[hp, :, 128 * i : 128 * i + 128] = (
+                ldall[4 * i : 4 * i + 4].reshape(128, 128).T[:8]
+            )
+        ldb[hp, 1, 1] = ld_ref[hp]
+        for dn, dc in NEAR:
+            go(
+                ld_ref.at[hp], ldb.at[hp, 1 - dn, 1 - dc], ld_send.at[hp, dn + 1, dc + 1],
+                ld_recv.at[hp, 1 - dn, 1 - dc], device(n + dn + 8, chip + dc + 16, core),
+            )
+
+    def share_q(j):
+        for d in (2, 1, 3):
+            go(
+                dq_ref.at[2 * j + lax.rem(ypeer(d), 2)], gall.at[4 - d, Q_BLOCKS[j]],
+                q_send.at[j, d - 1], q_recv.at[j, 3 - d], at(xh, z, core, ypeer(d), xl),
+            )
 
     def share(hp):
         for d in (2, 1, 3):
             go(
-                kv.at[hp, lax.rem(ypeer(d), 2)], gall.at[4 - d, 2 + hp],
+                kv.at[hp, lax.rem(ypeer(d), 2)], gall.at[4 - d, KV_BLOCKS[hp]],
                 k_send.at[hp, d - 1], k_recv.at[hp, 3 - d], at(xh, z, core, ypeer(d), xl),
             )
 
-    def product(first, count):
-        if count == 2:
-            columns = jnp.concatenate(
-                [gall[:, first + j].reshape(1024, 128) for j in range(count)], axis=1
-            )
-        else:
-            columns = gall[:, first].reshape(1024, 128)
+    def product(b):
+        columns = gall[:, b].reshape(1024, 128)
 
         def rows(i, carry):
             out = nn(xt_ref[pl.ds(pl.multiple_of(i * 128, 128), 128), :], columns)
-            out = out.reshape(2, 2, 2, 2, 8, 128 * count)
-            for j in range(count):
-                p[first + j, pl.ds(2 * i, 2)] = out[..., 128 * j : 128 * j + 128]
+            p[b, pl.ds(2 * i, 2)] = out.reshape(2, 2, 2, 2, 8, 128)
             return carry
 
         lax.fori_loop(0, 4, rows, 0)
-        for b in range(first, first + count):
-            for i in (2, 0, 1):
-                a, l = flip(xh, XPEERS[i][0]), flip(xl, XPEERS[i][1])
-                go(
-                    p.at[b, :, l, a], rx.at[b, i], x_send.at[b, i], x_recv.at[b, i],
-                    at(a, z, core, y, l),
-                )
-
-    def product_q():
+        for i in (2, 0, 1):
+            a, l = flip(xh, XPEERS[i][0]), flip(xl, XPEERS[i][1])
+            go(p.at[b, :, l, a], rx.at[b, i], x_send.at[b, i], x_recv.at[b, i], at(a, z, core, y, l))
+
+    def product_q(j):
+        b = Q_BLOCKS[j]
         for r in range(3):
-            came(gall.at[r + 1, pl.ds(0, 2)], q_send.at[r], q_recv.at[r])
-        for j in range(2):
-            gall[0, j] = dq_ref[2 * col_half + j]
-        product(0, 2)
+            came(gall.at[r + 1, b], q_send.at[j, r], q_recv.at[j, r])
+        gall[0, b] = dq_ref[2 * j + col_half]
+        product(b)
 
     def product_kv(hp):
+        b = KV_BLOCKS[hp]
         for r in range(3):
-            came(gall.at[r + 1, 2 + hp], k_send.at[hp, r], k_recv.at[hp, r])
-        gall[0, 2 + hp] = kv[hp, col_half]
-        product(2 + hp, 1)
+            came(gall.at[r + 1, b], k_send.at[hp, r], k_recv.at[hp, r])
+        gall[0, b] = kv[hp, col_half]
+        product(b)
 
     def sum_x(b):
         for i in range(3):
@@ -433,11 +429,90 @@
             for d in range(7):
                 total = total + rc[d, b]
             total = total.reshape(16, 128) * factor
-            if b < 2:
-                fin_q[:, 128 * b : 128 * b + 128] = total
+            if b in Q_BLOCKS:
+                fin_q[Q_BLOCKS.index(b)] = total
             else:
-                fin_kv[:, 128 * (b - 2) : 128 * (b - 1)] = total
-
+                hp = KV_BLOCKS.index(b)
+                fin_kv[hp // 2, :, 128 * (hp % 2) : 128 * (hp % 2) + 128] = total
+
+    column = lax.rem(lax.broadcasted_iota(jnp.int32, (8, 256), 1), 32)
+
+    def totals_came(hp):
+        for dn, dc in NEAR:
+            came(
+                ldb.at[hp, 1 - dn, 1 - dc], ld_send.at[hp, dn + 1, dc + 1],
+                ld_recv.at[hp, 1 - dn, 1 - dc],
+            )
+        for hf in range(2):
+            parts = []
+            for r in range(3):
+                left, mid, right = ldb[hp, r, 0], ldb[hp, r, 1], ldb[hp, r, 2]
+                if hf == 0:
+                    part = jnp.where(column < 8, pltpu.roll(left, 232, 1), pltpu.roll(mid, 8, 1))
+                else:
+                    part = jnp.where(column < 24, pltpu.roll(mid, 248, 1), pltpu.roll(right, 24, 1))
+                parts.append(part)
+            lds[hp, hf] = pltpu.roll(jnp.concatenate(parts, axis=1), 768 - 64, 1)[:, :640]
+
+    def key_side(hp):
+        lanes = slice(128 * hp, 128 * hp + 128)
+        totals_came(hp)
+
+        def side(hf, carry):
+            window = pl.ds(pl.multiple_of(16 * hf, 16), 32)
+            query = qr_ref[:, window, lanes].reshape(640, 128)
+            grad = grs_ref[:, window, lanes].reshape(640, 128)
+            keys = kown_ref[hf, :, lanes]
+            values = vown_ref[hf, :, lanes]
+            s = nt(stacked(keys, masks), query).reshape(2, 128, 640) + bias[hf]
+            e = jnp.exp(s - lds[hp, hf, 0:2].reshape(2, 1, 640))
+            dvs = nn(e.astype(BF16).reshape(256, 640), grad)
+            dp = nt(stacked(values, masks), grad).reshape(2, 128, 640)
+            ds = (e * (dp - lds[hp, hf, 2:4].reshape(2, 1, 640)) * SCALE).astype(BF16)
+            dks = nn(ds.reshape(256, 640), query)
+            kv[hp, 0, hf] = jnp.where(low, dks[:128], dks[128:]).astype(BF16)
+            kv[hp, 1, hf] = jnp.where(low, dvs[:128], dvs[128:]).astype(BF16)
+            return carry
+
+        lax.fori_loop(0, 2, side, 0)
+        share(hp)
+
+    def spots(c, part, a):
+        rows = pl.ds(pl.multiple_of(16 * a, 16), 16)
+        q_at = c * 512 + part * 128
+        kv_at = (1 + part) * 1024 + c * 512
+        return [
+            gw_out.at[rows, pl.ds(pl.multiple_of(first, 128), count)]
+            for first, count in ((q_at, 128), (q_at + 256, 128), (kv_at, 256), (kv_at + 256, 256))
+        ]
+
+    finals = [fin_q.at[0], fin_q.at[1], fin_kv.at[0], fin_kv.at[1]]
+    mine_at = spots(core, col_half, xh)
+    is_here = (core == xl) & (row_half == xh)
+
+    def deliver(which):
+        for i in which:
+            fin, spot, recv = finals[i], mine_at[i], f_recv.at[i, core, col_half, xh]
+            for d in (2, 1, 3):
+                for b in (0, 1):
+                    go(fin, spot, f_send.at[i, d, b], recv, at(row_half, z, xl, ypeer(d), flip(xl, b)))
+            go(fin, spot, f_send.at[i, 0, 1], recv, at(row_half, z, xl, y, 1 - xl))
+            away = remote(fin, spot, f_send.at[i, 0, 0], recv, at(row_half, z, xl, y, xl))
+            here = pltpu.make_async_copy(fin, spot, f_local.at[i])
+
+            @pl.when(is_here)
+            def _():
+                here.start()
+                here.wait()
+
+            @pl.when(jnp.logical_not(is_here))
+            def _():
+                away.start()
+                away.wait_send()
+
+    query_side(0)
+    query_side(1)
+    share_q(0)
     for dn, piece in pieces:
         if (dn, piece) != (0, 0):
             region_came(1, gr_ref, dn, piece)
@@ -464,54 +539,19 @@
                 xt_ref[128 * i : 128 * i + 128, to_lane : to_lane + 128] = (
                     tokens[:, 128 * i : 128 * i + 128].T.astype(BF16)
                 )
-    ldb[1, 1] = ld_ref[...]
-    for dn, dc in NEAR:
-        came(ldb.at[1 - dn, 1 - dc], ld_send.at[dn + 1, dc + 1], ld_recv.at[1 - dn, 1 - dc])
-    column = lax.rem(lax.broadcasted_iota(jnp.int32, (16, 256), 1), 32)
-    for hf in range(2):
-        parts = []
-        for r in range(3):
-            left, mid, right = ldb[r, 0], ldb[r, 1], ldb[r, 2]
-            if hf == 0:
-                part = jnp.where(column < 8, pltpu.roll(left, 232, 1), pltpu.roll(mid, 8, 1))
-            else:
-                part = jnp.where(column < 24, pltpu.roll(mid, 248, 1), pltpu.roll(right, 24, 1))
-            parts.append(part)
-        lds[hf] = pltpu.roll(jnp.concatenate(parts, axis=1), 768 - 64, 1)[:, :640]
-
-    low, masks, _ = head_masks()
-
-    def key_side(hp):
-        lanes = slice(128 * hp, 128 * hp + 128)
-
-        def side(hf, carry):
-            window = pl.ds(pl.multiple_of(16 * hf, 16), 32)
-            query = qr_ref[:, window, lanes].reshape(640, 128)
-            grad = grs_ref[:, window, lanes].reshape(640, 128)
-            keys = kown_ref[hf, :, lanes]
-            values = vown_ref[hf, :, lanes]
-            dks, dvs = [], []
-            for j in range(2):
-                head = 2 * hp + j
-                s = nt(keys * masks[j], query) + bias[hf]
-                e = jnp.exp(s - lds[hf, head : head + 1, :])
-                dvs.append(nn(e.astype(BF16), grad))
-                dp = nt(values * masks[j], grad)
-                ds = (e * (dp - lds[hf, head + 8 : head + 9, :]) * SCALE).astype(BF16)
-                dks.append(nn(ds, query))
-            kv[hp, 0, hf] = jnp.where(low, dks[0], dks[1]).astype(BF16)
-            kv[hp, 1, hf] = jnp.where(low, dvs[0], dvs[1]).astype(BF16)
-            return carry
-
-        lax.fori_loop(0, 2, side, 0)
-        share(hp)
-
     key_side(0)
-    product_q()
+    query_side(2)
+    product_q(0)
     key_side(1)
     product_kv(0)
+    query_side(3)
+    share_q(1)
+    go(attn_ref.at[other], attn_out.at[:, half_of(core)], a_send, a_recv, sibling)
+    attn_own = pltpu.make_async_copy(attn_ref.at[core], attn_out.at[:, half_of(core)], o_sem.at[0])
+    attn_own.start()
+    product_kv(1)
     key_side(2)
-    product_kv(1)
+    product_q(1)
     sum_x(0)
     sum_x(1)
     key_side(3)
@@ -531,9 +571,11 @@
         gx[:, :, rows] = total.reshape(2, 128, 256)
         return carry
 
-    product_kv(3)
     lax.fori_loop(0, 4, input_columns, 0)
     go(gx.at[other], gxr, g_send, g_recv, sibling)
+    product_kv(3)
+    sum_z(0)
+    deliver(range(3))
     sum_x(4)
     sum_x(5)
     spread(1)
@@ -541,35 +583,8 @@
     gxo[...] = (gx[core] + gxr[...]).astype(BF16)
     gx_own = pltpu.make_async_copy(gxo, gx_out, o_sem.at[1])
     gx_own.start()
-    sum_z(0)
     sum_z(1)
-
-    def spots(c, part, a):
-        rows = pl.ds(pl.multiple_of(16 * a, 16), 16)
-        q_at = pl.multiple_of(c * 512 + part * 256, 256)
-        kv_at = pl.multiple_of((1 + part) * 1024 + c * 512, 512)
-        return gw_out.at[rows, pl.ds(q_at, 256)], gw_out.at[rows, pl.ds(kv_at, 512)]
-
-    mine = spots(core, col_half, xh)
-    for i, fin in enumerate((fin_q, fin_kv)):
-        recv = f_recv.at[i, core, col_half, xh]
-        for d in (2, 1, 3):
-            for b in (0, 1):
-                go(fin, mine[i], f_send.at[i, d, b], recv, at(row_half, z, xl, ypeer(d), flip(xl, b)))
-        go(fin, mine[i], f_send.at[i, 0, 1], recv, at(row_half, z, xl, y, 1 - xl))
-        away = remote(fin, mine[i], f_send.at[i, 0, 0], recv, at(row_half, z, xl, y, xl))
-        here = pltpu.make_async_copy(fin, mine[i], f_local.at[i])
-        is_here = (core == xl) & (row_half == xh)
-
-        @pl.when(is_here)
-        def _():
-            here.start()
-            here.wait()
-
-        @pl.when(jnp.logical_not(is_here))
-        def _():
-            away.start()
-            away.wait_send()
+    deliver((3,))
 
     attn_own.wait()
     gx_own.wait()
@@ -581,7 +596,7 @@
                 own = (
                     (c == core) & (part == col_half) & (a == xh) & (row_half == xh) & (xl == core)
                 )
-                for i in range(2):
+                for i in range(4):
 
                     @pl.when(jnp.logical_not(own))
                     def _():
@@ -609,18 +624,18 @@
             half(3, 2, 8, 2, 8, 512), vmem(2, 8, 128),
             vmem(3, 20, 6, 8, 512), half(20, 48, 512), half(20, 48, 512), half(20, 48, 512),
             half(20, 48, 512), half(2, 128, 512), half(2, 128, 512), half(2, 128, 512),
-            half(2, 128, 512), vmem(128, 128), vmem(8, 32, 128), vmem(16, 256),
+            half(2, 128, 512), vmem(2, 128, 128), vmem(8, 32, 128), vmem(4, 8, 256),
             half(4, 2, 128, 128), half(2, 128, 512), half(512, 1024),
             half(4, 6, 2, 128, 128), vmem(6, 8, 2, 2, 2, 8, 128), vmem(6, 3, 8, 2, 8, 128),
-            vmem(8, 6, 2, 8, 128), vmem(7, 6, 2, 8, 128), vmem(16, 256), vmem(16, 512),
-            half(4, 2, 2, 128, 128), vmem(2, 16, 640), vmem(3, 3, 16, 256), vmem(2, 128, 640),
+            vmem(8, 6, 2, 8, 128), vmem(7, 6, 2, 8, 128), vmem(2, 16, 128), vmem(2, 16, 256),
+            half(4, 2, 2, 128, 128), vmem(4, 2, 8, 640), vmem(4, 3, 3, 8, 256), vmem(2, 128, 640),
             vmem(2, 128, 1024), vmem(128, 1024), half(128, 1024),
             dma((2, 3, 2, 2)), dma((2, 3, 4)), dma((2,)), dma, dma, dma, dma,
             dma((3,)), dma((3,)), dma((3,)), dma((3,)), dma((3,)),
             dma((2, 2, 4, 3)), dma((2, 2, 4, 3)), dma((3, 2)), dma((3, 2)),
-            dma((3, 3)), dma((3, 3)), dma((2,)), dma, dma, dma, dma,
-            dma((3,)), dma((3,)), dma((4, 3)), dma((4, 3)), dma((6, 3)), dma((6, 3)),
-            dma((2, 7)), dma((2, 7)), dma((2, 4, 2)), dma((2, 2, 2, 2)), dma((2,)),
+            dma((4, 3, 3)), dma((4, 3, 3)), dma((2,)), dma, dma, dma, dma,
+            dma((2, 3)), dma((2, 3)), dma((4, 3)), dma((4, 3)), dma((6, 3)), dma((6, 3)),
+            dma((2, 7)), dma((2, 7)), dma((4, 4, 2)), dma((4, 2, 2, 2)), dma((4,)),
         ],
         compiler_params=pltpu.CompilerParams(
             collective_id=0, has_side_effects=True, vmem_limit_bytes=VMEM_LIMIT

time: 123 us -> 116 us (0.943)
  Pallas kernels: 119 us -> 112 us
    pallas_call x1, Pallas kernels: 119 us -> 112 us  [layer(): pl.pallas_call(layer_kernel, out_shape=(shape((128, 1024), BF16), shape((...]
where the time goes in v5:
time: 116 us
  Pallas kernels  112 us (97%)
  local copies, waits for them, and re-layouts  3.19 us (3%)
  between operations  1.3 us (1%)
    pallas_call x1, Pallas kernels, layer(): pl.pallas_call(layer_kernel, out_shape=(shape((128, 1024), BF16), shape((...  112 us
    unnamed x7, local copies, waits for them, and re-layouts  3.19 us

profile of v5, /device:TPU:1, one launch (start us, length us, event | category | flops | bytes accessed | tf_op | source)
XLA Modules:
  0.0 116.4 jit_solution(15964878941769397315)
XLA Ops:
  1.3 111.9 %layer.1 = (bf16[128,1024]{1,0:T(8,128)(2,1)}, bf16[128,1024]{1,0:T(8,128)(2,1)}, f32[32,3072]{1,0:T(8,128)}) custom-call(bf16[8,2,8,1024]{3,2,1,0:T(8,128)(2,1)} %bitcast.4, bf16[8,2,8,1024]{3,2,1,0:T(8,128)(2,1)} %bitcast.5, bf16[32,3072]{1,0:T(8,128)(2,1)} %w_ref.1, s32[1,2]{1,0:T(1,128)} %list_ref.1, s32[1,1]{1,0:T(1,128)S(6)} %copy.11.count_ref), custom_call_target="tpu_custom_call" | custom-call | tf_op jit(solution)/shard_map/layer/pallas_call | solution.py:615
  113.1 0.0 copy-start.1
  113.2 0.0 copy-start
  113.2 1.7 %copy.12 = bf16[8,16,1024]{2,1,0:T(8,128)(2,1)} copy(bf16[8,16,1024]{2,1,0:T(8,128)(2,1)} %bitcast.7) | data formatting | bytes 524288
  114.9 0.0 copy-done.1
  114.9 0.7 copy.13
  115.6 0.0 copy-done
  115.6 0.7 copy.14
Async XLA Ops:
  113.1 1.8 %copy-start.1 = (bf16[128,1024]{1,0:T(8,128)(2,1)S(1)}, bf16[128,1024]{1,0:T(8,128)(2,1)}, u32[]{:S(2)}) copy-start(bf16[128,1024]{1,0:T(8,128)(2,1)} %get-tuple-element.7) | copy-start | bytes 786436
  113.2 2.5 %copy-start = (f32[32,3072]{1,0:T(8,128)S(1)}, f32[32,3072]{1,0:T(8,128)}, u32[]{:S(2)}) copy-start(f32[32,3072]{1,0:T(8,128)} %get-tuple-element.14) | copy-start | bytes 1179652

commit v6 on v5

--- a/solution.py
+++ b/solution.py
@@ -489,6 +489,7 @@
     finals = [fin_q.at[0], fin_q.at[1], fin_kv.at[0], fin_kv.at[1]]
     mine_at = spots(core, col_half, xh)
     is_here = (core == xl) & (row_half == xh)
+    kept = []
 
     def deliver(which):
         for i in which:
@@ -500,15 +501,15 @@
             away = remote(fin, spot, f_send.at[i, 0, 0], recv, at(row_half, z, xl, y, xl))
             here = pltpu.make_async_copy(fin, spot, f_local.at[i])
 
+            kept.append((here, away))
+
             @pl.when(is_here)
             def _():
                 here.start()
-                here.wait()
 
             @pl.when(jnp.logical_not(is_here))
             def _():
                 away.start()
-                away.wait_send()
 
     query_side(0)
     query_side(1)
@@ -602,6 +603,16 @@
                     def _():
                         came(landed[i], f_send.at[i, 0, 0], f_recv.at[i, c, part, a])
 
+    for here, away in kept:
+
+        @pl.when(is_here)
+        def _():
+            here.wait()
+
+        @pl.when(jnp.logical_not(is_here))
+        def _():
+            away.wait_send()
+
     for cp in sends:
         cp.wait_send()
 

time: 116 us -> 112 us (0.966)
  Pallas kernels: 112 us -> 108 us
    pallas_call x1, Pallas kernels: 112 us -> 108 us  [layer(): pl.pallas_call(layer_kernel, out_shape=(shape((128, 1024), BF16), shape((...]
where the time goes in v6:
time: 112 us
  Pallas kernels  108 us (96%)
  local copies, waits for them, and re-layouts  3.19 us (3%)
  between operations  1.3 us (1%)
    pallas_call x1, Pallas kernels, layer(): pl.pallas_call(layer_kernel, out_shape=(shape((128, 1024), BF16), shape((...  108 us
    unnamed x7, local copies, waits for them, and re-layouts  3.19 us

profile of v6, /device:TPU:1, one launch (start us, length us, event | category | flops | bytes accessed | tf_op | source)
XLA Modules:
  0.0 112.2 jit_solution(838703866091530252)
XLA Ops:
  1.3 107.7 %layer.1 = (bf16[128,1024]{1,0:T(8,128)(2,1)}, bf16[128,1024]{1,0:T(8,128)(2,1)}, f32[32,3072]{1,0:T(8,128)}) custom-call(bf16[8,2,8,1024]{3,2,1,0:T(8,128)(2,1)} %bitcast.4, bf16[8,2,8,1024]{3,2,1,0:T(8,128)(2,1)} %bitcast.5, bf16[32,3072]{1,0:T(8,128)(2,1)} %w_ref.1, s32[1,2]{1,0:T(1,128)} %list_ref.1, s32[1,1]{1,0:T(1,128)S(6)} %copy.11.count_ref), custom_call_target="tpu_custom_call" | custom-call | tf_op jit(solution)/shard_map/layer/pallas_call | solution.py:626
  109.0 0.0 copy-start.1
  109.0 0.0 copy-start
  109.0 1.7 %copy.12 = bf16[8,16,1024]{2,1,0:T(8,128)(2,1)} copy(bf16[8,16,1024]{2,1,0:T(8,128)(2,1)} %bitcast.7) | data formatting | bytes 524288
  110.8 0.0 copy-done.1
  110.8 0.7 copy.13
  111.5 0.0 copy-done
  111.5 0.7 copy.14
Async XLA Ops:
  109.0 1.8 %copy-start.1 = (bf16[128,1024]{1,0:T(8,128)(2,1)S(1)}, bf16[128,1024]{1,0:T(8,128)(2,1)}, u32[]{:S(2)}) copy-start(bf16[128,1024]{1,0:T(8,128)(2,1)} %get-tuple-element.7) | copy-start | bytes 786436
  109.0 2.5 %copy-start = (f32[32,3072]{1,0:T(8,128)S(1)}, f32[32,3072]{1,0:T(8,128)}, u32[]{:S(2)}) copy-start(f32[32,3072]{1,0:T(8,128)} %get-tuple-element.14) | copy-start | bytes 1179652

commit v7 on v6

--- a/solution.py
+++ b/solution.py
@@ -575,11 +575,11 @@
     lax.fori_loop(0, 4, input_columns, 0)
     go(gx.at[other], gxr, g_send, g_recv, sibling)
     product_kv(3)
+    sum_x(4)
     sum_z(0)
-    deliver(range(3))
-    sum_x(4)
     sum_x(5)
     spread(1)
+    deliver(range(3))
     came(gxr, g_send, g_recv)
     gxo[...] = (gx[core] + gxr[...]).astype(BF16)
     gx_own = pltpu.make_async_copy(gxo, gx_out, o_sem.at[1])

time: 112 us -> 113 us (level)
  no operation moved by 1% of the time
where the time goes in v7:
time: 113 us
  Pallas kernels  109 us (96%)
  local copies, waits for them, and re-layouts  3.19 us (3%)
  between operations  1.3 us (1%)
    pallas_call x1, Pallas kernels, layer(): pl.pallas_call(layer_kernel, out_shape=(shape((128, 1024), BF16), shape((...  109 us
    unnamed x7, local copies, waits for them, and re-layouts  3.19 us

profile of v7, /device:TPU:1, one launch (start us, length us, event | category | flops | bytes accessed | tf_op | source)
XLA Modules:
  0.0 113.1 jit_solution(11717636360640227173)
XLA Ops:
  1.3 108.6 %layer.1 = (bf16[128,1024]{1,0:T(8,128)(2,1)}, bf16[128,1024]{1,0:T(8,128)(2,1)}, f32[32,3072]{1,0:T(8,128)}) custom-call(bf16[8,2,8,1024]{3,2,1,0:T(8,128)(2,1)} %bitcast.4, bf16[8,2,8,1024]{3,2,1,0:T(8,128)(2,1)} %bitcast.5, bf16[32,3072]{1,0:T(8,128)(2,1)} %w_ref.1, s32[1,2]{1,0:T(1,128)} %list_ref.1, s32[1,1]{1,0:T(1,128)S(6)} %copy.11.count_ref), custom_call_target="tpu_custom_call" | custom-call | tf_op jit(solution)/shard_map/layer/pallas_call | solution.py:626
  109.9 0.0 copy-start.1
  109.9 0.0 copy-start
  109.9 1.7 %copy.12 = bf16[8,16,1024]{2,1,0:T(8,128)(2,1)} copy(bf16[8,16,1024]{2,1,0:T(8,128)(2,1)} %bitcast.7) | data formatting | bytes 524288
  111.7 0.0 copy-done.1
  111.7 0.7 copy.13
  112.4 0.0 copy-done
  112.4 0.7 copy.14
Async XLA Ops:
  109.9 1.8 %copy-start.1 = (bf16[128,1024]{1,0:T(8,128)(2,1)S(1)}, bf16[128,1024]{1,0:T(8,128)(2,1)}, u32[]{:S(2)}) copy-start(bf16[128,1024]{1,0:T(8,128)(2,1)} %get-tuple-element.7) | copy-start | bytes 786436
  109.9 2.5 %copy-start = (f32[32,3072]{1,0:T(8,128)S(1)}, f32[32,3072]{1,0:T(8,128)}, u32[]{:S(2)}) copy-start(f32[32,3072]{1,0:T(8,128)} %get-tuple-element.14) | copy-start | bytes 1179652
